TPU v7x, 32 devices: a whole 2x2x4 slice. The times are simulated.
32 devices in a mesh: wide: 8 (over y, x, core), cell: 4 (over z).
Axes of the slice: x: 2, y: 2, z: 4, core: 2. Of those that a mesh axis runs over, the one named last changes fastest.
Arguments:
- green_pair: float32 [2, 2, 32, 4, 128, 128], P(None, None, 'wide', 'cell'), may hold values from -5 to 5
- coulomb: float32 [4, 2, 128, 128], P('cell'), may hold values from -0.5 to 0.5
- green_retarded: float32 [2, 32, 4, 2, 128, 128], P(None, 'wide', 'cell'), may hold values from -0.375 to 0.375
- offsets: int32 [4, 2], P('cell'), may hold values from -1 to 1, as said below
Outputs:
- dressed: float32 [2, 32, 4, 128, 128], P(None, 'wide', 'cell')
Inputs may be any that keep to these rules, and one draw needn't show every extreme that they name: Block row r stores its blocks at block columns r + offsets[r, 0] and r + offsets[r, 1], two different entries of -1, 0, 1 in increasing order. Every block row r with r even has offsets -1 and 1.
All inputs are finite; a program needn't handle non-finite values.
Results may differ from a plain program's by a relative error of at most 0.00014.
Values sent between devices are 32-bit elements; how exact they have to be, the bound alone decides.
No kernel may reach another device: no remote copies, remote signals or barrier semaphores. Data moves between devices by JAX's collectives and lax.ppermute only.
A program may use at most 64 MiB of HBM per device.

v0:
```python
from functools import partial
import math

import jax
import jax.numpy as jnp
from jax import lax
from jax.sharding import PartitionSpec as P


def padded_2(value, sides, width):
    for axis, dim in sides:
        peers, length = (lax.axis_size(axis), value.shape[dim])
        up = [(i, (i + 1) % peers) for i in range(peers - 1)]
        down = [(j, i) for i, j in up]
        last = lax.slice_in_dim(value, length - width, length, axis=dim)
        initial = lax.slice_in_dim(value, 0, width, axis=dim)
        before = lax.ppermute(last, axis, up)
        after = lax.ppermute(initial, axis, down)
        value = jnp.concatenate([before, value, after], axis=dim)
    return value


def phases(leading, trailing, period):
    product = leading[:, None] * trailing[None, :] % period
    angles = product.astype(jnp.float32) * (2.0 * math.pi / period)
    return (jnp.cos(angles), jnp.sin(angles))


def rotate(real_part, imag_part, cosines, sines):
    multiply = partial(jnp.dot, precision=lax.Precision.HIGHEST, preferred_element_type=jnp.float32)
    return (
        multiply(cosines, real_part) - multiply(sines, imag_part),
        multiply(cosines, imag_part) + multiply(sines, real_part),
    )


def to_elements(pieces):
    return lax.all_to_all(pieces, "wide", split_axis=4, concat_axis=2, tiled=True)


def to_energies(pieces):
    return lax.all_to_all(pieces, "wide", split_axis=2, concat_axis=4, tiled=True)


def neighbours(blocks):
    return padded_2(blocks, (("cell", 2),), 1)


def choose_block(padded, offsets, local_row, position):
    shift_value = offsets[local_row, position]
    return jnp.where(
        shift_value < 0,
        padded[:, :, local_row],
        jnp.where(shift_value > 0, padded[:, :, local_row + 2], padded[:, :, local_row + 1]),
    )


def screen(polar_energy, coulomb, offsets):
    padded = neighbours(polar_energy)
    running = jnp.zeros(polar_energy[:, :, 0].shape, jnp.float32)
    for position in range(2):
        coupling = coulomb[0, position]
        middle = choose_block(padded, offsets, 0, position)
        running = running + jnp.einsum(
            "ab,pfbc,dc->pfad",
            coupling,
            middle,
            coupling,
            precision=lax.Precision.HIGHEST,
            preferred_element_type=jnp.float32,
        )
    blocks = [running]
    return jnp.stack(blocks, axis=2)


def congruence(green_block, middle):
    multiply = partial(
        jnp.einsum,
        "eab,ebc->eac",
        precision=lax.Precision.HIGHEST,
        preferred_element_type=jnp.float32,
    )
    times_transposed = partial(
        jnp.einsum,
        "eab,edb->ead",
        precision=lax.Precision.HIGHEST,
        preferred_element_type=jnp.float32,
    )
    left_real = multiply(green_block[0], middle[0]) - multiply(green_block[1], middle[1])
    left_imag = multiply(green_block[0], middle[1]) + multiply(green_block[1], middle[0])
    out_real = times_transposed(left_real, green_block[0]) - times_transposed(
        left_imag, green_block[1]
    )
    out_imag = times_transposed(left_real, green_block[1]) + times_transposed(
        left_imag, green_block[0]
    )
    return jnp.stack([out_real, out_imag])


def dressed_blocks(sigma_energy, green_retarded, offsets):
    padded = neighbours(sigma_energy)
    running = jnp.zeros(sigma_energy[:, :, 0].shape, jnp.float32)
    for position in range(2):
        green_block = green_retarded[:, :, 0, position]
        middle = choose_block(padded, offsets, 0, position)
        running = running + congruence(green_block, middle)
    blocks = [running]
    return jnp.stack(blocks, axis=2)


def complex_product(first_pair, second_pair):
    return (
        first_pair[0] * second_pair[0] - first_pair[1] * second_pair[1],
        first_pair[0] * second_pair[1] + first_pair[1] * second_pair[0],
    )


def body(green_pair, coulomb, green_retarded, offsets):
    count_wide = lax.axis_size("wide")
    energies = green_pair.shape[2] * count_wide
    period = 2 * energies
    norming = 1.0 / (period * math.sqrt(energies))
    element_pair = to_elements(green_pair)
    element_tail = element_pair.shape[3:]
    element_count = element_pair[0, 0, 0].size
    lesser_real = element_pair[0, 0].reshape(energies, element_count)
    lesser_imag = element_pair[0, 1].reshape(energies, element_count)
    greater_real = element_pair[1, 0].reshape(energies, element_count)
    greater_imag = element_pair[1, 1].reshape(energies, element_count)
    times_all = jnp.arange(period, dtype=jnp.int32)
    energy_grid = jnp.arange(energies, dtype=jnp.int32)
    forward_cos, forward_sin = phases(times_all, energy_grid, period)
    lesser_hat = rotate(lesser_real, lesser_imag, forward_cos, -forward_sin)
    greater_hat = rotate(greater_real, greater_imag, forward_cos, forward_sin)
    joint_real, joint_imag = complex_product(lesser_hat, greater_hat)
    polarization = jnp.stack([joint_real, joint_imag]) * (1.0 / math.sqrt(energies))
    polar_energy = to_energies(polarization.reshape((1, 2, period) + element_tail))[0]
    screened = screen(polar_energy, coulomb, offsets)
    screened_elements = to_elements(screened[None])
    screened_real = screened_elements[0, 0].reshape(period, element_count)
    screened_imag = screened_elements[0, 1].reshape(period, element_count)
    screened_hat = (screened_real, screened_imag)
    product_real, product_imag = complex_product(lesser_hat, screened_hat)
    output_cos, output_sin = phases(energy_grid, times_all, period)
    sigma_real, sigma_imag = rotate(product_real, product_imag, output_cos, output_sin)
    self_energy = (jnp.stack([sigma_real, sigma_imag]) * norming).reshape(
        (1, 2, energies) + element_tail
    )
    sigma_energy = to_energies(self_energy)[0]
    return dressed_blocks(sigma_energy, green_retarded, offsets)


def solution(mesh):
    placed = (
        P(None, None, "wide", "cell", None, None),
        P("cell", None, None, None),
        P(None, "wide", "cell", None, None, None),
        P("cell", None),
    )
    return jax.shard_map(
        body,
        mesh=mesh,
        in_specs=placed,
        out_specs=P(None, "wide", "cell", None, None),
        check_vma=False,
    )
```

profile of v0, /device:TPU:0, one launch (start us, length us, event | category | flops | bytes accessed | tf_op | source)
XLA Modules:
  0.0 140.8 jit_solution(10779834640348830553)
XLA Ops:
  0.0 1.9 %copy.69 = f32[2,2,4,1,128,128]{5,2,1,0,3,4:T(4,128)S(1)} copy(f32[2,2,4,1,128,128]{5,4,3,2,1,0:T(8,128)} %param.4) | data formatting | bytes 2097152 | tf_op args[0]
  1.9 20.3 %all_to_all.66 = f32[2,2,4,1,128,128]{5,2,1,0,3,4:T(4,128)S(1)} all-to-all(f32[2,2,4,1,128,128]{5,2,1,0,3,4:T(4,128)S(1)} %copy.69), channel_id=1, replica_groups=mesh['wide'=8,'cell'=4] {'wide'}, dimensions={4} | all-to-all | bytes 2097152 | tf_op jit(solution)/shard_map/all_to_all | solution.py:38
  22.8 0.7 fusion.28
  23.5 0.7 fusion.24
  24.3 0.8 convolution_add_fusion
  25.0 0.7 fusion.30
  25.8 0.7 fusion.34
  26.5 0.8 convolution_add_fusion.1
  27.2 0.7 convolution_subtract_fusion.1
  28.0 0.9 subtract_bitcast_fusion
  29.2 17.8 %all_to_all.67 = f32[1,2,64,1,16,128]{5,4,1,3,0,2:T(8,128)S(1)} all-to-all(f32[1,2,64,1,16,128]{5,4,1,3,0,2:T(8,128)S(1)} %maximum_multiply_fusion), channel_id=1, replica_groups=mesh['wide'=8,'cell'=4] {'wide'}, dimensions={2} | all-to-all | bytes 2097152 | tf_op jit(solution)/shard_map/all_to_all | solution.py:42
  47.2 1.3 collective-permute-start.1
  48.5 4.8 %collective-permute-start = (f32[2,8,1,128,128]{4,3,1,0,2:T(8,128)S(1)}, f32[2,8,1,128,128]{4,3,1,0,2:T(8,128)S(1)}, u32[]{:S(2)}, u32[]{:S(2)}) collective-permute-start(f32[2,8,1,128,128]{4,3,1,0,2:T(8,128)S(1)} %bitcast.224), channel_id=1, source_target_pairs={{0,1},{1,2},{2,3},{4,5},{5,6},{6,7},{8,9},{9,10},{10,11},{12,13},{... | collective-permute-start | bytes 3145736 | tf_op jit(solution)/shard_map/ppermute | solution.py:17
  56.4 17.0 %collective-permute-done.1 = f32[2,8,1,128,128]{4,3,1,0,2:T(8,128)S(1)} collective-permute-done((f32[2,8,1,128,128]{4,3,1,0,2:T(8,128)S(1)}, f32[2,8,1,128,128]{4,3,1,0,2:T(8,128)S(1)}, u32[]{:S(2)}, u32[]{:S(2)}) %collective-permute-start.1) | collective-permute-done | bytes 1048608 | tf_op jit(solution)/shard_map/ppermute | solution.py:18
  73.4 1.2 collective-permute-done
  74.6 1.2 fusion.9
  75.8 1.0 fusion.86
  76.7 1.2 fusion.7
  77.9 1.0 fusion
  79.5 17.8 %all_to_all.68 = f32[1,2,8,1,128,128]{5,2,1,3,0,4:T(8,128)S(1)} all-to-all(f32[1,2,8,1,128,128]{5,2,1,3,0,4:T(8,128)S(1)} %copy.80), channel_id=1, replica_groups=mesh['wide'=8,'cell'=4] {'wide'}, dimensions={4} | all-to-all | bytes 2097152 | tf_op jit(solution)/shard_map/all_to_all | solution.py:38
  100.2 12.1 %all_to_all.69 = f32[1,2,32,1,16,128]{5,4,1,3,0,2:T(8,128)S(1)} all-to-all(f32[1,2,32,1,16,128]{5,4,1,3,0,2:T(8,128)S(1)} %maximum_multiply_fusion.1), channel_id=1, replica_groups=mesh['wide'=8,'cell'=4] {'wide'}, dimensions={2} | all-to-all | bytes 1048576 | tf_op jit(solution)/shard_map/all_to_all | solution.py:42
  112.6 1.3 collective-permute-start.3
  113.9 5.3 %collective-permute-start.2 = (f32[2,4,1,128,128]{3,4,1,0,2:T(8,128)S(1)}, f32[2,4,1,128,128]{3,4,1,0,2:T(8,128)S(1)}, u32[]{:S(2)}, u32[]{:S(2)}) collective-permute-start(f32[2,4,1,128,128]{3,4,1,0,2:T(8,128)S(1)} %copy.86), channel_id=1, source_target_pairs={{0,1},{1,2},{2,3},{4,5},{5,6},{6,7},{8,9},{9,10},{10,11},{12,13},{... | collective-permute-start | bytes 1572872 | tf_op jit(solution)/shard_map/ppermute | solution.py:17
  119.4 9.0 %collective-permute-done.3 = f32[2,4,1,128,128]{3,4,1,0,2:T(8,128)S(1)} collective-permute-done((f32[2,4,1,128,128]{3,4,1,0,2:T(8,128)S(1)}, f32[2,4,1,128,128]{3,4,1,0,2:T(8,128)S(1)}, u32[]{:S(2)}, u32[]{:S(2)}) %collective-permute-start.3) | collective-permute-done | bytes 524320 | tf_op jit(solution)/shard_map/ppermute | solution.py:18
  128.4 1.2 collective-permute-done.2
  130.4 0.7 fusion.41
  131.0 0.7 convolution_subtract_fusion.4
  132.9 0.7 fusion.51
  134.3 0.7 convolution_subtract_fusion.6
  136.2 0.7 convolution_add_fusion.5
  138.1 0.7 convolution_add_fusion.7
  140.0 0.9 fusion.17
  (41 shorter events, 11.9 us)
Async XLA Ops:
  47.0 27.6 %copy-start.1 = (f32[1,2,128,128]{3,2,1,0:T(8,128)S(1)}, f32[1,2,128,128]{3,2,1,0:T(8,128)}, u32[]{:S(2)}) copy-start(f32[1,2,128,128]{3,2,1,0:T(8,128)} %param.5) | copy-start | bytes 393220
  47.2 6.1 %copy-start.2 = (s32[1,2]{1,0:T(1,128)S(1)}, s32[1,2]{1,0:T(1,128)}, u32[]{:S(2)}) copy-start(s32[1,2]{1,0:T(1,128)} %param.7) | copy-start | bytes 28
  47.2 26.2 %collective-permute-start.1 = (f32[2,8,1,128,128]{4,3,1,0,2:T(8,128)S(1)}, f32[2,8,1,128,128]{4,3,1,0,2:T(8,128)S(1)}, u32[]{:S(2)}, u32[]{:S(2)}) collective-permute-start(f32[2,8,1,128,128]{4,3,1,0,2:T(8,128)S(1)} %bitcast.223), channel_id=1, source_target_pairs={{1,0},{2,1},{3,2},{5,4},{6,5},{7,6},{9,8},{10,9},{11,10},{13,12},{... | collective-permute-start | bytes 3145736 | tf_op jit(solution)/shard_map/ppermute | solution.py:18
  48.5 26.1 %collective-permute-start = (f32[2,8,1,128,128]{4,3,1,0,2:T(8,128)S(1)}, f32[2,8,1,128,128]{4,3,1,0,2:T(8,128)S(1)}, u32[]{:S(2)}, u32[]{:S(2)}) collective-permute-start(f32[2,8,1,128,128]{4,3,1,0,2:T(8,128)S(1)} %bitcast.224), channel_id=1, source_target_pairs={{0,1},{1,2},{2,3},{4,5},{5,6},{6,7},{8,9},{9,10},{10,11},{12,13},{... | collective-permute-start | bytes 3145736 | tf_op jit(solution)/shard_map/ppermute | solution.py:17
  112.6 15.7 %collective-permute-start.3 = (f32[2,4,1,128,128]{3,4,1,0,2:T(8,128)S(1)}, f32[2,4,1,128,128]{3,4,1,0,2:T(8,128)S(1)}, u32[]{:S(2)}, u32[]{:S(2)}) collective-permute-start(f32[2,4,1,128,128]{3,4,1,0,2:T(8,128)S(1)} %copy.86), channel_id=1, source_target_pairs={{1,0},{2,1},{3,2},{5,4},{6,5},{7,6},{9,8},{10,9},{11,10},{13,12},{... | collective-permute-start | bytes 1572872 | tf_op jit(solution)/shard_map/ppermute | solution.py:18
  113.9 15.6 %collective-permute-start.2 = (f32[2,4,1,128,128]{3,4,1,0,2:T(8,128)S(1)}, f32[2,4,1,128,128]{3,4,1,0,2:T(8,128)S(1)}, u32[]{:S(2)}, u32[]{:S(2)}) collective-permute-start(f32[2,4,1,128,128]{3,4,1,0,2:T(8,128)S(1)} %copy.86), channel_id=1, source_target_pairs={{0,1},{1,2},{2,3},{4,5},{5,6},{6,7},{8,9},{9,10},{10,11},{12,13},{... | collective-permute-start | bytes 1572872 | tf_op jit(solution)/shard_map/ppermute | solution.py:17
  119.4 10.3 %copy-start = (f32[2,4,1,2,128,128]{5,4,3,2,1,0:T(8,128)S(1)}, f32[2,4,1,2,128,128]{5,4,3,2,1,0:T(8,128)}, u32[]{:S(2)}) copy-start(f32[2,4,1,2,128,128]{5,4,3,2,1,0:T(8,128)} %param.6) | copy-start | bytes 3145732
where the time goes:
time: 141 us
  blocking collectives  68 us (48%)
  waiting for transfers between devices  28.3 us (20%)
  matrix products  22.3 us (16%)
  starting transfers between devices  12.6 us (9%)
  local copies, waits for them, and re-layouts  5.02 us (4%)
  between operations  2.99 us (2%)
  other arithmetic  1.63 us (1%)
    all_to_all x2, blocking collectives, to_elements(): lax.all_to_all(pieces, 'wide', split_axis=4, concat_axis=2, tiled=True)  38.1 us
    all_to_all x2, blocking collectives, to_energies(): lax.all_to_all(pieces, 'wide', split_axis=2, concat_axis=4, tiled=True)  29.9 us
    ppermute x2, waiting for transfers between devices, padded_2(): after = lax.ppermute(initial, axis, down)  25.9 us
    ppermute x2, starting transfers between devices, padded_2(): before = lax.ppermute(last, axis, up)  10.1 us
    dot_general x4, matrix products, screen(): jnp.einsum('ab,pfbc,dc->pfad', coupling, middle, coupling, precision=lax....  4.28 us
  transfers between devices with their start and end apart: 4, of which 4 were waited for; matrix products, arithmetic and copies ran while one was open for 1% of the time, Pallas kernels for 0%

commit v1 on v0

v1 whole, which is shorter than its diff:
```python
import math

import jax
import jax.numpy as jnp
from jax import lax
from jax.experimental import pallas as pl
from jax.experimental.pallas import tpu as pltpu
from jax.sharding import PartitionSpec as P

USES_PALLAS = True
FORWARD = 3
BACKWARD = 2
HIGH = lax.Precision.HIGH
TILE = 8


def heights(order, parts):
    tiles = order // TILE
    sizes = [tiles // parts + (1 if k < tiles % parts else 0) for k in range(parts)]
    return [s * TILE for s in sizes]


def starts_of(sizes):
    return [sum(sizes[:k]) for k in range(len(sizes))]


def bits_of(peers):
    return peers.bit_length() - 1


def own_bit(me, bit):
    return (me >> bit) & 1


def spin(pair, flag, turns):
    c, s = math.cos(2 * math.pi * turns), math.sin(2 * math.pi * turns)
    on = flag == 1
    re, im = pair
    return (jnp.where(on, c * re - s * im, re), jnp.where(on, c * im + s * re, im))


def phase(me, bits, low, unit, top=0):
    pair = (jnp.float32(1.0), jnp.float32(0.0))
    if top:
        angle = 2 * math.pi * unit * (top << bits)
        pair = (jnp.float32(math.cos(angle)), jnp.float32(math.sin(angle)))
    for s in range(low):
        pair = spin(pair, own_bit(me, bits - 1 - s), unit * (1 << s))
    return pair


def times(value, c, s):
    re, im = value
    return (c * re - s * im, c * im + s * re)


def dft(values, sign):
    count = len(values)
    if count == 1:
        return values
    even, odd = dft(values[0::2], sign), dft(values[1::2], sign)
    out = [None] * count
    for k in range(count // 2):
        re, im = odd[k]
        if k == 0:
            turned = (re, im)
        elif 4 * k == count:
            turned = (-im, re) if sign > 0 else (im, -re)
        else:
            angle = sign * 2 * math.pi * k / count
            turned = times(odd[k], math.cos(angle), math.sin(angle))
        out[k] = (even[k][0] + turned[0], even[k][1] + turned[1])
        out[k + count // 2] = (even[k][0] - turned[0], even[k][1] - turned[1])
    return out


def tiles_loop(rows, step):
    def run(i, carry):
        step(pl.ds(pl.multiple_of(i * TILE, TILE), TILE))
        return carry

    lax.fori_loop(0, rows // TILE, run, 0)


def call(kernel, out_shapes, *args, smem=()):
    specs = [
        pl.BlockSpec(memory_space=pltpu.SMEM if i in smem else pltpu.VMEM)
        for i in range(len(args))
    ]
    nbytes = sum(a.size * 4 for a in args) + sum(4 * math.prod(s) for s in out_shapes)
    return pl.pallas_call(
        kernel,
        out_shape=[jax.ShapeDtypeStruct(s, jnp.float32) for s in out_shapes],
        in_specs=specs,
        out_specs=[pl.BlockSpec(memory_space=pltpu.VMEM) for _ in out_shapes],
        cost_estimate=pl.CostEstimate(flops=nbytes, bytes_accessed=nbytes, transcendentals=0),
        compiler_params=pltpu.CompilerParams(vmem_limit_bytes=nbytes + (1 << 20)),
    )(*args)


def split_first(own, got, had):
    return jnp.where(had == 1, got, own), jnp.where(had == 1, own, got)


def forward_kernel(stage, bits, own_ref, got_ref, keep_ref, send_ref):
    me = lax.axis_index("wide")
    local, rows = own_ref.shape[2], own_ref.shape[3]
    had = own_bit(me, bits - stage)
    mine = own_bit(me, bits - 1 - stage)
    c, s = phase(me, bits, stage, 1.0 / (1 << (stage + 1)))
    flip = jnp.where(mine == 1, jnp.float32(-1.0), jnp.float32(1.0))
    c, s = c * flip, s * flip

    def step(at):
        for which in range(2):
            side = -s if which == 0 else s
            for j in range(local):
                pairs = [
                    split_first(own_ref[which, i, j, at], got_ref[which, i, j, at], had)
                    for i in range(2)
                ]
                turned = times((pairs[0][1], pairs[1][1]), c, side)
                for i in range(2):
                    keep_ref[which, i, j, at] = pairs[i][0] + turned[i]
                    send_ref[which, i, j, at] = pairs[i][0] - turned[i]

    tiles_loop(rows, step)


def product_kernel(bits, own_ref, got_ref, lesser_ref, polar_ref):
    me = lax.axis_index("wide")
    local, rows = own_ref.shape[2], own_ref.shape[3]
    peers = 1 << bits
    period = 2 * peers * local
    had = own_bit(me, 0)
    c, s = phase(me, bits, bits, 1.0 / (2 * peers))
    twist = [
        [phase(me, bits, bits, j / period, top) for j in range(local)] for top in range(2)
    ]

    def step(at):
        hats = []
        for which in range(2):
            sign = -1 if which == 0 else 1
            tops = [[], []]
            for j in range(local):
                pairs = [
                    split_first(own_ref[which, i, j, at], got_ref[which, i, j, at], had)
                    for i in range(2)
                ]
                turned = times((pairs[0][1], pairs[1][1]), c, sign * s)
                for top in range(2):
                    value = tuple(
                        pairs[i][0] + turned[i] if top == 0 else pairs[i][0] - turned[i]
                        for i in range(2)
                    )
                    if j > 0:
                        value = times(value, twist[top][j][0], sign * twist[top][j][1])
                    tops[top].append(value)
            hats.append(dft(tops[0], sign) + dft(tops[1], sign))
        for f in range(2 * local):
            a, b = hats[0][f], hats[1][f]
            lesser_ref[0, f, at], lesser_ref[1, f, at] = a
            polar_ref[0, f, at], polar_ref[1, f, at] = times(a, b[0], b[1])

    tiles_loop(rows, step)


def inverse_kernel(bits, sizes, *refs):
    me = lax.axis_index("wide")
    lesser_refs, (screened_ref, keep_ref, send_ref) = refs[:-3], refs[-3:]
    local = keep_ref.shape[1]
    peers = 1 << bits
    period = 2 * peers * local
    mine = own_bit(me, 0)
    c, s = phase(me, bits, bits, 1.0 / (2 * peers))
    twist = [
        [phase(me, bits, bits, j / period, top) for j in range(local)] for top in range(2)
    ]
    for lesser_ref, start, size in zip(lesser_refs, starts_of(sizes), sizes):

        def run(k, carry, lesser_ref=lesser_ref, start=start):
            at = pl.ds(pl.multiple_of(k * TILE, TILE), TILE)
            to = pl.ds(pl.multiple_of(start + k * TILE, TILE), TILE)
            tops = []
            for top in range(2):
                values = []
                for t in range(local):
                    f = top * local + t
                    a = (lesser_ref[0, f, at], lesser_ref[1, f, at])
                    values.append(times(a, screened_ref[0, f, to], screened_ref[1, f, to]))
                values = dft(values, 1)
                tops.append(
                    [v if j == 0 else times(v, *twist[top][j]) for j, v in enumerate(values)]
                )
            for j in range(local):
                total = [tops[0][j][i] + tops[1][j][i] for i in range(2)]
                gap = times([tops[0][j][i] - tops[1][j][i] for i in range(2)], c, s)
                for i in range(2):
                    keep_ref[i, j, to] = jnp.where(mine == 1, gap[i], total[i])
                    send_ref[i, j, to] = jnp.where(mine == 1, total[i], gap[i])
            return carry

        lax.fori_loop(0, size // TILE, run, 0)


def backward_kernel(bit, bits, sizes, own_ref, got_ref, *outs):
    me = lax.axis_index("wide")
    local = own_ref.shape[1]
    had, mine = own_bit(me, bit - 1), own_bit(me, bit)
    low = bits - bit
    c, s = phase(me, bits, low, 1.0 / (1 << (low + 1)))
    for k, (start, size) in enumerate(zip(starts_of(sizes), sizes)):
        keep_ref, send_ref = outs[2 * k], outs[2 * k + 1]

        def run(i, carry, start=start, keep_ref=keep_ref, send_ref=send_ref):
            to = pl.ds(pl.multiple_of(i * TILE, TILE), TILE)
            at = pl.ds(pl.multiple_of(start + i * TILE, TILE), TILE)
            for j in range(local):
                pairs = [
                    split_first(own_ref[p, j, at], got_ref[p, j, at], had) for p in range(2)
                ]
                total = [pairs[p][0] + pairs[p][1] for p in range(2)]
                gap = times([pairs[p][0] - pairs[p][1] for p in range(2)], c, s)
                for p in range(2):
                    keep_ref[p, j, to] = jnp.where(mine == 1, gap[p], total[p])
                    send_ref[p, j, to] = jnp.where(mine == 1, total[p], gap[p])
            return carry

        lax.fori_loop(0, size // TILE, run, 0)


def add_kernel(own_ref, got_ref, out_ref):
    out_ref[...] = own_ref[...] + got_ref[...]


def chosen(slots, at_zero, at_one):
    return jnp.where(slots[0], at_zero, 0.0) + jnp.where(slots[1], at_one, 0.0)


def places_of(row):
    side = 1 - 2 * (row & 1)
    return [0, side, -side]


def prepare_coulomb(scale, offsets_ref, coulomb_ref, plain_ref, scaled_ref):
    row = lax.axis_index("cell")
    for slot, place in enumerate(places_of(row)):
        hit = [offsets_ref[0, j] == place for j in range(2)]
        value = chosen(hit, coulomb_ref[0, 0], coulomb_ref[0, 1])
        plain_ref[slot] = value
        scaled_ref[slot] = value * scale


def prepare_green(offsets_ref, green_ref, out_ref):
    row = lax.axis_index("cell")
    local, order = green_ref.shape[1], green_ref.shape[-1]
    for slot, place in enumerate(places_of(row)):
        hit = [offsets_ref[0, j] == place for j in range(2)]
        for e in range(local):
            re, im = (chosen(hit, green_ref[i, e, 0, 0], green_ref[i, e, 0, 1]) for i in range(2))
            out_ref[slot, e, :order, :order] = re
            out_ref[slot, e, :order, order:] = -im
            out_ref[slot, e, order:, :order] = im
            out_ref[slot, e, order:, order:] = re


def congruence(left, middle):
    order = middle.shape[-1]
    stacked = jnp.concatenate([middle[0], middle[1]], axis=-2)
    half = jnp.einsum("eab,ebc->eac", left, stacked, precision=HIGH)
    flat = jnp.concatenate([half[:, :order], half[:, order:]], axis=-1)
    out = jnp.einsum("eab,ecb->eac", flat, left, precision=HIGH)
    return jnp.stack([out[..., :order], out[..., order:]])


def body(green_pair, coulomb, green_retarded, offsets):
    peers, cells = lax.axis_size("wide"), lax.axis_size("cell")
    local, order = green_pair.shape[2], green_pair.shape[-1]
    bits = bits_of(peers)
    energies = peers * local
    scale = 1.0 / (2 * energies * energies)

    def swap(value, bit):
        return lax.ppermute(value, "wide", [(i, i ^ (1 << bit)) for i in range(peers)])

    links = []
    for first in range(2):
        up = [(i, i + 1) for i in range(first, cells - 1, 2)]
        links.append(up + [(j, i) for i, j in up])

    def beside(value):
        return [lax.ppermute(value, "cell", pairs) for pairs in links]

    pair = green_pair[:, :, :, 0]
    sizes = heights(order, FORWARD)
    keep = [
        lax.slice_in_dim(pair, at, at + size, axis=3) for at, size in zip(starts_of(sizes), sizes)
    ]
    got = [swap(k, bits - 1) for k in keep]
    plain, scaled = call(
        lambda *refs: prepare_coulomb(scale, *refs),
        [(3, order, order)] * 2, offsets, coulomb, smem=(0,),
    )
    left, = call(prepare_green, [(3, local, 2 * order, 2 * order)], offsets, green_retarded, smem=(0,))
    for stage in range(1, bits):
        for k in range(FORWARD):
            keep[k], send = call(
                lambda *refs: forward_kernel(stage, bits, *refs), [keep[k].shape] * 2, keep[k], got[k]
            )
            got[k] = swap(send, bits - 1 - stage)
    lesser, polar, near = [], [], []
    for k, size in enumerate(sizes):
        hat, product = call(
            lambda *refs: product_kernel(bits, *refs),
            [(2, 2 * local, size, order)] * 2, keep[k], got[k],
        )
        lesser.append(hat)
        polar.append(product)
        near.append([product] + beside(product))

    screened = 0.0
    for slot in range(3):
        whole = jnp.concatenate([n[slot] for n in near], axis=2)
        half = jnp.einsum("pfbc,dc->pfbd", whole, scaled[slot], precision=HIGH)
        screened = screened + jnp.einsum("ab,pfbd->pfad", plain[slot], half, precision=HIGH)

    keep, send = call(
        lambda *refs: inverse_kernel(bits, sizes, *refs),
        [(2, local, order, order)] * 2, *lesser, screened,
    )
    got = swap(send, 0)
    sizes = heights(order, BACKWARD)
    outs = call(
        lambda *refs: backward_kernel(1, bits, sizes, *refs),
        [(2, local, size, order) for size in sizes for _ in range(2)], keep, got,
    )
    keep, got = list(outs[0::2]), [swap(s, 1) for s in outs[1::2]]
    for bit in range(2, bits):
        for k, size in enumerate(sizes):
            keep[k], send = call(
                lambda *refs: backward_kernel(bit, bits, [size], *refs),
                [keep[k].shape] * 2, keep[k], got[k],
            )
            got[k] = swap(send, bit)
    near = []
    for k, size in enumerate(sizes):
        sigma, = call(add_kernel, [keep[k].shape], keep[k], got[k])
        near.append([sigma] + beside(sigma))
    result = 0.0
    for slot in range(3):
        middle = jnp.concatenate([n[slot] for n in near], axis=2)
        result = result + congruence(left[slot], middle)
    return result[:, :, None]


def solution(mesh):
    placed = (
        P(None, None, "wide", "cell", None, None),
        P("cell", None, None, None),
        P(None, "wide", "cell", None, None, None),
        P("cell", None),
    )
    return jax.shard_map(
        body,
        mesh=mesh,
        in_specs=placed,
        out_specs=P(None, "wide", "cell", None, None),
        check_vma=False,
    )
```

time: 141 us -> 109 us (0.77)
  blocking collectives: 68 us -> 0 us
  waiting for transfers between devices: 28.3 us -> 59 us
  starting transfers between devices: 12.6 us -> 33.5 us
  matrix products: 22.3 us -> 7.64 us
  Pallas kernels: 0 us -> 4.27 us
  between operations: 2.99 us -> 0.48 us
  local copies, waits for them, and re-layouts: 5.02 us -> 2.59 us
    all_to_all x4 -> x0, blocking collectives: 68 us -> none  [the longest x2 38.1 us: to_elements(): lax.all_to_all(pieces, 'wide', split_axis=4, concat_axis=2, tiled=True)]
    ppermute x4 -> x24, waiting for transfers between devices: 28.3 us -> 59 us  [the longest x14 36.8 us: swap(): lax.ppermute(value, 'wide', [(i, i ^ 1 << bit) for i in range(peers)])]
    ppermute x4 -> x24, starting transfers between devices: 12.6 us -> 33.5 us  [the longest x10 16.9 us: beside(): return [lax.ppermute(value, 'cell', pairs) for pairs in links]]
    dot_general x32 -> x12, matrix products: 22.3 us -> 7.64 us  [the longest x3 2.08 us: congruence(): out = jnp.einsum('eab,ecb->eac', flat, left, precision=HIGH)]
    pallas_call x0 -> x17, Pallas kernels: none -> 4.27 us  [call(): pl.pallas_call(kernel, out_shape=[jax.ShapeDtypeStruct(s, jnp.float32) fo...]
    unnamed x11 -> x8, local copies, waits for them, and re-layouts: 2.21 us -> 0.05 us
    slice x3 -> x5, local copies, waits for them, and re-layouts: 0.74 us -> 2.29 us  [the longest x2 2.18 us: body(): lax.slice_in_dim(pair, at, at + size, axis=3)]
  transfers between devices with their start and end apart: 4 -> 24, of which waited for: 4 -> 13; matrix products, arithmetic and copies ran while one was open for 1% -> 5% of each run, Pallas kernels for 0% -> 3%
where the time goes in v1:
time: 109 us; the launch traced here: 108 us
  waiting for transfers between devices  59 us (54%)
  starting transfers between devices  33.5 us (31%)
  matrix products  7.64 us (7%)
  Pallas kernels  4.27 us (4%)
  local copies, waits for them, and re-layouts  2.59 us (2%)
    ppermute x14, waiting for transfers between devices, swap(): lax.ppermute(value, 'wide', [(i, i ^ 1 << bit) for i in range(peers)])  36.8 us
    ppermute x10, waiting for transfers between devices, beside(): return [lax.ppermute(value, 'cell', pairs) for pairs in links]  22.3 us
    ppermute x10, starting transfers between devices, beside(): return [lax.ppermute(value, 'cell', pairs) for pairs in links]  16.9 us
    ppermute x14, starting transfers between devices, swap(): lax.ppermute(value, 'wide', [(i, i ^ 1 << bit) for i in range(peers)])  16.6 us
    pallas_call x17, Pallas kernels, call(): pl.pallas_call(kernel, out_shape=[jax.ShapeDtypeStruct(s, jnp.float32) fo...  4.27 us
  transfers between devices with their start and end apart: 24, of which 13 were waited for; matrix products, arithmetic and copies ran while one was open for 5% of the time, Pallas kernels for 3%

profile of v1, /device:TPU:0, one launch (start us, length us, event | category | flops | bytes accessed | tf_op | source)
XLA Modules:
  0.0 108.4 jit_solution(14623573839789525598)
XLA Ops:
  0.0 1.1 slice.121.refs_0_
  1.1 3.1 %collective-permute-start = (f32[2,2,4,48,128]{4,3,2,1,0:T(8,128)S(1)}, f32[2,2,4,48,128]{4,3,2,1,0:T(8,128)S(1)}, u32[]{:S(2)}, u32[]{:S(2)}) collective-permute-start(f32[2,2,4,48,128]{4,3,2,1,0:T(8,128)S(1)} %slice.121.refs_0_), channel_id=1, source_target_pairs={{0,16},{4,20},{8,24},{12,28},{16,0},{20,4},{24,8},{28,12},{1,17},{... | collective-permute-start | bytes 1179656 | tf_op jit(solution)/shard_map/ppermute | solution.py:285
  4.1 1.1 %fusion.70 = (f32[2,2,4,40,128]{4,3,2,1,0:T(8,128)S(1)}, f32[2,2,4,40,128]{4,3,2,1,0:T(8,128)S(1)}) fusion(f32[2,2,4,128,128]{4,3,2,1,0:T(8,128)} %bitcast.87), kind=kLoop, calls=%fused_computation.93 | loop fusion | bytes 1310720 | tf_op jit(solution)/shard_map/slice | solution.py:298
  5.3 2.0 %collective-permute-start.3 = (f32[2,2,4,40,128]{4,3,2,1,0:T(8,128)S(1)}, f32[2,2,4,40,128]{4,3,2,1,0:T(8,128)S(1)}, u32[]{:S(2)}, u32[]{:S(2)}) collective-permute-start(f32[2,2,4,40,128]{4,3,2,1,0:T(8,128)S(1)} %get-tuple-element.66.refs_0_), channel_id=1, source_target_pairs={{0,16},{4,20},{8,24},{12,28},{16,0},{20,4},{24,8},{28,12},{1,17},{... | collective-permute-start | bytes 983048 | tf_op jit(solution)/shard_map/ppermute | solution.py:285
  7.3 6.7 %collective-permute-done.refs_1_ = f32[2,2,4,48,128]{4,3,2,1,0:T(8,128)S(1)} collective-permute-done((f32[2,2,4,48,128]{4,3,2,1,0:T(8,128)S(1)}, f32[2,2,4,48,128]{4,3,2,1,0:T(8,128)S(1)}, u32[]{:S(2)}, u32[]{:S(2)}) %collective-permute-start) | collective-permute-done | bytes 393248 | tf_op jit(solution)/shard_map/ppermute | solution.py:285
  14.2 2.1 %collective-permute-start.1 = (f32[2,2,4,48,128]{4,3,2,1,0:T(8,128)S(1)}, f32[2,2,4,48,128]{4,3,2,1,0:T(8,128)S(1)}, u32[]{:S(2)}, u32[]{:S(2)}) collective-permute-start(f32[2,2,4,48,128]{4,3,2,1,0:T(8,128)S(1)} %get-tuple-element.36), channel_id=1, source_target_pairs={{0,8},{4,12},{8,0},{12,4},{16,24},{20,28},{24,16},{28,20},{1,9},{5... | collective-permute-start | bytes 1179656 | tf_op jit(solution)/shard_map/ppermute | solution.py:285
  16.3 4.8 %collective-permute-done.6.refs_1_ = f32[2,2,4,40,128]{4,3,2,1,0:T(8,128)S(1)} collective-permute-done((f32[2,2,4,40,128]{4,3,2,1,0:T(8,128)S(1)}, f32[2,2,4,40,128]{4,3,2,1,0:T(8,128)S(1)}, u32[]{:S(2)}, u32[]{:S(2)}) %collective-permute-start.6) | collective-permute-done | bytes 327712 | tf_op jit(solution)/shard_map/ppermute | solution.py:285
  21.2 2.1 %collective-permute-start.7 = (f32[2,2,4,40,128]{4,3,2,1,0:T(8,128)S(1)}, f32[2,2,4,40,128]{4,3,2,1,0:T(8,128)S(1)}, u32[]{:S(2)}, u32[]{:S(2)}) collective-permute-start(f32[2,2,4,40,128]{4,3,2,1,0:T(8,128)S(1)} %get-tuple-element.46), channel_id=1, source_target_pairs={{0,8},{4,12},{8,0},{12,4},{16,24},{20,28},{24,16},{28,20},{1,9},{5... | collective-permute-start | bytes 983048 | tf_op jit(solution)/shard_map/ppermute | solution.py:285
  23.3 4.0 %collective-permute-done.3.refs_1_ = f32[2,2,4,40,128]{4,3,2,1,0:T(8,128)S(1)} collective-permute-done((f32[2,2,4,40,128]{4,3,2,1,0:T(8,128)S(1)}, f32[2,2,4,40,128]{4,3,2,1,0:T(8,128)S(1)}, u32[]{:S(2)}, u32[]{:S(2)}) %collective-permute-start.3) | collective-permute-done | bytes 327712 | tf_op jit(solution)/shard_map/ppermute | solution.py:285
  27.4 1.8 %collective-permute-start.4 = (f32[2,2,4,40,128]{4,3,2,1,0:T(8,128)S(1)}, f32[2,2,4,40,128]{4,3,2,1,0:T(8,128)S(1)}, u32[]{:S(2)}, u32[]{:S(2)}) collective-permute-start(f32[2,2,4,40,128]{4,3,2,1,0:T(8,128)S(1)} %get-tuple-element.41), channel_id=1, source_target_pairs={{0,8},{4,12},{8,0},{12,4},{16,24},{20,28},{24,16},{28,20},{1,9},{5... | collective-permute-start | bytes 983048 | tf_op jit(solution)/shard_map/ppermute | solution.py:285
  29.4 2.8 %collective-permute-done.7.refs_1_ = f32[2,2,4,40,128]{4,3,2,1,0:T(8,128)S(1)} collective-permute-done((f32[2,2,4,40,128]{4,3,2,1,0:T(8,128)S(1)}, f32[2,2,4,40,128]{4,3,2,1,0:T(8,128)S(1)}, u32[]{:S(2)}, u32[]{:S(2)}) %collective-permute-start.7) | collective-permute-done | bytes 327712 | tf_op jit(solution)/shard_map/ppermute | solution.py:285
  32.3 5.4 %collective-permute-done.4.refs_1_ = f32[2,2,4,40,128]{4,3,2,1,0:T(8,128)S(1)} collective-permute-done((f32[2,2,4,40,128]{4,3,2,1,0:T(8,128)S(1)}, f32[2,2,4,40,128]{4,3,2,1,0:T(8,128)S(1)}, u32[]{:S(2)}, u32[]{:S(2)}) %collective-permute-start.4) | collective-permute-done | bytes 327712 | tf_op jit(solution)/shard_map/ppermute | solution.py:285
  39.6 4.4 %collective-permute-start.11 = (f32[2,8,40,128]{3,2,1,0:T(8,128)S(1)}, f32[2,8,40,128]{3,2,1,0:T(8,128)S(1)}, u32[]{:S(2)}, u32[]{:S(2)}) collective-permute-start(f32[2,8,40,128]{3,2,1,0:T(8,128)S(1)} %get-tuple-element.52), channel_id=1, source_target_pairs={{0,1},{2,3},{1,0},{3,2},{4,5},{6,7},{5,4},{7,6},{8,9},{10,11},{9,8... | collective-permute-start | bytes 983048 | tf_op jit(solution)/shard_map/ppermute | solution.py:293
  45.0 1.8 %collective-permute-start.10 = (f32[2,8,40,128]{3,2,1,0:T(8,128)S(1)}, f32[2,8,40,128]{3,2,1,0:T(8,128)S(1)}, u32[]{:S(2)}, u32[]{:S(2)}) collective-permute-start(f32[2,8,40,128]{3,2,1,0:T(8,128)S(1)} %get-tuple-element.51), channel_id=1, source_target_pairs={{0,1},{2,3},{1,0},{3,2},{4,5},{6,7},{5,4},{7,6},{8,9},{10,11},{9,8... | collective-permute-start | bytes 983048 | tf_op jit(solution)/shard_map/ppermute | solution.py:293
  48.6 3.9 %collective-permute-done.11 = f32[2,8,40,128]{3,2,1,0:T(8,128)S(1)} collective-permute-done((f32[2,8,40,128]{3,2,1,0:T(8,128)S(1)}, f32[2,8,40,128]{3,2,1,0:T(8,128)S(1)}, u32[]{:S(2)}, u32[]{:S(2)}) %collective-permute-start.11) | collective-permute-done | bytes 327712 | tf_op jit(solution)/shard_map/ppermute | solution.py:293
  53.2 6.3 %collective-permute-done.10 = f32[2,8,40,128]{3,2,1,0:T(8,128)S(1)} collective-permute-done((f32[2,8,40,128]{3,2,1,0:T(8,128)S(1)}, f32[2,8,40,128]{3,2,1,0:T(8,128)S(1)}, u32[]{:S(2)}, u32[]{:S(2)}) %collective-permute-start.10) | collective-permute-done | bytes 327712 | tf_op jit(solution)/shard_map/ppermute | solution.py:293
  59.6 7.9 %collective-permute-done.9 = f32[2,8,48,128]{3,2,1,0:T(8,128)S(1)} collective-permute-done((f32[2,8,48,128]{3,2,1,0:T(8,128)S(1)}, f32[2,8,48,128]{3,2,1,0:T(8,128)S(1)}, u32[]{:S(2)}, u32[]{:S(2)}) %collective-permute-start.9) | collective-permute-done | bytes 393248 | tf_op jit(solution)/shard_map/ppermute | solution.py:293
  70.7 1.9 %collective-permute-done.15.refs_1_ = f32[2,4,128,128]{3,2,1,0:T(8,128)S(1)} collective-permute-done((f32[2,4,128,128]{3,2,1,0:T(8,128)S(1)}, f32[2,4,128,128]{3,2,1,0:T(8,128)S(1)}, u32[]{:S(2)}, u32[]{:S(2)}) %collective-permute-start.15) | collective-permute-done | bytes 524320 | tf_op jit(solution)/shard_map/ppermute | solution.py:285
  72.8 1.6 %collective-permute-start.16 = (f32[2,4,64,128]{3,2,1,0:T(8,128)S(1)}, f32[2,4,64,128]{3,2,1,0:T(8,128)S(1)}, u32[]{:S(2)}, u32[]{:S(2)}) collective-permute-start(f32[2,4,64,128]{3,2,1,0:T(8,128)S(1)} %get-tuple-element.58), channel_id=1, source_target_pairs={{0,8},{4,12},{8,0},{12,4},{16,24},{20,28},{24,16},{28,20},{1,9},{5... | collective-permute-start | bytes 786440 | tf_op jit(solution)/shard_map/ppermute | solution.py:285
  74.9 7.1 %collective-permute-done.16.refs_1_ = f32[2,4,64,128]{3,2,1,0:T(8,128)S(1)} collective-permute-done((f32[2,4,64,128]{3,2,1,0:T(8,128)S(1)}, f32[2,4,64,128]{3,2,1,0:T(8,128)S(1)}, u32[]{:S(2)}, u32[]{:S(2)}) %collective-permute-start.16) | collective-permute-done | bytes 262176 | tf_op jit(solution)/shard_map/ppermute | solution.py:285
  82.2 1.6 %collective-permute-start.17 = (f32[2,4,64,128]{3,2,1,0:T(8,128)S(1)}, f32[2,4,64,128]{3,2,1,0:T(8,128)S(1)}, u32[]{:S(2)}, u32[]{:S(2)}) collective-permute-start(f32[2,4,64,128]{3,2,1,0:T(8,128)S(1)} %get-tuple-element.60), channel_id=1, source_target_pairs={{0,16},{4,20},{8,24},{12,28},{16,0},{20,4},{24,8},{28,12},{1,17},{... | collective-permute-start | bytes 786440 | tf_op jit(solution)/shard_map/ppermute | solution.py:285
  83.8 3.1 %collective-permute-done.18.refs_1_ = f32[2,4,64,128]{3,2,1,0:T(8,128)S(1)} collective-permute-done((f32[2,4,64,128]{3,2,1,0:T(8,128)S(1)}, f32[2,4,64,128]{3,2,1,0:T(8,128)S(1)}, u32[]{:S(2)}, u32[]{:S(2)}) %collective-permute-start.18) | collective-permute-done | bytes 262176 | tf_op jit(solution)/shard_map/ppermute | solution.py:285
  87.0 1.6 %collective-permute-start.19 = (f32[2,4,64,128]{3,2,1,0:T(8,128)S(1)}, f32[2,4,64,128]{3,2,1,0:T(8,128)S(1)}, u32[]{:S(2)}, u32[]{:S(2)}) collective-permute-start(f32[2,4,64,128]{3,2,1,0:T(8,128)S(1)} %get-tuple-element.64), channel_id=1, source_target_pairs={{0,16},{4,20},{8,24},{12,28},{16,0},{20,4},{24,8},{28,12},{1,17},{... | collective-permute-start | bytes 786440 | tf_op jit(solution)/shard_map/ppermute | solution.py:285
  88.6 0.9 shard_map.46
  90.2 3.5 %collective-permute-start.20 = (f32[2,4,64,128]{3,2,1,0:T(8,128)S(1)}, f32[2,4,64,128]{3,2,1,0:T(8,128)S(1)}, u32[]{:S(2)}, u32[]{:S(2)}) collective-permute-start(f32[2,4,64,128]{3,2,1,0:T(8,128)S(1)} %shard_map.60), channel_id=1, source_target_pairs={{0,1},{2,3},{1,0},{3,2},{4,5},{6,7},{5,4},{7,6},{8,9},{10,11},{9,8... | collective-permute-start | bytes 786440 | tf_op jit(solution)/shard_map/ppermute | solution.py:293
  93.7 0.9 collective-permute-done.19.got_ref
  95.3 3.5 %collective-permute-start.21 = (f32[2,4,64,128]{3,2,1,0:T(8,128)S(1)}, f32[2,4,64,128]{3,2,1,0:T(8,128)S(1)}, u32[]{:S(2)}, u32[]{:S(2)}) collective-permute-start(f32[2,4,64,128]{3,2,1,0:T(8,128)S(1)} %shard_map.62), channel_id=1, source_target_pairs={{0,1},{2,3},{1,0},{3,2},{4,5},{6,7},{5,4},{7,6},{8,9},{10,11},{9,8... | collective-permute-start | bytes 786440 | tf_op jit(solution)/shard_map/ppermute | solution.py:293
  99.5 0.7 fusion.19
  100.4 4.0 %collective-permute-done.21 = f32[2,4,64,128]{3,2,1,0:T(8,128)S(1)} collective-permute-done((f32[2,4,64,128]{3,2,1,0:T(8,128)S(1)}, f32[2,4,64,128]{3,2,1,0:T(8,128)S(1)}, u32[]{:S(2)}, u32[]{:S(2)}) %collective-permute-start.21) | collective-permute-done | bytes 262176 | tf_op jit(solution)/shard_map/ppermute | solution.py:293
  104.5 0.7 fusion.22
  106.0 0.7 fusion.21
  107.5 0.9 fusion.32
  (66 shorter events, 14.1 us)
Async XLA Ops:
  0.0 38.0 %copy-start.1 = (f32[1,2,128,128]{3,2,1,0:T(8,128)S(1)}, f32[1,2,128,128]{3,2,1,0:T(8,128)}, u32[]{:S(2)}) copy-start(f32[1,2,128,128]{3,2,1,0:T(8,128)} %refs_1_.1) | copy-start | bytes 393220
  0.0 38.0 %copy-start.2 = (s32[1,2]{1,0:T(1,128)S(1)}, s32[1,2]{1,0:T(1,128)}, u32[]{:S(2)}) copy-start(s32[1,2]{1,0:T(1,128)} %refs_0_.1) | copy-start | bytes 28
  1.1 13.0 %collective-permute-start = (f32[2,2,4,48,128]{4,3,2,1,0:T(8,128)S(1)}, f32[2,2,4,48,128]{4,3,2,1,0:T(8,128)S(1)}, u32[]{:S(2)}, u32[]{:S(2)}) collective-permute-start(f32[2,2,4,48,128]{4,3,2,1,0:T(8,128)S(1)} %slice.121.refs_0_), channel_id=1, source_target_pairs={{0,16},{4,20},{8,24},{12,28},{16,0},{20,4},{24,8},{28,12},{1,17},{... | collective-permute-start | bytes 1179656 | tf_op jit(solution)/shard_map/ppermute | solution.py:285
  5.3 15.9 %collective-permute-start.6 = (f32[2,2,4,40,128]{4,3,2,1,0:T(8,128)S(1)}, f32[2,2,4,40,128]{4,3,2,1,0:T(8,128)S(1)}, u32[]{:S(2)}, u32[]{:S(2)}) collective-permute-start(f32[2,2,4,40,128]{4,3,2,1,0:T(8,128)S(1)} %get-tuple-element.65.refs_0_), channel_id=1, source_target_pairs={{0,16},{4,20},{8,24},{12,28},{16,0},{20,4},{24,8},{28,12},{1,17},{... | collective-permute-start | bytes 983048 | tf_op jit(solution)/shard_map/ppermute | solution.py:285
  5.3 21.9 %collective-permute-start.3 = (f32[2,2,4,40,128]{4,3,2,1,0:T(8,128)S(1)}, f32[2,2,4,40,128]{4,3,2,1,0:T(8,128)S(1)}, u32[]{:S(2)}, u32[]{:S(2)}) collective-permute-start(f32[2,2,4,40,128]{4,3,2,1,0:T(8,128)S(1)} %get-tuple-element.66.refs_0_), channel_id=1, source_target_pairs={{0,16},{4,20},{8,24},{12,28},{16,0},{20,4},{24,8},{28,12},{1,17},{... | collective-permute-start | bytes 983048 | tf_op jit(solution)/shard_map/ppermute | solution.py:285
  14.2 15.0 %collective-permute-start.1 = (f32[2,2,4,48,128]{4,3,2,1,0:T(8,128)S(1)}, f32[2,2,4,48,128]{4,3,2,1,0:T(8,128)S(1)}, u32[]{:S(2)}, u32[]{:S(2)}) collective-permute-start(f32[2,2,4,48,128]{4,3,2,1,0:T(8,128)S(1)} %get-tuple-element.36), channel_id=1, source_target_pairs={{0,8},{4,12},{8,0},{12,4},{16,24},{20,28},{24,16},{28,20},{1,9},{5... | collective-permute-start | bytes 1179656 | tf_op jit(solution)/shard_map/ppermute | solution.py:285
  21.2 10.9 %collective-permute-start.7 = (f32[2,2,4,40,128]{4,3,2,1,0:T(8,128)S(1)}, f32[2,2,4,40,128]{4,3,2,1,0:T(8,128)S(1)}, u32[]{:S(2)}, u32[]{:S(2)}) collective-permute-start(f32[2,2,4,40,128]{4,3,2,1,0:T(8,128)S(1)} %get-tuple-element.46), channel_id=1, source_target_pairs={{0,8},{4,12},{8,0},{12,4},{16,24},{20,28},{24,16},{28,20},{1,9},{5... | collective-permute-start | bytes 983048 | tf_op jit(solution)/shard_map/ppermute | solution.py:285
  27.4 10.4 %collective-permute-start.4 = (f32[2,2,4,40,128]{4,3,2,1,0:T(8,128)S(1)}, f32[2,2,4,40,128]{4,3,2,1,0:T(8,128)S(1)}, u32[]{:S(2)}, u32[]{:S(2)}) collective-permute-start(f32[2,2,4,40,128]{4,3,2,1,0:T(8,128)S(1)} %get-tuple-element.41), channel_id=1, source_target_pairs={{0,8},{4,12},{8,0},{12,4},{16,24},{20,28},{24,16},{28,20},{1,9},{5... | collective-permute-start | bytes 983048 | tf_op jit(solution)/shard_map/ppermute | solution.py:285
  29.3 17.5 %collective-permute-start.2 = (f32[2,2,4,48,128]{4,3,2,1,0:T(8,128)S(1)}, f32[2,2,4,48,128]{4,3,2,1,0:T(8,128)S(1)}, u32[]{:S(2)}, u32[]{:S(2)}) collective-permute-start(f32[2,2,4,48,128]{4,3,2,1,0:T(8,128)S(1)} %get-tuple-element.38), channel_id=1, source_target_pairs={{0,4},{4,0},{8,12},{12,8},{16,20},{20,16},{24,28},{28,24},{1,5},{5... | collective-permute-start | bytes 1179656 | tf_op jit(solution)/shard_map/ppermute | solution.py:285
  32.3 6.3 %collective-permute-start.8 = (f32[2,2,4,40,128]{4,3,2,1,0:T(8,128)S(1)}, f32[2,2,4,40,128]{4,3,2,1,0:T(8,128)S(1)}, u32[]{:S(2)}, u32[]{:S(2)}) collective-permute-start(f32[2,2,4,40,128]{4,3,2,1,0:T(8,128)S(1)} %get-tuple-element.48), channel_id=1, source_target_pairs={{0,4},{4,0},{8,12},{12,8},{16,20},{20,16},{24,28},{28,24},{1,5},{5... | collective-permute-start | bytes 983048 | tf_op jit(solution)/shard_map/ppermute | solution.py:285
  37.9 6.1 %collective-permute-start.5 = (f32[2,2,4,40,128]{4,3,2,1,0:T(8,128)S(1)}, f32[2,2,4,40,128]{4,3,2,1,0:T(8,128)S(1)}, u32[]{:S(2)}, u32[]{:S(2)}) collective-permute-start(f32[2,2,4,40,128]{4,3,2,1,0:T(8,128)S(1)} %get-tuple-element.43), channel_id=1, source_target_pairs={{0,4},{4,0},{8,12},{12,8},{16,20},{20,16},{24,28},{28,24},{1,5},{5... | collective-permute-start | bytes 983048 | tf_op jit(solution)/shard_map/ppermute | solution.py:285
  38.9 29.8 %collective-permute-start.14 = (f32[2,8,40,128]{3,2,1,0:T(8,128)S(1)}, f32[2,8,40,128]{3,2,1,0:T(8,128)S(1)}, u32[]{:S(2)}, u32[]{:S(2)}) collective-permute-start(f32[2,8,40,128]{3,2,1,0:T(8,128)S(1)} %get-tuple-element.52), channel_id=1, source_target_pairs={{1,2},{2,1},{5,6},{6,5},{9,10},{10,9},{13,14},{14,13},{17,18},{18,... | collective-permute-start | bytes 983048 | tf_op jit(solution)/shard_map/ppermute | solution.py:293
  39.6 12.9 %collective-permute-start.11 = (f32[2,8,40,128]{3,2,1,0:T(8,128)S(1)}, f32[2,8,40,128]{3,2,1,0:T(8,128)S(1)}, u32[]{:S(2)}, u32[]{:S(2)}) collective-permute-start(f32[2,8,40,128]{3,2,1,0:T(8,128)S(1)} %get-tuple-element.52), channel_id=1, source_target_pairs={{0,1},{2,3},{1,0},{3,2},{4,5},{6,7},{5,4},{7,6},{8,9},{10,11},{9,8... | collective-permute-start | bytes 983048 | tf_op jit(solution)/shard_map/ppermute | solution.py:293
  44.3 24.4 %collective-permute-start.13 = (f32[2,8,40,128]{3,2,1,0:T(8,128)S(1)}, f32[2,8,40,128]{3,2,1,0:T(8,128)S(1)}, u32[]{:S(2)}, u32[]{:S(2)}) collective-permute-start(f32[2,8,40,128]{3,2,1,0:T(8,128)S(1)} %get-tuple-element.51), channel_id=1, source_target_pairs={{1,2},{2,1},{5,6},{6,5},{9,10},{10,9},{13,14},{14,13},{17,18},{18,... | collective-permute-start | bytes 983048 | tf_op jit(solution)/shard_map/ppermute | solution.py:293
  45.0 14.6 %collective-permute-start.10 = (f32[2,8,40,128]{3,2,1,0:T(8,128)S(1)}, f32[2,8,40,128]{3,2,1,0:T(8,128)S(1)}, u32[]{:S(2)}, u32[]{:S(2)}) collective-permute-start(f32[2,8,40,128]{3,2,1,0:T(8,128)S(1)} %get-tuple-element.51), channel_id=1, source_target_pairs={{0,1},{2,3},{1,0},{3,2},{4,5},{6,7},{5,4},{7,6},{8,9},{10,11},{9,8... | collective-permute-start | bytes 983048 | tf_op jit(solution)/shard_map/ppermute | solution.py:293
  47.1 20.4 %collective-permute-start.9 = (f32[2,8,48,128]{3,2,1,0:T(8,128)S(1)}, f32[2,8,48,128]{3,2,1,0:T(8,128)S(1)}, u32[]{:S(2)}, u32[]{:S(2)}) collective-permute-start(f32[2,8,48,128]{3,2,1,0:T(8,128)S(1)} %get-tuple-element.50), channel_id=1, source_target_pairs={{0,1},{2,3},{1,0},{3,2},{4,5},{6,7},{5,4},{7,6},{8,9},{10,11},{9,8... | collective-permute-start | bytes 1179656 | tf_op jit(solution)/shard_map/ppermute | solution.py:293
  52.5 16.2 %collective-permute-start.12 = (f32[2,8,48,128]{3,2,1,0:T(8,128)S(1)}, f32[2,8,48,128]{3,2,1,0:T(8,128)S(1)}, u32[]{:S(2)}, u32[]{:S(2)}) collective-permute-start(f32[2,8,48,128]{3,2,1,0:T(8,128)S(1)} %get-tuple-element.50), channel_id=1, source_target_pairs={{1,2},{2,1},{5,6},{6,5},{9,10},{10,9},{13,14},{14,13},{17,18},{18,... | collective-permute-start | bytes 1179656 | tf_op jit(solution)/shard_map/ppermute | solution.py:293
  69.3 19.3 %copy-start = (f32[2,4,1,2,128,128]{5,4,3,2,1,0:T(8,128)S(1)}, f32[2,4,1,2,128,128]{5,4,3,2,1,0:T(8,128)}, u32[]{:S(2)}) copy-start(f32[2,4,1,2,128,128]{5,4,3,2,1,0:T(8,128)} %green_ref.1) | copy-start | bytes 3145732
  70.6 2.0 %collective-permute-start.15 = (f32[2,4,128,128]{3,2,1,0:T(8,128)S(1)}, f32[2,4,128,128]{3,2,1,0:T(8,128)S(1)}, u32[]{:S(2)}, u32[]{:S(2)}) collective-permute-start(f32[2,4,128,128]{3,2,1,0:T(8,128)S(1)} %get-tuple-element.56), channel_id=1, source_target_pairs={{0,4},{4,0},{8,12},{12,8},{16,20},{20,16},{24,28},{28,24},{1,5},{5... | collective-permute-start | bytes 1572872 | tf_op jit(solution)/shard_map/ppermute | solution.py:285
  72.8 9.2 %collective-permute-start.16 = (f32[2,4,64,128]{3,2,1,0:T(8,128)S(1)}, f32[2,4,64,128]{3,2,1,0:T(8,128)S(1)}, u32[]{:S(2)}, u32[]{:S(2)}) collective-permute-start(f32[2,4,64,128]{3,2,1,0:T(8,128)S(1)} %get-tuple-element.58), channel_id=1, source_target_pairs={{0,8},{4,12},{8,0},{12,4},{16,24},{20,28},{24,16},{28,20},{1,9},{5... | collective-permute-start | bytes 786440 | tf_op jit(solution)/shard_map/ppermute | solution.py:285
  74.4 12.5 %collective-permute-start.18 = (f32[2,4,64,128]{3,2,1,0:T(8,128)S(1)}, f32[2,4,64,128]{3,2,1,0:T(8,128)S(1)}, u32[]{:S(2)}, u32[]{:S(2)}) collective-permute-start(f32[2,4,64,128]{3,2,1,0:T(8,128)S(1)} %get-tuple-element.62), channel_id=1, source_target_pairs={{0,8},{4,12},{8,0},{12,4},{16,24},{20,28},{24,16},{28,20},{1,9},{5... | collective-permute-start | bytes 786440 | tf_op jit(solution)/shard_map/ppermute | solution.py:285
  82.2 7.3 %collective-permute-start.17 = (f32[2,4,64,128]{3,2,1,0:T(8,128)S(1)}, f32[2,4,64,128]{3,2,1,0:T(8,128)S(1)}, u32[]{:S(2)}, u32[]{:S(2)}) collective-permute-start(f32[2,4,64,128]{3,2,1,0:T(8,128)S(1)} %get-tuple-element.60), channel_id=1, source_target_pairs={{0,16},{4,20},{8,24},{12,28},{16,0},{20,4},{24,8},{28,12},{1,17},{... | collective-permute-start | bytes 786440 | tf_op jit(solution)/shard_map/ppermute | solution.py:285
  87.0 7.6 %collective-permute-start.19 = (f32[2,4,64,128]{3,2,1,0:T(8,128)S(1)}, f32[2,4,64,128]{3,2,1,0:T(8,128)S(1)}, u32[]{:S(2)}, u32[]{:S(2)}) collective-permute-start(f32[2,4,64,128]{3,2,1,0:T(8,128)S(1)} %get-tuple-element.64), channel_id=1, source_target_pairs={{0,16},{4,20},{8,24},{12,28},{16,0},{20,4},{24,8},{28,12},{1,17},{... | collective-permute-start | bytes 786440 | tf_op jit(solution)/shard_map/ppermute | solution.py:285
  89.5 10.8 %collective-permute-start.22 = (f32[2,4,64,128]{3,2,1,0:T(8,128)S(1)}, f32[2,4,64,128]{3,2,1,0:T(8,128)S(1)}, u32[]{:S(2)}, u32[]{:S(2)}) collective-permute-start(f32[2,4,64,128]{3,2,1,0:T(8,128)S(1)} %shard_map.60), channel_id=1, source_target_pairs={{1,2},{2,1},{5,6},{6,5},{9,10},{10,9},{13,14},{14,13},{17,18},{18,... | collective-permute-start | bytes 786440 | tf_op jit(solution)/shard_map/ppermute | solution.py:293
  90.2 10.1 %collective-permute-start.20 = (f32[2,4,64,128]{3,2,1,0:T(8,128)S(1)}, f32[2,4,64,128]{3,2,1,0:T(8,128)S(1)}, u32[]{:S(2)}, u32[]{:S(2)}) collective-permute-start(f32[2,4,64,128]{3,2,1,0:T(8,128)S(1)} %shard_map.60), channel_id=1, source_target_pairs={{0,1},{2,3},{1,0},{3,2},{4,5},{6,7},{5,4},{7,6},{8,9},{10,11},{9,8... | collective-permute-start | bytes 786440 | tf_op jit(solution)/shard_map/ppermute | solution.py:293
  94.6 5.7 %collective-permute-start.23 = (f32[2,4,64,128]{3,2,1,0:T(8,128)S(1)}, f32[2,4,64,128]{3,2,1,0:T(8,128)S(1)}, u32[]{:S(2)}, u32[]{:S(2)}) collective-permute-start(f32[2,4,64,128]{3,2,1,0:T(8,128)S(1)} %shard_map.62), channel_id=1, source_target_pairs={{1,2},{2,1},{5,6},{6,5},{9,10},{10,9},{13,14},{14,13},{17,18},{18,... | collective-permute-start | bytes 786440 | tf_op jit(solution)/shard_map/ppermute | solution.py:293
  95.3 9.2 %collective-permute-start.21 = (f32[2,4,64,128]{3,2,1,0:T(8,128)S(1)}, f32[2,4,64,128]{3,2,1,0:T(8,128)S(1)}, u32[]{:S(2)}, u32[]{:S(2)}) collective-permute-start(f32[2,4,64,128]{3,2,1,0:T(8,128)S(1)} %shard_map.62), channel_id=1, source_target_pairs={{0,1},{2,3},{1,0},{3,2},{4,5},{6,7},{5,4},{7,6},{8,9},{10,11},{9,8... | collective-permute-start | bytes 786440 | tf_op jit(solution)/shard_map/ppermute | solution.py:293

commit v2 on v1

--- a/solution.py
+++ b/solution.py
@@ -1,3 +1,4 @@
+from functools import partial
 import math
 
 import jax
@@ -7,7 +8,7 @@
 from jax.experimental.pallas import tpu as pltpu
 from jax.sharding import PartitionSpec as P
 
-USES_PALLAS = True
+
 FORWARD = 3
 BACKWARD = 2
 HIGH = lax.Precision.HIGH
@@ -22,6 +23,11 @@
 
 def starts_of(sizes):
     return [sum(sizes[:k]) for k in range(len(sizes))]
+
+
+def waves(parts, stages):
+    pairs = [(k, stage) for k in range(parts) for stage in stages]
+    return sorted(pairs, key=lambda p: (p[0] + p[1], p[1]))
 
 
 def bits_of(peers):
@@ -290,34 +296,38 @@
         links.append(up + [(j, i) for i, j in up])
 
     def beside(value):
-        return [lax.ppermute(value, "cell", pairs) for pairs in links]
+        blocks = []
+        for pairs in links:
+            blocks.append(lax.ppermute(value, "cell", pairs))
+        return blocks
 
     pair = green_pair[:, :, :, 0]
     sizes = heights(order, FORWARD)
     keep = [
         lax.slice_in_dim(pair, at, at + size, axis=3) for at, size in zip(starts_of(sizes), sizes)
     ]
-    got = [swap(k, bits - 1) for k in keep]
+    got = [swap(own, bits - 1) for own in keep]
     plain, scaled = call(
-        lambda *refs: prepare_coulomb(scale, *refs),
+        partial(prepare_coulomb, scale),
         [(3, order, order)] * 2, offsets, coulomb, smem=(0,),
     )
-    left, = call(prepare_green, [(3, local, 2 * order, 2 * order)], offsets, green_retarded, smem=(0,))
-    for stage in range(1, bits):
-        for k in range(FORWARD):
-            keep[k], send = call(
-                lambda *refs: forward_kernel(stage, bits, *refs), [keep[k].shape] * 2, keep[k], got[k]
+    left, = call(
+        prepare_green, [(3, local, 2 * order, 2 * order)],
+        offsets, green_retarded, smem=(0,),
+    )
+    lesser, near = [None] * FORWARD, [None] * FORWARD
+    for k, stage in waves(FORWARD, range(1, bits)):
+        keep[k], send = call(
+            partial(forward_kernel, stage, bits),
+            [keep[k].shape] * 2, keep[k], got[k],
+        )
+        got[k] = swap(send, bits - 1 - stage)
+        if stage == bits - 1:
+            lesser[k], polar = call(
+                partial(product_kernel, bits),
+                [(2, 2 * local, sizes[k], order)] * 2, keep[k], got[k],
             )
-            got[k] = swap(send, bits - 1 - stage)
-    lesser, polar, near = [], [], []
-    for k, size in enumerate(sizes):
-        hat, product = call(
-            lambda *refs: product_kernel(bits, *refs),
-            [(2, 2 * local, size, order)] * 2, keep[k], got[k],
-        )
-        lesser.append(hat)
-        polar.append(product)
-        near.append([product] + beside(product))
+            near[k] = [polar] + beside(polar)
 
     screened = 0.0
     for slot in range(3):
@@ -326,27 +336,28 @@
         screened = screened + jnp.einsum("ab,pfbd->pfad", plain[slot], half, precision=HIGH)
 
     keep, send = call(
-        lambda *refs: inverse_kernel(bits, sizes, *refs),
+        partial(inverse_kernel, bits, sizes),
         [(2, local, order, order)] * 2, *lesser, screened,
     )
     got = swap(send, 0)
     sizes = heights(order, BACKWARD)
     outs = call(
-        lambda *refs: backward_kernel(1, bits, sizes, *refs),
+        partial(backward_kernel, 1, bits, sizes),
         [(2, local, size, order) for size in sizes for _ in range(2)], keep, got,
     )
-    keep, got = list(outs[0::2]), [swap(s, 1) for s in outs[1::2]]
-    for bit in range(2, bits):
-        for k, size in enumerate(sizes):
+    keep = list(outs[0::2])
+    got = [swap(send, 1) for send in outs[1::2]]
+    near = [None] * BACKWARD
+    for k, bit in waves(BACKWARD, range(2, bits + 1)):
+        if bit < bits:
             keep[k], send = call(
-                lambda *refs: backward_kernel(bit, bits, [size], *refs),
+                partial(backward_kernel, bit, bits, [sizes[k]]),
                 [keep[k].shape] * 2, keep[k], got[k],
             )
             got[k] = swap(send, bit)
-    near = []
-    for k, size in enumerate(sizes):
-        sigma, = call(add_kernel, [keep[k].shape], keep[k], got[k])
-        near.append([sigma] + beside(sigma))
+        else:
+            sigma, = call(add_kernel, [keep[k].shape], keep[k], got[k])
+            near[k] = [sigma] + beside(sigma)
     result = 0.0
     for slot in range(3):
         middle = jnp.concatenate([n[slot] for n in near], axis=2)
@@ -361,6 +372,7 @@
         P(None, "wide", "cell", None, None, None),
         P("cell", None),
     )
+
     return jax.shard_map(
         body,
         mesh=mesh,

time: 109 us -> 109 us (level)
  no operation moved by 1% of the time
where the time goes in v2:
time: 109 us; the launch traced here: 108 us
  waiting for transfers between devices  59 us (54%)
  starting transfers between devices  33.5 us (31%)
  matrix products  7.64 us (7%)
  Pallas kernels  4.27 us (4%)
  local copies, waits for them, and re-layouts  2.59 us (2%)
    ppermute x14, waiting for transfers between devices, swap(): lax.ppermute(value, 'wide', [(i, i ^ 1 << bit) for i in range(peers)])  36.8 us
    ppermute x10, waiting for transfers between devices, beside(): blocks.append(lax.ppermute(value, 'cell', pairs))  22.3 us
    ppermute x10, starting transfers between devices, beside(): blocks.append(lax.ppermute(value, 'cell', pairs))  16.9 us
    ppermute x14, starting transfers between devices, swap(): lax.ppermute(value, 'wide', [(i, i ^ 1 << bit) for i in range(peers)])  16.6 us
    pallas_call x17, Pallas kernels, call(): pl.pallas_call(kernel, out_shape=[jax.ShapeDtypeStruct(s, jnp.float32) fo...  4.27 us
  transfers between devices with their start and end apart: 24, of which 13 were waited for; matrix products, arithmetic and copies ran while one was open for 5% of the time, Pallas kernels for 3%

profile of v2, /device:TPU:0, one launch (start us, length us, event | category | flops | bytes accessed | tf_op | source)
XLA Modules:
  0.0 108.4 jit_solution(14623573839789525598)
XLA Ops:
  0.0 1.1 slice.121.own_ref
  1.1 3.1 %collective-permute-start = (f32[2,2,4,48,128]{4,3,2,1,0:T(8,128)S(1)}, f32[2,2,4,48,128]{4,3,2,1,0:T(8,128)S(1)}, u32[]{:S(2)}, u32[]{:S(2)}) collective-permute-start(f32[2,2,4,48,128]{4,3,2,1,0:T(8,128)S(1)} %slice.121.own_ref), channel_id=1, source_target_pairs={{0,16},{4,20},{8,24},{12,28},{16,0},{20,4},{24,8},{28,12},{1,17},{... | collective-permute-start | bytes 1179656 | tf_op jit(solution)/shard_map/ppermute | solution.py:291
  4.1 1.1 %fusion.70 = (f32[2,2,4,40,128]{4,3,2,1,0:T(8,128)S(1)}, f32[2,2,4,40,128]{4,3,2,1,0:T(8,128)S(1)}) fusion(f32[2,2,4,128,128]{4,3,2,1,0:T(8,128)} %bitcast.87), kind=kLoop, calls=%fused_computation.93 | loop fusion | bytes 1310720 | tf_op jit(solution)/shard_map/slice | solution.py:307
  5.3 2.0 %collective-permute-start.3 = (f32[2,2,4,40,128]{4,3,2,1,0:T(8,128)S(1)}, f32[2,2,4,40,128]{4,3,2,1,0:T(8,128)S(1)}, u32[]{:S(2)}, u32[]{:S(2)}) collective-permute-start(f32[2,2,4,40,128]{4,3,2,1,0:T(8,128)S(1)} %get-tuple-element.66.own_ref), channel_id=1, source_target_pairs={{0,16},{4,20},{8,24},{12,28},{16,0},{20,4},{24,8},{28,12},{1,17},{... | collective-permute-start | bytes 983048 | tf_op jit(solution)/shard_map/ppermute | solution.py:291
  7.3 6.7 %collective-permute-done.got_ref = f32[2,2,4,48,128]{4,3,2,1,0:T(8,128)S(1)} collective-permute-done((f32[2,2,4,48,128]{4,3,2,1,0:T(8,128)S(1)}, f32[2,2,4,48,128]{4,3,2,1,0:T(8,128)S(1)}, u32[]{:S(2)}, u32[]{:S(2)}) %collective-permute-start) | collective-permute-done | bytes 393248 | tf_op jit(solution)/shard_map/ppermute | solution.py:291
  14.2 2.1 %collective-permute-start.1 = (f32[2,2,4,48,128]{4,3,2,1,0:T(8,128)S(1)}, f32[2,2,4,48,128]{4,3,2,1,0:T(8,128)S(1)}, u32[]{:S(2)}, u32[]{:S(2)}) collective-permute-start(f32[2,2,4,48,128]{4,3,2,1,0:T(8,128)S(1)} %get-tuple-element.36), channel_id=1, source_target_pairs={{0,8},{4,12},{8,0},{12,4},{16,24},{20,28},{24,16},{28,20},{1,9},{5... | collective-permute-start | bytes 1179656 | tf_op jit(solution)/shard_map/ppermute | solution.py:291
  16.3 4.8 %collective-permute-done.6.got_ref = f32[2,2,4,40,128]{4,3,2,1,0:T(8,128)S(1)} collective-permute-done((f32[2,2,4,40,128]{4,3,2,1,0:T(8,128)S(1)}, f32[2,2,4,40,128]{4,3,2,1,0:T(8,128)S(1)}, u32[]{:S(2)}, u32[]{:S(2)}) %collective-permute-start.6) | collective-permute-done | bytes 327712 | tf_op jit(solution)/shard_map/ppermute | solution.py:291
  21.2 2.1 %collective-permute-start.7 = (f32[2,2,4,40,128]{4,3,2,1,0:T(8,128)S(1)}, f32[2,2,4,40,128]{4,3,2,1,0:T(8,128)S(1)}, u32[]{:S(2)}, u32[]{:S(2)}) collective-permute-start(f32[2,2,4,40,128]{4,3,2,1,0:T(8,128)S(1)} %get-tuple-element.46), channel_id=1, source_target_pairs={{0,8},{4,12},{8,0},{12,4},{16,24},{20,28},{24,16},{28,20},{1,9},{5... | collective-permute-start | bytes 983048 | tf_op jit(solution)/shard_map/ppermute | solution.py:291
  23.3 4.0 %collective-permute-done.3.got_ref = f32[2,2,4,40,128]{4,3,2,1,0:T(8,128)S(1)} collective-permute-done((f32[2,2,4,40,128]{4,3,2,1,0:T(8,128)S(1)}, f32[2,2,4,40,128]{4,3,2,1,0:T(8,128)S(1)}, u32[]{:S(2)}, u32[]{:S(2)}) %collective-permute-start.3) | collective-permute-done | bytes 327712 | tf_op jit(solution)/shard_map/ppermute | solution.py:291
  27.4 1.8 %collective-permute-start.4 = (f32[2,2,4,40,128]{4,3,2,1,0:T(8,128)S(1)}, f32[2,2,4,40,128]{4,3,2,1,0:T(8,128)S(1)}, u32[]{:S(2)}, u32[]{:S(2)}) collective-permute-start(f32[2,2,4,40,128]{4,3,2,1,0:T(8,128)S(1)} %get-tuple-element.41), channel_id=1, source_target_pairs={{0,8},{4,12},{8,0},{12,4},{16,24},{20,28},{24,16},{28,20},{1,9},{5... | collective-permute-start | bytes 983048 | tf_op jit(solution)/shard_map/ppermute | solution.py:291
  29.4 2.8 %collective-permute-done.7.got_ref = f32[2,2,4,40,128]{4,3,2,1,0:T(8,128)S(1)} collective-permute-done((f32[2,2,4,40,128]{4,3,2,1,0:T(8,128)S(1)}, f32[2,2,4,40,128]{4,3,2,1,0:T(8,128)S(1)}, u32[]{:S(2)}, u32[]{:S(2)}) %collective-permute-start.7) | collective-permute-done | bytes 327712 | tf_op jit(solution)/shard_map/ppermute | solution.py:291
  32.3 5.4 %collective-permute-done.4.got_ref = f32[2,2,4,40,128]{4,3,2,1,0:T(8,128)S(1)} collective-permute-done((f32[2,2,4,40,128]{4,3,2,1,0:T(8,128)S(1)}, f32[2,2,4,40,128]{4,3,2,1,0:T(8,128)S(1)}, u32[]{:S(2)}, u32[]{:S(2)}) %collective-permute-start.4) | collective-permute-done | bytes 327712 | tf_op jit(solution)/shard_map/ppermute | solution.py:291
  39.6 4.4 %collective-permute-start.11 = (f32[2,8,40,128]{3,2,1,0:T(8,128)S(1)}, f32[2,8,40,128]{3,2,1,0:T(8,128)S(1)}, u32[]{:S(2)}, u32[]{:S(2)}) collective-permute-start(f32[2,8,40,128]{3,2,1,0:T(8,128)S(1)} %get-tuple-element.52), channel_id=1, source_target_pairs={{0,1},{2,3},{1,0},{3,2},{4,5},{6,7},{5,4},{7,6},{8,9},{10,11},{9,8... | collective-permute-start | bytes 983048 | tf_op jit(solution)/shard_map/ppermute | solution.py:301
  45.0 1.8 %collective-permute-start.10 = (f32[2,8,40,128]{3,2,1,0:T(8,128)S(1)}, f32[2,8,40,128]{3,2,1,0:T(8,128)S(1)}, u32[]{:S(2)}, u32[]{:S(2)}) collective-permute-start(f32[2,8,40,128]{3,2,1,0:T(8,128)S(1)} %get-tuple-element.51), channel_id=1, source_target_pairs={{0,1},{2,3},{1,0},{3,2},{4,5},{6,7},{5,4},{7,6},{8,9},{10,11},{9,8... | collective-permute-start | bytes 983048 | tf_op jit(solution)/shard_map/ppermute | solution.py:301
  48.6 3.9 %collective-permute-done.11 = f32[2,8,40,128]{3,2,1,0:T(8,128)S(1)} collective-permute-done((f32[2,8,40,128]{3,2,1,0:T(8,128)S(1)}, f32[2,8,40,128]{3,2,1,0:T(8,128)S(1)}, u32[]{:S(2)}, u32[]{:S(2)}) %collective-permute-start.11) | collective-permute-done | bytes 327712 | tf_op jit(solution)/shard_map/ppermute | solution.py:301
  53.2 6.3 %collective-permute-done.10 = f32[2,8,40,128]{3,2,1,0:T(8,128)S(1)} collective-permute-done((f32[2,8,40,128]{3,2,1,0:T(8,128)S(1)}, f32[2,8,40,128]{3,2,1,0:T(8,128)S(1)}, u32[]{:S(2)}, u32[]{:S(2)}) %collective-permute-start.10) | collective-permute-done | bytes 327712 | tf_op jit(solution)/shard_map/ppermute | solution.py:301
  59.6 7.9 %collective-permute-done.9 = f32[2,8,48,128]{3,2,1,0:T(8,128)S(1)} collective-permute-done((f32[2,8,48,128]{3,2,1,0:T(8,128)S(1)}, f32[2,8,48,128]{3,2,1,0:T(8,128)S(1)}, u32[]{:S(2)}, u32[]{:S(2)}) %collective-permute-start.9) | collective-permute-done | bytes 393248 | tf_op jit(solution)/shard_map/ppermute | solution.py:301
  70.7 1.9 %collective-permute-done.15.got_ref = f32[2,4,128,128]{3,2,1,0:T(8,128)S(1)} collective-permute-done((f32[2,4,128,128]{3,2,1,0:T(8,128)S(1)}, f32[2,4,128,128]{3,2,1,0:T(8,128)S(1)}, u32[]{:S(2)}, u32[]{:S(2)}) %collective-permute-start.15) | collective-permute-done | bytes 524320 | tf_op jit(solution)/shard_map/ppermute | solution.py:291
  72.8 1.6 %collective-permute-start.16 = (f32[2,4,64,128]{3,2,1,0:T(8,128)S(1)}, f32[2,4,64,128]{3,2,1,0:T(8,128)S(1)}, u32[]{:S(2)}, u32[]{:S(2)}) collective-permute-start(f32[2,4,64,128]{3,2,1,0:T(8,128)S(1)} %get-tuple-element.58), channel_id=1, source_target_pairs={{0,8},{4,12},{8,0},{12,4},{16,24},{20,28},{24,16},{28,20},{1,9},{5... | collective-permute-start | bytes 786440 | tf_op jit(solution)/shard_map/ppermute | solution.py:291
  74.9 7.1 %collective-permute-done.16.got_ref = f32[2,4,64,128]{3,2,1,0:T(8,128)S(1)} collective-permute-done((f32[2,4,64,128]{3,2,1,0:T(8,128)S(1)}, f32[2,4,64,128]{3,2,1,0:T(8,128)S(1)}, u32[]{:S(2)}, u32[]{:S(2)}) %collective-permute-start.16) | collective-permute-done | bytes 262176 | tf_op jit(solution)/shard_map/ppermute | solution.py:291
  82.2 1.6 %collective-permute-start.17 = (f32[2,4,64,128]{3,2,1,0:T(8,128)S(1)}, f32[2,4,64,128]{3,2,1,0:T(8,128)S(1)}, u32[]{:S(2)}, u32[]{:S(2)}) collective-permute-start(f32[2,4,64,128]{3,2,1,0:T(8,128)S(1)} %get-tuple-element.60), channel_id=1, source_target_pairs={{0,16},{4,20},{8,24},{12,28},{16,0},{20,4},{24,8},{28,12},{1,17},{... | collective-permute-start | bytes 786440 | tf_op jit(solution)/shard_map/ppermute | solution.py:291
  83.8 3.1 %collective-permute-done.18.got_ref = f32[2,4,64,128]{3,2,1,0:T(8,128)S(1)} collective-permute-done((f32[2,4,64,128]{3,2,1,0:T(8,128)S(1)}, f32[2,4,64,128]{3,2,1,0:T(8,128)S(1)}, u32[]{:S(2)}, u32[]{:S(2)}) %collective-permute-start.18) | collective-permute-done | bytes 262176 | tf_op jit(solution)/shard_map/ppermute | solution.py:291
  87.0 1.6 %collective-permute-start.19 = (f32[2,4,64,128]{3,2,1,0:T(8,128)S(1)}, f32[2,4,64,128]{3,2,1,0:T(8,128)S(1)}, u32[]{:S(2)}, u32[]{:S(2)}) collective-permute-start(f32[2,4,64,128]{3,2,1,0:T(8,128)S(1)} %get-tuple-element.64), channel_id=1, source_target_pairs={{0,16},{4,20},{8,24},{12,28},{16,0},{20,4},{24,8},{28,12},{1,17},{... | collective-permute-start | bytes 786440 | tf_op jit(solution)/shard_map/ppermute | solution.py:291
  88.6 0.9 shard_map.46
  90.2 3.5 %collective-permute-start.20 = (f32[2,4,64,128]{3,2,1,0:T(8,128)S(1)}, f32[2,4,64,128]{3,2,1,0:T(8,128)S(1)}, u32[]{:S(2)}, u32[]{:S(2)}) collective-permute-start(f32[2,4,64,128]{3,2,1,0:T(8,128)S(1)} %shard_map.60), channel_id=1, source_target_pairs={{0,1},{2,3},{1,0},{3,2},{4,5},{6,7},{5,4},{7,6},{8,9},{10,11},{9,8... | collective-permute-start | bytes 786440 | tf_op jit(solution)/shard_map/ppermute | solution.py:301
  93.7 0.9 collective-permute-done.19.got_ref
  95.3 3.5 %collective-permute-start.21 = (f32[2,4,64,128]{3,2,1,0:T(8,128)S(1)}, f32[2,4,64,128]{3,2,1,0:T(8,128)S(1)}, u32[]{:S(2)}, u32[]{:S(2)}) collective-permute-start(f32[2,4,64,128]{3,2,1,0:T(8,128)S(1)} %shard_map.62), channel_id=1, source_target_pairs={{0,1},{2,3},{1,0},{3,2},{4,5},{6,7},{5,4},{7,6},{8,9},{10,11},{9,8... | collective-permute-start | bytes 786440 | tf_op jit(solution)/shard_map/ppermute | solution.py:301
  99.5 0.7 fusion.19
  100.4 4.0 %collective-permute-done.21 = f32[2,4,64,128]{3,2,1,0:T(8,128)S(1)} collective-permute-done((f32[2,4,64,128]{3,2,1,0:T(8,128)S(1)}, f32[2,4,64,128]{3,2,1,0:T(8,128)S(1)}, u32[]{:S(2)}, u32[]{:S(2)}) %collective-permute-start.21) | collective-permute-done | bytes 262176 | tf_op jit(solution)/shard_map/ppermute | solution.py:301
  104.5 0.7 fusion.22
  106.0 0.7 fusion.21
  107.5 0.9 fusion.32
  (66 shorter events, 14.1 us)
Async XLA Ops:
  0.0 38.0 %copy-start.1 = (f32[1,2,128,128]{3,2,1,0:T(8,128)S(1)}, f32[1,2,128,128]{3,2,1,0:T(8,128)}, u32[]{:S(2)}) copy-start(f32[1,2,128,128]{3,2,1,0:T(8,128)} %coulomb_ref.1) | copy-start | bytes 393220
  0.0 38.0 %copy-start.2 = (s32[1,2]{1,0:T(1,128)S(1)}, s32[1,2]{1,0:T(1,128)}, u32[]{:S(2)}) copy-start(s32[1,2]{1,0:T(1,128)} %offsets_ref.3) | copy-start | bytes 28
  1.1 13.0 %collective-permute-start = (f32[2,2,4,48,128]{4,3,2,1,0:T(8,128)S(1)}, f32[2,2,4,48,128]{4,3,2,1,0:T(8,128)S(1)}, u32[]{:S(2)}, u32[]{:S(2)}) collective-permute-start(f32[2,2,4,48,128]{4,3,2,1,0:T(8,128)S(1)} %slice.121.own_ref), channel_id=1, source_target_pairs={{0,16},{4,20},{8,24},{12,28},{16,0},{20,4},{24,8},{28,12},{1,17},{... | collective-permute-start | bytes 1179656 | tf_op jit(solution)/shard_map/ppermute | solution.py:291
  5.3 15.9 %collective-permute-start.6 = (f32[2,2,4,40,128]{4,3,2,1,0:T(8,128)S(1)}, f32[2,2,4,40,128]{4,3,2,1,0:T(8,128)S(1)}, u32[]{:S(2)}, u32[]{:S(2)}) collective-permute-start(f32[2,2,4,40,128]{4,3,2,1,0:T(8,128)S(1)} %get-tuple-element.65.own_ref), channel_id=1, source_target_pairs={{0,16},{4,20},{8,24},{12,28},{16,0},{20,4},{24,8},{28,12},{1,17},{... | collective-permute-start | bytes 983048 | tf_op jit(solution)/shard_map/ppermute | solution.py:291
  5.3 21.9 %collective-permute-start.3 = (f32[2,2,4,40,128]{4,3,2,1,0:T(8,128)S(1)}, f32[2,2,4,40,128]{4,3,2,1,0:T(8,128)S(1)}, u32[]{:S(2)}, u32[]{:S(2)}) collective-permute-start(f32[2,2,4,40,128]{4,3,2,1,0:T(8,128)S(1)} %get-tuple-element.66.own_ref), channel_id=1, source_target_pairs={{0,16},{4,20},{8,24},{12,28},{16,0},{20,4},{24,8},{28,12},{1,17},{... | collective-permute-start | bytes 983048 | tf_op jit(solution)/shard_map/ppermute | solution.py:291
  14.2 15.0 %collective-permute-start.1 = (f32[2,2,4,48,128]{4,3,2,1,0:T(8,128)S(1)}, f32[2,2,4,48,128]{4,3,2,1,0:T(8,128)S(1)}, u32[]{:S(2)}, u32[]{:S(2)}) collective-permute-start(f32[2,2,4,48,128]{4,3,2,1,0:T(8,128)S(1)} %get-tuple-element.36), channel_id=1, source_target_pairs={{0,8},{4,12},{8,0},{12,4},{16,24},{20,28},{24,16},{28,20},{1,9},{5... | collective-permute-start | bytes 1179656 | tf_op jit(solution)/shard_map/ppermute | solution.py:291
  21.2 10.9 %collective-permute-start.7 = (f32[2,2,4,40,128]{4,3,2,1,0:T(8,128)S(1)}, f32[2,2,4,40,128]{4,3,2,1,0:T(8,128)S(1)}, u32[]{:S(2)}, u32[]{:S(2)}) collective-permute-start(f32[2,2,4,40,128]{4,3,2,1,0:T(8,128)S(1)} %get-tuple-element.46), channel_id=1, source_target_pairs={{0,8},{4,12},{8,0},{12,4},{16,24},{20,28},{24,16},{28,20},{1,9},{5... | collective-permute-start | bytes 983048 | tf_op jit(solution)/shard_map/ppermute | solution.py:291
  27.4 10.4 %collective-permute-start.4 = (f32[2,2,4,40,128]{4,3,2,1,0:T(8,128)S(1)}, f32[2,2,4,40,128]{4,3,2,1,0:T(8,128)S(1)}, u32[]{:S(2)}, u32[]{:S(2)}) collective-permute-start(f32[2,2,4,40,128]{4,3,2,1,0:T(8,128)S(1)} %get-tuple-element.41), channel_id=1, source_target_pairs={{0,8},{4,12},{8,0},{12,4},{16,24},{20,28},{24,16},{28,20},{1,9},{5... | collective-permute-start | bytes 983048 | tf_op jit(solution)/shard_map/ppermute | solution.py:291
  29.3 17.5 %collective-permute-start.2 = (f32[2,2,4,48,128]{4,3,2,1,0:T(8,128)S(1)}, f32[2,2,4,48,128]{4,3,2,1,0:T(8,128)S(1)}, u32[]{:S(2)}, u32[]{:S(2)}) collective-permute-start(f32[2,2,4,48,128]{4,3,2,1,0:T(8,128)S(1)} %get-tuple-element.38), channel_id=1, source_target_pairs={{0,4},{4,0},{8,12},{12,8},{16,20},{20,16},{24,28},{28,24},{1,5},{5... | collective-permute-start | bytes 1179656 | tf_op jit(solution)/shard_map/ppermute | solution.py:291
  32.3 6.3 %collective-permute-start.8 = (f32[2,2,4,40,128]{4,3,2,1,0:T(8,128)S(1)}, f32[2,2,4,40,128]{4,3,2,1,0:T(8,128)S(1)}, u32[]{:S(2)}, u32[]{:S(2)}) collective-permute-start(f32[2,2,4,40,128]{4,3,2,1,0:T(8,128)S(1)} %get-tuple-element.48), channel_id=1, source_target_pairs={{0,4},{4,0},{8,12},{12,8},{16,20},{20,16},{24,28},{28,24},{1,5},{5... | collective-permute-start | bytes 983048 | tf_op jit(solution)/shard_map/ppermute | solution.py:291
  37.9 6.1 %collective-permute-start.5 = (f32[2,2,4,40,128]{4,3,2,1,0:T(8,128)S(1)}, f32[2,2,4,40,128]{4,3,2,1,0:T(8,128)S(1)}, u32[]{:S(2)}, u32[]{:S(2)}) collective-permute-start(f32[2,2,4,40,128]{4,3,2,1,0:T(8,128)S(1)} %get-tuple-element.43), channel_id=1, source_target_pairs={{0,4},{4,0},{8,12},{12,8},{16,20},{20,16},{24,28},{28,24},{1,5},{5... | collective-permute-start | bytes 983048 | tf_op jit(solution)/shard_map/ppermute | solution.py:291
  38.9 29.8 %collective-permute-start.14 = (f32[2,8,40,128]{3,2,1,0:T(8,128)S(1)}, f32[2,8,40,128]{3,2,1,0:T(8,128)S(1)}, u32[]{:S(2)}, u32[]{:S(2)}) collective-permute-start(f32[2,8,40,128]{3,2,1,0:T(8,128)S(1)} %get-tuple-element.52), channel_id=1, source_target_pairs={{1,2},{2,1},{5,6},{6,5},{9,10},{10,9},{13,14},{14,13},{17,18},{18,... | collective-permute-start | bytes 983048 | tf_op jit(solution)/shard_map/ppermute | solution.py:301
  39.6 12.9 %collective-permute-start.11 = (f32[2,8,40,128]{3,2,1,0:T(8,128)S(1)}, f32[2,8,40,128]{3,2,1,0:T(8,128)S(1)}, u32[]{:S(2)}, u32[]{:S(2)}) collective-permute-start(f32[2,8,40,128]{3,2,1,0:T(8,128)S(1)} %get-tuple-element.52), channel_id=1, source_target_pairs={{0,1},{2,3},{1,0},{3,2},{4,5},{6,7},{5,4},{7,6},{8,9},{10,11},{9,8... | collective-permute-start | bytes 983048 | tf_op jit(solution)/shard_map/ppermute | solution.py:301
  44.3 24.4 %collective-permute-start.13 = (f32[2,8,40,128]{3,2,1,0:T(8,128)S(1)}, f32[2,8,40,128]{3,2,1,0:T(8,128)S(1)}, u32[]{:S(2)}, u32[]{:S(2)}) collective-permute-start(f32[2,8,40,128]{3,2,1,0:T(8,128)S(1)} %get-tuple-element.51), channel_id=1, source_target_pairs={{1,2},{2,1},{5,6},{6,5},{9,10},{10,9},{13,14},{14,13},{17,18},{18,... | collective-permute-start | bytes 983048 | tf_op jit(solution)/shard_map/ppermute | solution.py:301
  45.0 14.6 %collective-permute-start.10 = (f32[2,8,40,128]{3,2,1,0:T(8,128)S(1)}, f32[2,8,40,128]{3,2,1,0:T(8,128)S(1)}, u32[]{:S(2)}, u32[]{:S(2)}) collective-permute-start(f32[2,8,40,128]{3,2,1,0:T(8,128)S(1)} %get-tuple-element.51), channel_id=1, source_target_pairs={{0,1},{2,3},{1,0},{3,2},{4,5},{6,7},{5,4},{7,6},{8,9},{10,11},{9,8... | collective-permute-start | bytes 983048 | tf_op jit(solution)/shard_map/ppermute | solution.py:301
  47.1 20.4 %collective-permute-start.9 = (f32[2,8,48,128]{3,2,1,0:T(8,128)S(1)}, f32[2,8,48,128]{3,2,1,0:T(8,128)S(1)}, u32[]{:S(2)}, u32[]{:S(2)}) collective-permute-start(f32[2,8,48,128]{3,2,1,0:T(8,128)S(1)} %get-tuple-element.50), channel_id=1, source_target_pairs={{0,1},{2,3},{1,0},{3,2},{4,5},{6,7},{5,4},{7,6},{8,9},{10,11},{9,8... | collective-permute-start | bytes 1179656 | tf_op jit(solution)/shard_map/ppermute | solution.py:301
  52.5 16.2 %collective-permute-start.12 = (f32[2,8,48,128]{3,2,1,0:T(8,128)S(1)}, f32[2,8,48,128]{3,2,1,0:T(8,128)S(1)}, u32[]{:S(2)}, u32[]{:S(2)}) collective-permute-start(f32[2,8,48,128]{3,2,1,0:T(8,128)S(1)} %get-tuple-element.50), channel_id=1, source_target_pairs={{1,2},{2,1},{5,6},{6,5},{9,10},{10,9},{13,14},{14,13},{17,18},{18,... | collective-permute-start | bytes 1179656 | tf_op jit(solution)/shard_map/ppermute | solution.py:301
  69.3 19.3 %copy-start = (f32[2,4,1,2,128,128]{5,4,3,2,1,0:T(8,128)S(1)}, f32[2,4,1,2,128,128]{5,4,3,2,1,0:T(8,128)}, u32[]{:S(2)}) copy-start(f32[2,4,1,2,128,128]{5,4,3,2,1,0:T(8,128)} %green_ref.1) | copy-start | bytes 3145732
  70.6 2.0 %collective-permute-start.15 = (f32[2,4,128,128]{3,2,1,0:T(8,128)S(1)}, f32[2,4,128,128]{3,2,1,0:T(8,128)S(1)}, u32[]{:S(2)}, u32[]{:S(2)}) collective-permute-start(f32[2,4,128,128]{3,2,1,0:T(8,128)S(1)} %get-tuple-element.56), channel_id=1, source_target_pairs={{0,4},{4,0},{8,12},{12,8},{16,20},{20,16},{24,28},{28,24},{1,5},{5... | collective-permute-start | bytes 1572872 | tf_op jit(solution)/shard_map/ppermute | solution.py:291
  72.8 9.2 %collective-permute-start.16 = (f32[2,4,64,128]{3,2,1,0:T(8,128)S(1)}, f32[2,4,64,128]{3,2,1,0:T(8,128)S(1)}, u32[]{:S(2)}, u32[]{:S(2)}) collective-permute-start(f32[2,4,64,128]{3,2,1,0:T(8,128)S(1)} %get-tuple-element.58), channel_id=1, source_target_pairs={{0,8},{4,12},{8,0},{12,4},{16,24},{20,28},{24,16},{28,20},{1,9},{5... | collective-permute-start | bytes 786440 | tf_op jit(solution)/shard_map/ppermute | solution.py:291
  74.4 12.5 %collective-permute-start.18 = (f32[2,4,64,128]{3,2,1,0:T(8,128)S(1)}, f32[2,4,64,128]{3,2,1,0:T(8,128)S(1)}, u32[]{:S(2)}, u32[]{:S(2)}) collective-permute-start(f32[2,4,64,128]{3,2,1,0:T(8,128)S(1)} %get-tuple-element.62), channel_id=1, source_target_pairs={{0,8},{4,12},{8,0},{12,4},{16,24},{20,28},{24,16},{28,20},{1,9},{5... | collective-permute-start | bytes 786440 | tf_op jit(solution)/shard_map/ppermute | solution.py:291
  82.2 7.3 %collective-permute-start.17 = (f32[2,4,64,128]{3,2,1,0:T(8,128)S(1)}, f32[2,4,64,128]{3,2,1,0:T(8,128)S(1)}, u32[]{:S(2)}, u32[]{:S(2)}) collective-permute-start(f32[2,4,64,128]{3,2,1,0:T(8,128)S(1)} %get-tuple-element.60), channel_id=1, source_target_pairs={{0,16},{4,20},{8,24},{12,28},{16,0},{20,4},{24,8},{28,12},{1,17},{... | collective-permute-start | bytes 786440 | tf_op jit(solution)/shard_map/ppermute | solution.py:291
  87.0 7.6 %collective-permute-start.19 = (f32[2,4,64,128]{3,2,1,0:T(8,128)S(1)}, f32[2,4,64,128]{3,2,1,0:T(8,128)S(1)}, u32[]{:S(2)}, u32[]{:S(2)}) collective-permute-start(f32[2,4,64,128]{3,2,1,0:T(8,128)S(1)} %get-tuple-element.64), channel_id=1, source_target_pairs={{0,16},{4,20},{8,24},{12,28},{16,0},{20,4},{24,8},{28,12},{1,17},{... | collective-permute-start | bytes 786440 | tf_op jit(solution)/shard_map/ppermute | solution.py:291
  89.5 10.8 %collective-permute-start.22 = (f32[2,4,64,128]{3,2,1,0:T(8,128)S(1)}, f32[2,4,64,128]{3,2,1,0:T(8,128)S(1)}, u32[]{:S(2)}, u32[]{:S(2)}) collective-permute-start(f32[2,4,64,128]{3,2,1,0:T(8,128)S(1)} %shard_map.60), channel_id=1, source_target_pairs={{1,2},{2,1},{5,6},{6,5},{9,10},{10,9},{13,14},{14,13},{17,18},{18,... | collective-permute-start | bytes 786440 | tf_op jit(solution)/shard_map/ppermute | solution.py:301
  90.2 10.1 %collective-permute-start.20 = (f32[2,4,64,128]{3,2,1,0:T(8,128)S(1)}, f32[2,4,64,128]{3,2,1,0:T(8,128)S(1)}, u32[]{:S(2)}, u32[]{:S(2)}) collective-permute-start(f32[2,4,64,128]{3,2,1,0:T(8,128)S(1)} %shard_map.60), channel_id=1, source_target_pairs={{0,1},{2,3},{1,0},{3,2},{4,5},{6,7},{5,4},{7,6},{8,9},{10,11},{9,8... | collective-permute-start | bytes 786440 | tf_op jit(solution)/shard_map/ppermute | solution.py:301
  94.6 5.7 %collective-permute-start.23 = (f32[2,4,64,128]{3,2,1,0:T(8,128)S(1)}, f32[2,4,64,128]{3,2,1,0:T(8,128)S(1)}, u32[]{:S(2)}, u32[]{:S(2)}) collective-permute-start(f32[2,4,64,128]{3,2,1,0:T(8,128)S(1)} %shard_map.62), channel_id=1, source_target_pairs={{1,2},{2,1},{5,6},{6,5},{9,10},{10,9},{13,14},{14,13},{17,18},{18,... | collective-permute-start | bytes 786440 | tf_op jit(solution)/shard_map/ppermute | solution.py:301
  95.3 9.2 %collective-permute-start.21 = (f32[2,4,64,128]{3,2,1,0:T(8,128)S(1)}, f32[2,4,64,128]{3,2,1,0:T(8,128)S(1)}, u32[]{:S(2)}, u32[]{:S(2)}) collective-permute-start(f32[2,4,64,128]{3,2,1,0:T(8,128)S(1)} %shard_map.62), channel_id=1, source_target_pairs={{0,1},{2,3},{1,0},{3,2},{4,5},{6,7},{5,4},{7,6},{8,9},{10,11},{9,8... | collective-permute-start | bytes 786440 | tf_op jit(solution)/shard_map/ppermute | solution.py:301

commit v3 on v2

--- a/solution.py
+++ b/solution.py
@@ -9,16 +9,16 @@
 from jax.sharding import PartitionSpec as P
 
 
-FORWARD = 3
-BACKWARD = 2
-HIGH = lax.Precision.HIGH
+FORWARD = 4
+BACKWARD = 3
 TILE = 8
+GRAIN = 16
 
 
 def heights(order, parts):
-    tiles = order // TILE
-    sizes = [tiles // parts + (1 if k < tiles % parts else 0) for k in range(parts)]
-    return [s * TILE for s in sizes]
+    grains = order // GRAIN
+    sizes = [grains // parts + (1 if k < grains % parts else 0) for k in range(parts)]
+    return [s * GRAIN for s in sizes]
 
 
 def starts_of(sizes):
@@ -88,20 +88,41 @@
     lax.fori_loop(0, rows // TILE, run, 0)
 
 
-def call(kernel, out_shapes, *args, smem=()):
+def call(kernel, outs, *args, smem=(), scratch=(), alias=None):
     specs = [
         pl.BlockSpec(memory_space=pltpu.SMEM if i in smem else pltpu.VMEM)
         for i in range(len(args))
     ]
-    nbytes = sum(a.size * 4 for a in args) + sum(4 * math.prod(s) for s in out_shapes)
+    outs = [o if isinstance(o, jax.ShapeDtypeStruct) else full(o) for o in outs]
+    nbytes = sum(a.size * a.dtype.itemsize for a in [*args, *outs, *map(full, scratch)])
     return pl.pallas_call(
         kernel,
-        out_shape=[jax.ShapeDtypeStruct(s, jnp.float32) for s in out_shapes],
+        out_shape=outs,
         in_specs=specs,
-        out_specs=[pl.BlockSpec(memory_space=pltpu.VMEM) for _ in out_shapes],
+        out_specs=[pl.BlockSpec(memory_space=pltpu.VMEM) for _ in outs],
+        scratch_shapes=[pltpu.VMEM(shape, jnp.float32) for shape in scratch],
+        input_output_aliases=alias or {},
         cost_estimate=pl.CostEstimate(flops=nbytes, bytes_accessed=nbytes, transcendentals=0),
-        compiler_params=pltpu.CompilerParams(vmem_limit_bytes=nbytes + (1 << 20)),
+        compiler_params=pltpu.CompilerParams(vmem_limit_bytes=nbytes + (4 << 20)),
     )(*args)
+
+
+def full(shape):
+    return jax.ShapeDtypeStruct(shape, jnp.float32)
+
+
+def half(shape):
+    return jax.ShapeDtypeStruct(shape, jnp.bfloat16)
+
+
+def halves(value):
+    high = value.astype(jnp.bfloat16)
+    return high, (value - high.astype(jnp.float32)).astype(jnp.bfloat16)
+
+
+def product_of(left, right):
+    dot = partial(jnp.dot, preferred_element_type=jnp.float32)
+    return dot(left[0], right[0]) + (dot(left[0], right[1]) + dot(left[1], right[0]))
 
 
 def split_first(own, got, had):
@@ -172,44 +193,6 @@
     tiles_loop(rows, step)
 
 
-def inverse_kernel(bits, sizes, *refs):
-    me = lax.axis_index("wide")
-    lesser_refs, (screened_ref, keep_ref, send_ref) = refs[:-3], refs[-3:]
-    local = keep_ref.shape[1]
-    peers = 1 << bits
-    period = 2 * peers * local
-    mine = own_bit(me, 0)
-    c, s = phase(me, bits, bits, 1.0 / (2 * peers))
-    twist = [
-        [phase(me, bits, bits, j / period, top) for j in range(local)] for top in range(2)
-    ]
-    for lesser_ref, start, size in zip(lesser_refs, starts_of(sizes), sizes):
-
-        def run(k, carry, lesser_ref=lesser_ref, start=start):
-            at = pl.ds(pl.multiple_of(k * TILE, TILE), TILE)
-            to = pl.ds(pl.multiple_of(start + k * TILE, TILE), TILE)
-            tops = []
-            for top in range(2):
-                values = []
-                for t in range(local):
-                    f = top * local + t
-                    a = (lesser_ref[0, f, at], lesser_ref[1, f, at])
-                    values.append(times(a, screened_ref[0, f, to], screened_ref[1, f, to]))
-                values = dft(values, 1)
-                tops.append(
-                    [v if j == 0 else times(v, *twist[top][j]) for j, v in enumerate(values)]
-                )
-            for j in range(local):
-                total = [tops[0][j][i] + tops[1][j][i] for i in range(2)]
-                gap = times([tops[0][j][i] - tops[1][j][i] for i in range(2)], c, s)
-                for i in range(2):
-                    keep_ref[i, j, to] = jnp.where(mine == 1, gap[i], total[i])
-                    send_ref[i, j, to] = jnp.where(mine == 1, total[i], gap[i])
-            return carry
-
-        lax.fori_loop(0, size // TILE, run, 0)
-
-
 def backward_kernel(bit, bits, sizes, own_ref, got_ref, *outs):
     me = lax.axis_index("wide")
     local = own_ref.shape[1]
@@ -249,35 +232,129 @@
     return [0, side, -side]
 
 
-def prepare_coulomb(scale, offsets_ref, coulomb_ref, plain_ref, scaled_ref):
+def prepare_coulomb(scale, offsets_ref, coulomb_ref, left_high, left_low, right_high, right_low):
     row = lax.axis_index("cell")
+    order = coulomb_ref.shape[-1]
     for slot, place in enumerate(places_of(row)):
         hit = [offsets_ref[0, j] == place for j in range(2)]
         value = chosen(hit, coulomb_ref[0, 0], coulomb_ref[0, 1])
-        plain_ref[slot] = value
-        scaled_ref[slot] = value * scale
-
-
-def prepare_green(offsets_ref, green_ref, out_ref):
+        at = slice(slot * order, (slot + 1) * order)
+        left_high[:, at], left_low[:, at] = halves(value)
+        right_high[slot], right_low[slot] = halves(value.T * scale)
+
+
+def prepare_green(offsets_ref, green_ref, left_high, left_low, right_high, right_low):
     row = lax.axis_index("cell")
     local, order = green_ref.shape[1], green_ref.shape[-1]
+    low, top = slice(0, order), slice(order, 2 * order)
     for slot, place in enumerate(places_of(row)):
         hit = [offsets_ref[0, j] == place for j in range(2)]
         for e in range(local):
-            re, im = (chosen(hit, green_ref[i, e, 0, 0], green_ref[i, e, 0, 1]) for i in range(2))
-            out_ref[slot, e, :order, :order] = re
-            out_ref[slot, e, :order, order:] = -im
-            out_ref[slot, e, order:, :order] = im
-            out_ref[slot, e, order:, order:] = re
-
-
-def congruence(left, middle):
-    order = middle.shape[-1]
-    stacked = jnp.concatenate([middle[0], middle[1]], axis=-2)
-    half = jnp.einsum("eab,ebc->eac", left, stacked, precision=HIGH)
-    flat = jnp.concatenate([half[:, :order], half[:, order:]], axis=-1)
-    out = jnp.einsum("eab,ecb->eac", flat, left, precision=HIGH)
-    return jnp.stack([out[..., :order], out[..., order:]])
+            parts = [chosen(hit, green_ref[i, e, 0, 0], green_ref[i, e, 0, 1]) for i in range(2)]
+            re, im = (halves(p) for p in parts)
+            re_t, im_t = (halves(p.T) for p in parts)
+            for i, (left, right) in enumerate(((left_high, right_high), (left_low, right_low))):
+                left[slot, e, low, low], left[slot, e, top, top] = re[i], re[i]
+                left[slot, e, low, top], left[slot, e, top, low] = -im[i], im[i]
+                right[slot, e, low, low], right[slot, e, top, top] = re_t[i], re_t[i]
+                right[slot, e, top, low], right[slot, e, low, top] = -im_t[i], im_t[i]
+
+
+def screen_kernel(start, *refs):
+    blocks, (right_high, right_low), (out_high, out_low) = refs[:3], refs[3:5], refs[-2:]
+    count, rows, order = blocks[0].shape[1], blocks[0].shape[2], blocks[0].shape[3]
+    for slot, ref in enumerate(blocks):
+        value = halves(ref[...].reshape(2 * count * rows, order))
+        result = halves(product_of(value, (right_high[slot], right_low[slot])))
+        at = slice(slot * order + start, slot * order + start + rows)
+        for i, out in enumerate((out_high, out_low)):
+            out[:, :, at] = result[i].reshape(2, count, rows, order)
+
+
+def inverse_kernel(bits, sizes, *refs):
+    me = lax.axis_index("wide")
+    lesser_refs, refs = refs[: len(sizes)], refs[len(sizes) :]
+    left_high, left_low, mid_high, mid_low, keep_ref, send_ref, screened = refs
+    for i in range(2):
+        for f in range(mid_high.shape[1]):
+            screened[i, f] = product_of(
+                (left_high[...], left_low[...]), (mid_high[i, f], mid_low[i, f])
+            )
+    local = keep_ref.shape[1]
+    peers = 1 << bits
+    period = 2 * peers * local
+    mine = own_bit(me, 0)
+    c, s = phase(me, bits, bits, 1.0 / (2 * peers))
+    twist = [
+        [phase(me, bits, bits, j / period, top) for j in range(local)] for top in range(2)
+    ]
+    for lesser_ref, start, size in zip(lesser_refs, starts_of(sizes), sizes):
+
+        def run(k, carry, lesser_ref=lesser_ref, start=start):
+            at = pl.ds(pl.multiple_of(k * TILE, TILE), TILE)
+            to = pl.ds(pl.multiple_of(start + k * TILE, TILE), TILE)
+            tops = []
+            for top in range(2):
+                values = []
+                for t in range(local):
+                    f = top * local + t
+                    a = (lesser_ref[0, f, at], lesser_ref[1, f, at])
+                    values.append(times(a, screened[0, f, to], screened[1, f, to]))
+                values = dft(values, 1)
+                tops.append(
+                    [v if j == 0 else times(v, *twist[top][j]) for j, v in enumerate(values)]
+                )
+            for j in range(local):
+                total = [tops[0][j][i] + tops[1][j][i] for i in range(2)]
+                gap = times([tops[0][j][i] - tops[1][j][i] for i in range(2)], c, s)
+                for i in range(2):
+                    keep_ref[i, j, to] = jnp.where(mine == 1, gap[i], total[i])
+                    send_ref[i, j, to] = jnp.where(mine == 1, total[i], gap[i])
+            return carry
+
+        lax.fori_loop(0, size // TILE, run, 0)
+
+
+def times_right(block_ref, e, right_high, right_low, slot):
+    value = halves(jnp.concatenate([block_ref[0, e], block_ref[1, e]], axis=-1))
+    return product_of(value, (right_high[slot, e], right_low[slot, e]))
+
+
+def own_dressing_kernel(count, *refs):
+    blocks, (left_high, left_low, right_high, right_low, out_ref) = refs[:count], refs[count:]
+    local, order = out_ref.shape[1], out_ref.shape[-1]
+    for e in range(local):
+        parts = [times_right(b, e, right_high, right_low, 0) for b in blocks]
+        middle = jnp.concatenate(
+            [p[:, :order] for p in parts] + [p[:, order:] for p in parts], axis=0
+        )
+        out = product_of((left_high[0, e], left_low[0, e]), halves(middle))
+        out_ref[0, e], out_ref[1, e] = out[:order], out[order:]
+
+
+def dress_kernel(start, *refs):
+    blocks, (right_high, right_low), (out_high, out_low) = refs[:2], refs[2:4], refs[-2:]
+    local, rows, order = blocks[0].shape[1], blocks[0].shape[2], blocks[0].shape[3]
+    for slot, ref in enumerate(blocks):
+        for e in range(local):
+            result = halves(times_right(ref, e, right_high, right_low, slot + 1))
+            for p in range(2):
+                to = slice((2 * slot + p) * order + start, (2 * slot + p) * order + start + rows)
+                at = slice(p * order, (p + 1) * order)
+                out_high[e, to], out_low[e, to] = result[0][:, at], result[1][:, at]
+
+
+def finish_kernel(own_ref, left_high, left_low, mid_high, mid_low, out_ref):
+    local, order = out_ref.shape[1], out_ref.shape[-1]
+    for e in range(local):
+        total = 0.0
+        for slot in range(2):
+            at = slice(2 * slot * order, 2 * (slot + 1) * order)
+            total = total + product_of(
+                (left_high[slot + 1, e], left_low[slot + 1, e]), (mid_high[e, at], mid_low[e, at])
+            )
+        out_ref[0, e, 0] = own_ref[0, e] + total[:order]
+        out_ref[1, e, 0] = own_ref[1, e] + total[order:]
 
 
 def body(green_pair, coulomb, green_retarded, offsets):
@@ -307,12 +384,13 @@
         lax.slice_in_dim(pair, at, at + size, axis=3) for at, size in zip(starts_of(sizes), sizes)
     ]
     got = [swap(own, bits - 1) for own in keep]
-    plain, scaled = call(
-        partial(prepare_coulomb, scale),
-        [(3, order, order)] * 2, offsets, coulomb, smem=(0,),
-    )
-    left, = call(
-        prepare_green, [(3, local, 2 * order, 2 * order)],
+    coulomb_shapes = [(order, 3 * order)] * 2 + [(3, order, order)] * 2
+    coulombs = call(
+        partial(prepare_coulomb, scale), [half(c) for c in coulomb_shapes],
+        offsets, coulomb, smem=(0,),
+    )
+    greens = call(
+        prepare_green, [half((3, local, 2 * order, 2 * order))] * 4,
         offsets, green_retarded, smem=(0,),
     )
     lesser, near = [None] * FORWARD, [None] * FORWARD
@@ -329,15 +407,17 @@
             )
             near[k] = [polar] + beside(polar)
 
-    screened = 0.0
-    for slot in range(3):
-        whole = jnp.concatenate([n[slot] for n in near], axis=2)
-        half = jnp.einsum("pfbc,dc->pfbd", whole, scaled[slot], precision=HIGH)
-        screened = screened + jnp.einsum("ab,pfbd->pfad", plain[slot], half, precision=HIGH)
-
+    middle = []
+    for k, start in enumerate(starts_of(sizes)):
+        middle = call(
+            partial(screen_kernel, start),
+            [half((2, 2 * local, 3 * order, order))] * 2, *near[k], *coulombs[2:], *middle,
+            alias={5: 0, 6: 1} if k else None,
+        )
     keep, send = call(
         partial(inverse_kernel, bits, sizes),
-        [(2, local, order, order)] * 2, *lesser, screened,
+        [(2, local, order, order)] * 2, *lesser, *coulombs[:2], *middle,
+        scratch=[(2, 2 * local, order, order)],
     )
     got = swap(send, 0)
     sizes = heights(order, BACKWARD)
@@ -358,11 +438,18 @@
         else:
             sigma, = call(add_kernel, [keep[k].shape], keep[k], got[k])
             near[k] = [sigma] + beside(sigma)
-    result = 0.0
-    for slot in range(3):
-        middle = jnp.concatenate([n[slot] for n in near], axis=2)
-        result = result + congruence(left[slot], middle)
-    return result[:, :, None]
+    own, = call(
+        partial(own_dressing_kernel, BACKWARD), [(2, local, order, order)],
+        *[n[0] for n in near], *greens,
+    )
+    middle = []
+    for k, start in enumerate(starts_of(sizes)):
+        middle = call(
+            partial(dress_kernel, start), [half((local, 4 * order, order))] * 2,
+            *near[k][1:], *greens[2:], *middle, alias={4: 0, 5: 1} if k else None,
+        )
+    result, = call(finish_kernel, [(2, local, 1, order, order)], own, *greens[:2], *middle)
+    return result
 
 
 def solution(mesh):

time: 109 us -> 104 us (0.954)
  waiting for transfers between devices: 59 us -> 36.4 us
  starting transfers between devices: 33.5 us -> 50.9 us
  Pallas kernels: 4.27 us -> 14.1 us
  matrix products: 7.64 us -> 0 us
  local copies, waits for them, and re-layouts: 2.59 us -> 1.29 us
    ppermute x10 -> x14, waiting for transfers between devices: 22.3 us -> 7.95 us  [beside(): blocks.append(lax.ppermute(value, 'cell', pairs))]
    ppermute x10 -> x14, starting transfers between devices: 16.9 us -> 28.6 us  [beside(): blocks.append(lax.ppermute(value, 'cell', pairs))]
    pallas_call x17 -> x31, Pallas kernels: 4.27 us -> 14.1 us  [call(): pl.pallas_call(kernel, out_shape=outs, in_specs=specs, out_specs=[pl.Bloc...]
    ppermute x14 -> x19, waiting for transfers between devices: 36.8 us -> 28.4 us  [swap(): lax.ppermute(value, 'wide', [(i, i ^ 1 << bit) for i in range(peers)])]
    dot_general x12 -> x0, matrix products: 7.64 us -> none  [the longest x3 2.08 us: congruence(): out = jnp.einsum('eab,ecb->eac', flat, left, precision=HIGH)]
    ppermute x14 -> x19, starting transfers between devices: 16.6 us -> 22.3 us  [swap(): lax.ppermute(value, 'wide', [(i, i ^ 1 << bit) for i in range(peers)])]
  transfers between devices with their start and end apart: 24 -> 33, of which waited for: 13 -> 10; matrix products, arithmetic and copies ran while one was open for 5% -> 0% of each run, Pallas kernels for 3% -> 9%
where the time goes in v3:
time: 104 us; the launch traced here: 103 us
  starting transfers between devices  50.9 us (49%)
  waiting for transfers between devices  36.4 us (35%)
  Pallas kernels  14.1 us (14%)
  local copies, waits for them, and re-layouts  1.29 us (1%)
    ppermute x14, starting transfers between devices, beside(): blocks.append(lax.ppermute(value, 'cell', pairs))  28.6 us
    ppermute x19, waiting for transfers between devices, swap(): lax.ppermute(value, 'wide', [(i, i ^ 1 << bit) for i in range(peers)])  28.4 us
    ppermute x19, starting transfers between devices, swap(): lax.ppermute(value, 'wide', [(i, i ^ 1 << bit) for i in range(peers)])  22.3 us
    pallas_call x31, Pallas kernels, call(): pl.pallas_call(kernel, out_shape=outs, in_specs=specs, out_specs=[pl.Bloc...  14.1 us
    ppermute x14, waiting for transfers between devices, beside(): blocks.append(lax.ppermute(value, 'cell', pairs))  7.95 us
  transfers between devices with their start and end apart: 33, of which 10 were waited for; matrix products, arithmetic and copies ran while one was open for 0% of the time, Pallas kernels for 9%

profile of v3, /device:TPU:0, one launch (start us, length us, event | category | flops | bytes accessed | tf_op | source)
XLA Modules:
  0.0 103.2 jit_solution(2363047534814249877)
XLA Ops:
  0.0 1.3 %fusion = (f32[2,2,4,32,128]{4,3,2,1,0:T(8,128)S(1)}, f32[2,2,4,32,128]{4,3,2,1,0:T(8,128)S(1)}, f32[2,2,4,32,128]{4,3,2,1,0:T(8,128)S(1)}, f32[2,2,4,32,128]{4,3,2,1,0:T(8,128)S(1)}) fusion(f32[2,2,4,128,128]{4,3,2,1,0:T(8,128)} %bitcast.1), kind=kLoop, calls=%fused_computation | loop fusion | bytes 2097152 | tf_op jit(solution)/shard_map/slice | solution.py:384
  1.3 3.1 %collective-permute-start = (f32[2,2,4,32,128]{4,3,2,1,0:T(8,128)S(1)}, f32[2,2,4,32,128]{4,3,2,1,0:T(8,128)S(1)}, u32[]{:S(2)}, u32[]{:S(2)}) collective-permute-start(f32[2,2,4,32,128]{4,3,2,1,0:T(8,128)S(1)} %get-tuple-element.128.own_ref), channel_id=1, source_target_pairs={{0,16},{4,20},{8,24},{12,28},{16,0},{20,4},{24,8},{28,12},{1,17},{... | collective-permute-start | bytes 786440 | tf_op jit(solution)/shard_map/ppermute | solution.py:368
  4.4 1.9 %collective-permute-start.6 = (f32[2,2,4,32,128]{4,3,2,1,0:T(8,128)S(1)}, f32[2,2,4,32,128]{4,3,2,1,0:T(8,128)S(1)}, u32[]{:S(2)}, u32[]{:S(2)}) collective-permute-start(f32[2,2,4,32,128]{4,3,2,1,0:T(8,128)S(1)} %get-tuple-element.126.own_ref), channel_id=1, source_target_pairs={{0,16},{4,20},{8,24},{12,28},{16,0},{20,4},{24,8},{28,12},{1,17},{... | collective-permute-start | bytes 786440 | tf_op jit(solution)/shard_map/ppermute | solution.py:368
  6.5 5.0 %collective-permute-done.got_ref = f32[2,2,4,32,128]{4,3,2,1,0:T(8,128)S(1)} collective-permute-done((f32[2,2,4,32,128]{4,3,2,1,0:T(8,128)S(1)}, f32[2,2,4,32,128]{4,3,2,1,0:T(8,128)S(1)}, u32[]{:S(2)}, u32[]{:S(2)}) %collective-permute-start) | collective-permute-done | bytes 262176 | tf_op jit(solution)/shard_map/ppermute | solution.py:368
  11.6 2.1 %collective-permute-start.1 = (f32[2,2,4,32,128]{4,3,2,1,0:T(8,128)S(1)}, f32[2,2,4,32,128]{4,3,2,1,0:T(8,128)S(1)}, u32[]{:S(2)}, u32[]{:S(2)}) collective-permute-start(f32[2,2,4,32,128]{4,3,2,1,0:T(8,128)S(1)} %get-tuple-element.66), channel_id=1, source_target_pairs={{0,8},{4,12},{8,0},{12,4},{16,24},{20,28},{24,16},{28,20},{1,9},{5... | collective-permute-start | bytes 786440 | tf_op jit(solution)/shard_map/ppermute | solution.py:368
  13.7 3.5 %collective-permute-done.3.got_ref = f32[2,2,4,32,128]{4,3,2,1,0:T(8,128)S(1)} collective-permute-done((f32[2,2,4,32,128]{4,3,2,1,0:T(8,128)S(1)}, f32[2,2,4,32,128]{4,3,2,1,0:T(8,128)S(1)}, u32[]{:S(2)}, u32[]{:S(2)}) %collective-permute-start.3) | collective-permute-done | bytes 262176 | tf_op jit(solution)/shard_map/ppermute | solution.py:368
  17.2 2.1 %collective-permute-start.4 = (f32[2,2,4,32,128]{4,3,2,1,0:T(8,128)S(1)}, f32[2,2,4,32,128]{4,3,2,1,0:T(8,128)S(1)}, u32[]{:S(2)}, u32[]{:S(2)}) collective-permute-start(f32[2,2,4,32,128]{4,3,2,1,0:T(8,128)S(1)} %get-tuple-element.71), channel_id=1, source_target_pairs={{0,8},{4,12},{8,0},{12,4},{16,24},{20,28},{24,16},{28,20},{1,9},{5... | collective-permute-start | bytes 786440 | tf_op jit(solution)/shard_map/ppermute | solution.py:368
  19.3 3.5 %collective-permute-done.6.got_ref = f32[2,2,4,32,128]{4,3,2,1,0:T(8,128)S(1)} collective-permute-done((f32[2,2,4,32,128]{4,3,2,1,0:T(8,128)S(1)}, f32[2,2,4,32,128]{4,3,2,1,0:T(8,128)S(1)}, u32[]{:S(2)}, u32[]{:S(2)}) %collective-permute-start.6) | collective-permute-done | bytes 262176 | tf_op jit(solution)/shard_map/ppermute | solution.py:368
  22.8 2.1 %collective-permute-start.7 = (f32[2,2,4,32,128]{4,3,2,1,0:T(8,128)S(1)}, f32[2,2,4,32,128]{4,3,2,1,0:T(8,128)S(1)}, u32[]{:S(2)}, u32[]{:S(2)}) collective-permute-start(f32[2,2,4,32,128]{4,3,2,1,0:T(8,128)S(1)} %get-tuple-element.76), channel_id=1, source_target_pairs={{0,8},{4,12},{8,0},{12,4},{16,24},{20,28},{24,16},{28,20},{1,9},{5... | collective-permute-start | bytes 786440 | tf_op jit(solution)/shard_map/ppermute | solution.py:368
  24.9 2.6 %collective-permute-done.9.got_ref = f32[2,2,4,32,128]{4,3,2,1,0:T(8,128)S(1)} collective-permute-done((f32[2,2,4,32,128]{4,3,2,1,0:T(8,128)S(1)}, f32[2,2,4,32,128]{4,3,2,1,0:T(8,128)S(1)}, u32[]{:S(2)}, u32[]{:S(2)}) %collective-permute-start.9) | collective-permute-done | bytes 262176 | tf_op jit(solution)/shard_map/ppermute | solution.py:368
  27.6 1.8 %collective-permute-start.10 = (f32[2,2,4,32,128]{4,3,2,1,0:T(8,128)S(1)}, f32[2,2,4,32,128]{4,3,2,1,0:T(8,128)S(1)}, u32[]{:S(2)}, u32[]{:S(2)}) collective-permute-start(f32[2,2,4,32,128]{4,3,2,1,0:T(8,128)S(1)} %get-tuple-element.81), channel_id=1, source_target_pairs={{0,8},{4,12},{8,0},{12,4},{16,24},{20,28},{24,16},{28,20},{1,9},{5... | collective-permute-start | bytes 786440 | tf_op jit(solution)/shard_map/ppermute | solution.py:368
  30.5 4.7 %collective-permute-done.10.got_ref = f32[2,2,4,32,128]{4,3,2,1,0:T(8,128)S(1)} collective-permute-done((f32[2,2,4,32,128]{4,3,2,1,0:T(8,128)S(1)}, f32[2,2,4,32,128]{4,3,2,1,0:T(8,128)S(1)}, u32[]{:S(2)}, u32[]{:S(2)}) %collective-permute-start.10) | collective-permute-done | bytes 262176 | tf_op jit(solution)/shard_map/ppermute | solution.py:368
  35.6 1.9 %collective-permute-start.18 = (f32[2,8,32,128]{3,2,1,0:T(8,128)S(1)}, f32[2,8,32,128]{3,2,1,0:T(8,128)S(1)}, u32[]{:S(2)}, u32[]{:S(2)}) collective-permute-start(f32[2,8,32,128]{3,2,1,0:T(8,128)S(1)} %get-tuple-element.92.refs_0_), channel_id=1, source_target_pairs={{0,1},{2,3},{1,0},{3,2},{4,5},{6,7},{5,4},{7,6},{8,9},{10,11},{9,8... | collective-permute-start | bytes 786440 | tf_op jit(solution)/shard_map/ppermute | solution.py:378
  38.5 4.4 %collective-permute-start.16 = (f32[2,8,32,128]{3,2,1,0:T(8,128)S(1)}, f32[2,8,32,128]{3,2,1,0:T(8,128)S(1)}, u32[]{:S(2)}, u32[]{:S(2)}) collective-permute-start(f32[2,8,32,128]{3,2,1,0:T(8,128)S(1)} %get-tuple-element.91.refs_0_), channel_id=1, source_target_pairs={{0,1},{2,3},{1,0},{3,2},{4,5},{6,7},{5,4},{7,6},{8,9},{10,11},{9,8... | collective-permute-start | bytes 786440 | tf_op jit(solution)/shard_map/ppermute | solution.py:378
  43.9 1.3 %collective-permute-start.14 = (f32[2,8,32,128]{3,2,1,0:T(8,128)S(1)}, f32[2,8,32,128]{3,2,1,0:T(8,128)S(1)}, u32[]{:S(2)}, u32[]{:S(2)}) collective-permute-start(f32[2,8,32,128]{3,2,1,0:T(8,128)S(1)} %get-tuple-element.90.refs_0_), channel_id=1, source_target_pairs={{0,1},{2,3},{1,0},{3,2},{4,5},{6,7},{5,4},{7,6},{8,9},{10,11},{9,8... | collective-permute-start | bytes 786440 | tf_op jit(solution)/shard_map/ppermute | solution.py:378
  46.3 4.3 %collective-permute-start.12 = (f32[2,8,32,128]{3,2,1,0:T(8,128)S(1)}, f32[2,8,32,128]{3,2,1,0:T(8,128)S(1)}, u32[]{:S(2)}, u32[]{:S(2)}) collective-permute-start(f32[2,8,32,128]{3,2,1,0:T(8,128)S(1)} %get-tuple-element.87.refs_0_), channel_id=1, source_target_pairs={{0,1},{2,3},{1,0},{3,2},{4,5},{6,7},{5,4},{7,6},{8,9},{10,11},{9,8... | collective-permute-start | bytes 786440 | tf_op jit(solution)/shard_map/ppermute | solution.py:378
  52.9 3.2 %collective-permute-done.14.refs_1_ = f32[2,8,32,128]{3,2,1,0:T(8,128)S(1)} collective-permute-done((f32[2,8,32,128]{3,2,1,0:T(8,128)S(1)}, f32[2,8,32,128]{3,2,1,0:T(8,128)S(1)}, u32[]{:S(2)}, u32[]{:S(2)}) %collective-permute-start.14) | collective-permute-done | bytes 262176 | tf_op jit(solution)/shard_map/ppermute | solution.py:378
  56.6 4.7 %collective-permute-done.12.refs_1_ = f32[2,8,32,128]{3,2,1,0:T(8,128)S(1)} collective-permute-done((f32[2,8,32,128]{3,2,1,0:T(8,128)S(1)}, f32[2,8,32,128]{3,2,1,0:T(8,128)S(1)}, u32[]{:S(2)}, u32[]{:S(2)}) %collective-permute-start.12) | collective-permute-done | bytes 262176 | tf_op jit(solution)/shard_map/ppermute | solution.py:378
  61.8 2.0 %shard_map.63 = (f32[2,4,128,128]{3,2,1,0:T(8,128)S(1)}, f32[2,4,128,128]{3,2,1,0:T(8,128)S(1)}) custom-call(f32[2,8,32,128]{3,2,1,0:T(8,128)S(1)} %get-tuple-element.69.refs_0_, f32[2,8,32,128]{3,2,1,0:T(8,128)S(1)} %get-tuple-element.74.refs_1_, f32[2,8,32,128]{3,2,1,0:T(8,128)S(1)} %get-tuple-element.79.refs_2_, ...), custom_call_target="tpu_custom_call" | custom-call | flops 6488064 | bytes 6488064 | tf_op jit(solution)/shard_map/pallas_call | solution.py:98
  63.9 1.9 %collective-permute-done.20.got_ref = f32[2,4,128,128]{3,2,1,0:T(8,128)S(1)} collective-permute-done((f32[2,4,128,128]{3,2,1,0:T(8,128)S(1)}, f32[2,4,128,128]{3,2,1,0:T(8,128)S(1)}, u32[]{:S(2)}, u32[]{:S(2)}) %collective-permute-start.20) | collective-permute-done | bytes 524320 | tf_op jit(solution)/shard_map/ppermute | solution.py:368
  66.0 1.7 %collective-permute-start.21 = (f32[2,4,48,128]{3,2,1,0:T(8,128)S(1)}, f32[2,4,48,128]{3,2,1,0:T(8,128)S(1)}, u32[]{:S(2)}, u32[]{:S(2)}) collective-permute-start(f32[2,4,48,128]{3,2,1,0:T(8,128)S(1)} %get-tuple-element.104), channel_id=1, source_target_pairs={{0,8},{4,12},{8,0},{12,4},{16,24},{20,28},{24,16},{28,20},{1,9},{5... | collective-permute-start | bytes 589832 | tf_op jit(solution)/shard_map/ppermute | solution.py:368
  68.1 5.7 %collective-permute-done.21.got_ref = f32[2,4,48,128]{3,2,1,0:T(8,128)S(1)} collective-permute-done((f32[2,4,48,128]{3,2,1,0:T(8,128)S(1)}, f32[2,4,48,128]{3,2,1,0:T(8,128)S(1)}, u32[]{:S(2)}, u32[]{:S(2)}) %collective-permute-start.21) | collective-permute-done | bytes 196640 | tf_op jit(solution)/shard_map/ppermute | solution.py:368
  74.0 1.7 %collective-permute-start.22 = (f32[2,4,48,128]{3,2,1,0:T(8,128)S(1)}, f32[2,4,48,128]{3,2,1,0:T(8,128)S(1)}, u32[]{:S(2)}, u32[]{:S(2)}) collective-permute-start(f32[2,4,48,128]{3,2,1,0:T(8,128)S(1)} %get-tuple-element.106), channel_id=1, source_target_pairs={{0,16},{4,20},{8,24},{12,28},{16,0},{20,4},{24,8},{28,12},{1,17},{... | collective-permute-start | bytes 589832 | tf_op jit(solution)/shard_map/ppermute | solution.py:368
  75.7 1.5 %collective-permute-done.23.got_ref = f32[2,4,48,128]{3,2,1,0:T(8,128)S(1)} collective-permute-done((f32[2,4,48,128]{3,2,1,0:T(8,128)S(1)}, f32[2,4,48,128]{3,2,1,0:T(8,128)S(1)}, u32[]{:S(2)}, u32[]{:S(2)}) %collective-permute-start.23) | collective-permute-done | bytes 196640 | tf_op jit(solution)/shard_map/ppermute | solution.py:368
  77.3 1.7 %collective-permute-start.24 = (f32[2,4,48,128]{3,2,1,0:T(8,128)S(1)}, f32[2,4,48,128]{3,2,1,0:T(8,128)S(1)}, u32[]{:S(2)}, u32[]{:S(2)}) collective-permute-start(f32[2,4,48,128]{3,2,1,0:T(8,128)S(1)} %get-tuple-element.110), channel_id=1, source_target_pairs={{0,16},{4,20},{8,24},{12,28},{16,0},{20,4},{24,8},{28,12},{1,17},{... | collective-permute-start | bytes 589832 | tf_op jit(solution)/shard_map/ppermute | solution.py:368
  79.1 1.5 %collective-permute-start.25 = (f32[2,4,32,128]{3,2,1,0:T(8,128)S(1)}, f32[2,4,32,128]{3,2,1,0:T(8,128)S(1)}, u32[]{:S(2)}, u32[]{:S(2)}) collective-permute-start(f32[2,4,32,128]{3,2,1,0:T(8,128)S(1)} %get-tuple-element.112), channel_id=1, source_target_pairs={{0,8},{4,12},{8,0},{12,4},{16,24},{20,28},{24,16},{28,20},{1,9},{5... | collective-permute-start | bytes 393224 | tf_op jit(solution)/shard_map/ppermute | solution.py:368
  80.6 4.7 %collective-permute-start.31 = (f32[2,4,48,128]{3,2,1,0:T(8,128)S(1)}, f32[2,4,48,128]{3,2,1,0:T(8,128)S(1)}, u32[]{:S(2)}, u32[]{:S(2)}) collective-permute-start(f32[2,4,48,128]{3,2,1,0:T(8,128)S(1)} %shard_map.66.refs_0_), channel_id=1, source_target_pairs={{0,1},{2,3},{1,0},{3,2},{4,5},{6,7},{5,4},{7,6},{8,9},{10,11},{9,8... | collective-permute-start | bytes 589832 | tf_op jit(solution)/shard_map/ppermute | solution.py:378
  87.3 5.7 %collective-permute-start.29 = (f32[2,4,48,128]{3,2,1,0:T(8,128)S(1)}, f32[2,4,48,128]{3,2,1,0:T(8,128)S(1)}, u32[]{:S(2)}, u32[]{:S(2)}) collective-permute-start(f32[2,4,48,128]{3,2,1,0:T(8,128)S(1)} %shard_map.68.refs_1_), channel_id=1, source_target_pairs={{0,1},{2,3},{1,0},{3,2},{4,5},{6,7},{5,4},{7,6},{8,9},{10,11},{9,8... | collective-permute-start | bytes 589832 | tf_op jit(solution)/shard_map/ppermute | solution.py:378
  93.7 1.6 %collective-permute-start.27 = (f32[2,4,32,128]{3,2,1,0:T(8,128)S(1)}, f32[2,4,32,128]{3,2,1,0:T(8,128)S(1)}, u32[]{:S(2)}, u32[]{:S(2)}) collective-permute-start(f32[2,4,32,128]{3,2,1,0:T(8,128)S(1)} %shard_map.70.refs_2_), channel_id=1, source_target_pairs={{0,1},{2,3},{1,0},{3,2},{4,5},{6,7},{5,4},{7,6},{8,9},{10,11},{9,8... | collective-permute-start | bytes 393224 | tf_op jit(solution)/shard_map/ppermute | solution.py:378
  96.0 1.4 %shard_map.71 = (bf16[3,4,256,256]{3,2,1,0:T(8,128)(2,1)S(1)}, bf16[3,4,256,256]{3,2,1,0:T(8,128)(2,1)S(1)}, bf16[3,4,256,256]{3,2,1,0:T(8,128)(2,1)S(1)}, bf16[3,4,256,256]{3,2,1,0:T(8,128)(2,1)S(1)}) custom-call(s32[1,2]{1,0:T(1,128)S(1)} %copy-done.2, f32[2,4,1,2,128,128]{5,4,3,2,1,0:T(8,128)S(1)} %copy-done), custom_call_target="tpu_custom_call" | custom-call | flops 7340040 | bytes 7340040 | tf_op jit(solution)/shard_map/pallas_call | solution.py:98
  97.4 2.0 %shard_map.72.own_ref = f32[2,4,128,128]{3,2,1,0:T(8,128)S(1)} custom-call(f32[2,4,48,128]{3,2,1,0:T(8,128)S(1)} %shard_map.66.refs_0_, f32[2,4,48,128]{3,2,1,0:T(8,128)S(1)} %shard_map.68.refs_1_, f32[2,4,32,128]{3,2,1,0:T(8,128)S(1)} %shard_map.70.refs_2_, bf16[3,4,256,256]{3,2,1,0:T(8,128)(2,1)S(1)} %get-tuple-element.115.refs_3_.left_high, ...), custom_call_target="tpu_custom_call" | custom-call | flops 7340032 | bytes 7340032 | tf_op jit(solution)/shard_map/pallas_call | solution.py:98
  101.4 1.8 %shard_map.76 = f32[2,4,1,128,128]{4,3,2,1,0:T(8,128)} custom-call(f32[2,4,128,128]{3,2,1,0:T(8,128)S(1)} %shard_map.72.own_ref, bf16[3,4,256,256]{3,2,1,0:T(8,128)(2,1)S(1)} %get-tuple-element.115.refs_3_.left_high, bf16[3,4,256,256]{3,2,1,0:T(8,128)(2,1)S(1)} %get-tuple-element.116.refs_4_.left_low, bf16[4,512,128]{2,1,0:T(8,128)(2,1)S(1)} %get-tuple-element.123.mid_high, ...), custom_call_target="tpu_custom_call" | custom-call | flops 5242880 | bytes 5242880 | tf_op jit(solution)/shard_map/pallas_call | solution.py:98
  (72 shorter events, 14.4 us)
Async XLA Ops:
  1.3 10.2 %collective-permute-start = (f32[2,2,4,32,128]{4,3,2,1,0:T(8,128)S(1)}, f32[2,2,4,32,128]{4,3,2,1,0:T(8,128)S(1)}, u32[]{:S(2)}, u32[]{:S(2)}) collective-permute-start(f32[2,2,4,32,128]{4,3,2,1,0:T(8,128)S(1)} %get-tuple-element.128.own_ref), channel_id=1, source_target_pairs={{0,16},{4,20},{8,24},{12,28},{16,0},{20,4},{24,8},{28,12},{1,17},{... | collective-permute-start | bytes 786440 | tf_op jit(solution)/shard_map/ppermute | solution.py:368
  4.3 12.8 %collective-permute-start.3 = (f32[2,2,4,32,128]{4,3,2,1,0:T(8,128)S(1)}, f32[2,2,4,32,128]{4,3,2,1,0:T(8,128)S(1)}, u32[]{:S(2)}, u32[]{:S(2)}) collective-permute-start(f32[2,2,4,32,128]{4,3,2,1,0:T(8,128)S(1)} %get-tuple-element.127.own_ref), channel_id=1, source_target_pairs={{0,16},{4,20},{8,24},{12,28},{16,0},{20,4},{24,8},{28,12},{1,17},{... | collective-permute-start | bytes 786440 | tf_op jit(solution)/shard_map/ppermute | solution.py:368
  4.4 18.3 %collective-permute-start.6 = (f32[2,2,4,32,128]{4,3,2,1,0:T(8,128)S(1)}, f32[2,2,4,32,128]{4,3,2,1,0:T(8,128)S(1)}, u32[]{:S(2)}, u32[]{:S(2)}) collective-permute-start(f32[2,2,4,32,128]{4,3,2,1,0:T(8,128)S(1)} %get-tuple-element.126.own_ref), channel_id=1, source_target_pairs={{0,16},{4,20},{8,24},{12,28},{16,0},{20,4},{24,8},{28,12},{1,17},{... | collective-permute-start | bytes 786440 | tf_op jit(solution)/shard_map/ppermute | solution.py:368
  6.4 21.1 %collective-permute-start.9 = (f32[2,2,4,32,128]{4,3,2,1,0:T(8,128)S(1)}, f32[2,2,4,32,128]{4,3,2,1,0:T(8,128)S(1)}, u32[]{:S(2)}, u32[]{:S(2)}) collective-permute-start(f32[2,2,4,32,128]{4,3,2,1,0:T(8,128)S(1)} %get-tuple-element.125.own_ref), channel_id=1, source_target_pairs={{0,16},{4,20},{8,24},{12,28},{16,0},{20,4},{24,8},{28,12},{1,17},{... | collective-permute-start | bytes 786440 | tf_op jit(solution)/shard_map/ppermute | solution.py:368
  11.6 17.8 %collective-permute-start.1 = (f32[2,2,4,32,128]{4,3,2,1,0:T(8,128)S(1)}, f32[2,2,4,32,128]{4,3,2,1,0:T(8,128)S(1)}, u32[]{:S(2)}, u32[]{:S(2)}) collective-permute-start(f32[2,2,4,32,128]{4,3,2,1,0:T(8,128)S(1)} %get-tuple-element.66), channel_id=1, source_target_pairs={{0,8},{4,12},{8,0},{12,4},{16,24},{20,28},{24,16},{28,20},{1,9},{5... | collective-permute-start | bytes 786440 | tf_op jit(solution)/shard_map/ppermute | solution.py:368
  17.2 12.4 %collective-permute-start.4 = (f32[2,2,4,32,128]{4,3,2,1,0:T(8,128)S(1)}, f32[2,2,4,32,128]{4,3,2,1,0:T(8,128)S(1)}, u32[]{:S(2)}, u32[]{:S(2)}) collective-permute-start(f32[2,2,4,32,128]{4,3,2,1,0:T(8,128)S(1)} %get-tuple-element.71), channel_id=1, source_target_pairs={{0,8},{4,12},{8,0},{12,4},{16,24},{20,28},{24,16},{28,20},{1,9},{5... | collective-permute-start | bytes 786440 | tf_op jit(solution)/shard_map/ppermute | solution.py:368
  22.8 7.4 %collective-permute-start.7 = (f32[2,2,4,32,128]{4,3,2,1,0:T(8,128)S(1)}, f32[2,2,4,32,128]{4,3,2,1,0:T(8,128)S(1)}, u32[]{:S(2)}, u32[]{:S(2)}) collective-permute-start(f32[2,2,4,32,128]{4,3,2,1,0:T(8,128)S(1)} %get-tuple-element.76), channel_id=1, source_target_pairs={{0,8},{4,12},{8,0},{12,4},{16,24},{20,28},{24,16},{28,20},{1,9},{5... | collective-permute-start | bytes 786440 | tf_op jit(solution)/shard_map/ppermute | solution.py:368
  27.6 7.5 %collective-permute-start.10 = (f32[2,2,4,32,128]{4,3,2,1,0:T(8,128)S(1)}, f32[2,2,4,32,128]{4,3,2,1,0:T(8,128)S(1)}, u32[]{:S(2)}, u32[]{:S(2)}) collective-permute-start(f32[2,2,4,32,128]{4,3,2,1,0:T(8,128)S(1)} %get-tuple-element.81), channel_id=1, source_target_pairs={{0,8},{4,12},{8,0},{12,4},{16,24},{20,28},{24,16},{28,20},{1,9},{5... | collective-permute-start | bytes 786440 | tf_op jit(solution)/shard_map/ppermute | solution.py:368
  29.5 5.8 %collective-permute-start.2 = (f32[2,2,4,32,128]{4,3,2,1,0:T(8,128)S(1)}, f32[2,2,4,32,128]{4,3,2,1,0:T(8,128)S(1)}, u32[]{:S(2)}, u32[]{:S(2)}) collective-permute-start(f32[2,2,4,32,128]{4,3,2,1,0:T(8,128)S(1)} %get-tuple-element.68), channel_id=1, source_target_pairs={{0,4},{4,0},{8,12},{12,8},{16,20},{20,16},{24,28},{28,24},{1,5},{5... | collective-permute-start | bytes 786440 | tf_op jit(solution)/shard_map/ppermute | solution.py:368
  29.7 8.5 %collective-permute-start.5 = (f32[2,2,4,32,128]{4,3,2,1,0:T(8,128)S(1)}, f32[2,2,4,32,128]{4,3,2,1,0:T(8,128)S(1)}, u32[]{:S(2)}, u32[]{:S(2)}) collective-permute-start(f32[2,2,4,32,128]{4,3,2,1,0:T(8,128)S(1)} %get-tuple-element.73), channel_id=1, source_target_pairs={{0,4},{4,0},{8,12},{12,8},{16,20},{20,16},{24,28},{28,24},{1,5},{5... | collective-permute-start | bytes 786440 | tf_op jit(solution)/shard_map/ppermute | solution.py:368
  30.4 12.6 %collective-permute-start.8 = (f32[2,2,4,32,128]{4,3,2,1,0:T(8,128)S(1)}, f32[2,2,4,32,128]{4,3,2,1,0:T(8,128)S(1)}, u32[]{:S(2)}, u32[]{:S(2)}) collective-permute-start(f32[2,2,4,32,128]{4,3,2,1,0:T(8,128)S(1)} %get-tuple-element.78), channel_id=1, source_target_pairs={{0,4},{4,0},{8,12},{12,8},{16,20},{20,16},{24,28},{28,24},{1,5},{5... | collective-permute-start | bytes 786440 | tf_op jit(solution)/shard_map/ppermute | solution.py:368
  35.3 8.7 %collective-permute-start.11 = (f32[2,2,4,32,128]{4,3,2,1,0:T(8,128)S(1)}, f32[2,2,4,32,128]{4,3,2,1,0:T(8,128)S(1)}, u32[]{:S(2)}, u32[]{:S(2)}) collective-permute-start(f32[2,2,4,32,128]{4,3,2,1,0:T(8,128)S(1)} %get-tuple-element.83), channel_id=1, source_target_pairs={{0,4},{4,0},{8,12},{12,8},{16,20},{20,16},{24,28},{28,24},{1,5},{5... | collective-permute-start | bytes 786440 | tf_op jit(solution)/shard_map/ppermute | solution.py:368
  35.6 9.6 %collective-permute-start.18 = (f32[2,8,32,128]{3,2,1,0:T(8,128)S(1)}, f32[2,8,32,128]{3,2,1,0:T(8,128)S(1)}, u32[]{:S(2)}, u32[]{:S(2)}) collective-permute-start(f32[2,8,32,128]{3,2,1,0:T(8,128)S(1)} %get-tuple-element.92.refs_0_), channel_id=1, source_target_pairs={{0,1},{2,3},{1,0},{3,2},{4,5},{6,7},{5,4},{7,6},{8,9},{10,11},{9,8... | collective-permute-start | bytes 786440 | tf_op jit(solution)/shard_map/ppermute | solution.py:378
  37.5 8.7 %collective-permute-start.19 = (f32[2,8,32,128]{3,2,1,0:T(8,128)S(1)}, f32[2,8,32,128]{3,2,1,0:T(8,128)S(1)}, u32[]{:S(2)}, u32[]{:S(2)}) collective-permute-start(f32[2,8,32,128]{3,2,1,0:T(8,128)S(1)} %get-tuple-element.92.refs_0_), channel_id=1, source_target_pairs={{1,2},{2,1},{5,6},{6,5},{9,10},{10,9},{13,14},{14,13},{17,18},{18,... | collective-permute-start | bytes 786440 | tf_op jit(solution)/shard_map/ppermute | solution.py:378
  38.5 12.1 %collective-permute-start.16 = (f32[2,8,32,128]{3,2,1,0:T(8,128)S(1)}, f32[2,8,32,128]{3,2,1,0:T(8,128)S(1)}, u32[]{:S(2)}, u32[]{:S(2)}) collective-permute-start(f32[2,8,32,128]{3,2,1,0:T(8,128)S(1)} %get-tuple-element.91.refs_0_), channel_id=1, source_target_pairs={{0,1},{2,3},{1,0},{3,2},{4,5},{6,7},{5,4},{7,6},{8,9},{10,11},{9,8... | collective-permute-start | bytes 786440 | tf_op jit(solution)/shard_map/ppermute | solution.py:378
  43.0 9.5 %collective-permute-start.17 = (f32[2,8,32,128]{3,2,1,0:T(8,128)S(1)}, f32[2,8,32,128]{3,2,1,0:T(8,128)S(1)}, u32[]{:S(2)}, u32[]{:S(2)}) collective-permute-start(f32[2,8,32,128]{3,2,1,0:T(8,128)S(1)} %get-tuple-element.91.refs_0_), channel_id=1, source_target_pairs={{1,2},{2,1},{5,6},{6,5},{9,10},{10,9},{13,14},{14,13},{17,18},{18,... | collective-permute-start | bytes 786440 | tf_op jit(solution)/shard_map/ppermute | solution.py:378
  43.9 12.2 %collective-permute-start.14 = (f32[2,8,32,128]{3,2,1,0:T(8,128)S(1)}, f32[2,8,32,128]{3,2,1,0:T(8,128)S(1)}, u32[]{:S(2)}, u32[]{:S(2)}) collective-permute-start(f32[2,8,32,128]{3,2,1,0:T(8,128)S(1)} %get-tuple-element.90.refs_0_), channel_id=1, source_target_pairs={{0,1},{2,3},{1,0},{3,2},{4,5},{6,7},{5,4},{7,6},{8,9},{10,11},{9,8... | collective-permute-start | bytes 786440 | tf_op jit(solution)/shard_map/ppermute | solution.py:378
  45.3 10.8 %collective-permute-start.15 = (f32[2,8,32,128]{3,2,1,0:T(8,128)S(1)}, f32[2,8,32,128]{3,2,1,0:T(8,128)S(1)}, u32[]{:S(2)}, u32[]{:S(2)}) collective-permute-start(f32[2,8,32,128]{3,2,1,0:T(8,128)S(1)} %get-tuple-element.90.refs_0_), channel_id=1, source_target_pairs={{1,2},{2,1},{5,6},{6,5},{9,10},{10,9},{13,14},{14,13},{17,18},{18,... | collective-permute-start | bytes 786440 | tf_op jit(solution)/shard_map/ppermute | solution.py:378
  46.3 15.0 %collective-permute-start.12 = (f32[2,8,32,128]{3,2,1,0:T(8,128)S(1)}, f32[2,8,32,128]{3,2,1,0:T(8,128)S(1)}, u32[]{:S(2)}, u32[]{:S(2)}) collective-permute-start(f32[2,8,32,128]{3,2,1,0:T(8,128)S(1)} %get-tuple-element.87.refs_0_), channel_id=1, source_target_pairs={{0,1},{2,3},{1,0},{3,2},{4,5},{6,7},{5,4},{7,6},{8,9},{10,11},{9,8... | collective-permute-start | bytes 786440 | tf_op jit(solution)/shard_map/ppermute | solution.py:378
  50.6 10.7 %collective-permute-start.13 = (f32[2,8,32,128]{3,2,1,0:T(8,128)S(1)}, f32[2,8,32,128]{3,2,1,0:T(8,128)S(1)}, u32[]{:S(2)}, u32[]{:S(2)}) collective-permute-start(f32[2,8,32,128]{3,2,1,0:T(8,128)S(1)} %get-tuple-element.87.refs_0_), channel_id=1, source_target_pairs={{1,2},{2,1},{5,6},{6,5},{9,10},{10,9},{13,14},{14,13},{17,18},{18,... | collective-permute-start | bytes 786440 | tf_op jit(solution)/shard_map/ppermute | solution.py:378
  66.0 7.8 %collective-permute-start.21 = (f32[2,4,48,128]{3,2,1,0:T(8,128)S(1)}, f32[2,4,48,128]{3,2,1,0:T(8,128)S(1)}, u32[]{:S(2)}, u32[]{:S(2)}) collective-permute-start(f32[2,4,48,128]{3,2,1,0:T(8,128)S(1)} %get-tuple-element.104), channel_id=1, source_target_pairs={{0,8},{4,12},{8,0},{12,4},{16,24},{20,28},{24,16},{28,20},{1,9},{5... | collective-permute-start | bytes 589832 | tf_op jit(solution)/shard_map/ppermute | solution.py:368
  67.7 9.5 %collective-permute-start.23 = (f32[2,4,48,128]{3,2,1,0:T(8,128)S(1)}, f32[2,4,48,128]{3,2,1,0:T(8,128)S(1)}, u32[]{:S(2)}, u32[]{:S(2)}) collective-permute-start(f32[2,4,48,128]{3,2,1,0:T(8,128)S(1)} %get-tuple-element.108), channel_id=1, source_target_pairs={{0,8},{4,12},{8,0},{12,4},{16,24},{20,28},{24,16},{28,20},{1,9},{5... | collective-permute-start | bytes 589832 | tf_op jit(solution)/shard_map/ppermute | solution.py:368
  74.0 6.6 %collective-permute-start.22 = (f32[2,4,48,128]{3,2,1,0:T(8,128)S(1)}, f32[2,4,48,128]{3,2,1,0:T(8,128)S(1)}, u32[]{:S(2)}, u32[]{:S(2)}) collective-permute-start(f32[2,4,48,128]{3,2,1,0:T(8,128)S(1)} %get-tuple-element.106), channel_id=1, source_target_pairs={{0,16},{4,20},{8,24},{12,28},{16,0},{20,4},{24,8},{28,12},{1,17},{... | collective-permute-start | bytes 589832 | tf_op jit(solution)/shard_map/ppermute | solution.py:368
  77.3 9.9 %collective-permute-start.24 = (f32[2,4,48,128]{3,2,1,0:T(8,128)S(1)}, f32[2,4,48,128]{3,2,1,0:T(8,128)S(1)}, u32[]{:S(2)}, u32[]{:S(2)}) collective-permute-start(f32[2,4,48,128]{3,2,1,0:T(8,128)S(1)} %get-tuple-element.110), channel_id=1, source_target_pairs={{0,16},{4,20},{8,24},{12,28},{16,0},{20,4},{24,8},{28,12},{1,17},{... | collective-permute-start | bytes 589832 | tf_op jit(solution)/shard_map/ppermute | solution.py:368
  79.1 6.2 %collective-permute-start.25 = (f32[2,4,32,128]{3,2,1,0:T(8,128)S(1)}, f32[2,4,32,128]{3,2,1,0:T(8,128)S(1)}, u32[]{:S(2)}, u32[]{:S(2)}) collective-permute-start(f32[2,4,32,128]{3,2,1,0:T(8,128)S(1)} %get-tuple-element.112), channel_id=1, source_target_pairs={{0,8},{4,12},{8,0},{12,4},{16,24},{20,28},{24,16},{28,20},{1,9},{5... | collective-permute-start | bytes 393224 | tf_op jit(solution)/shard_map/ppermute | solution.py:368
  80.6 14.8 %collective-permute-start.31 = (f32[2,4,48,128]{3,2,1,0:T(8,128)S(1)}, f32[2,4,48,128]{3,2,1,0:T(8,128)S(1)}, u32[]{:S(2)}, u32[]{:S(2)}) collective-permute-start(f32[2,4,48,128]{3,2,1,0:T(8,128)S(1)} %shard_map.66.refs_0_), channel_id=1, source_target_pairs={{0,1},{2,3},{1,0},{3,2},{4,5},{6,7},{5,4},{7,6},{8,9},{10,11},{9,8... | collective-permute-start | bytes 589832 | tf_op jit(solution)/shard_map/ppermute | solution.py:378
  85.3 8.4 %collective-permute-start.26 = (f32[2,4,32,128]{3,2,1,0:T(8,128)S(1)}, f32[2,4,32,128]{3,2,1,0:T(8,128)S(1)}, u32[]{:S(2)}, u32[]{:S(2)}) collective-permute-start(f32[2,4,32,128]{3,2,1,0:T(8,128)S(1)} %get-tuple-element.114), channel_id=1, source_target_pairs={{0,16},{4,20},{8,24},{12,28},{16,0},{20,4},{24,8},{28,12},{1,17},{... | collective-permute-start | bytes 393224 | tf_op jit(solution)/shard_map/ppermute | solution.py:368
  86.6 12.8 %collective-permute-start.32 = (f32[2,4,48,128]{3,2,1,0:T(8,128)S(1)}, f32[2,4,48,128]{3,2,1,0:T(8,128)S(1)}, u32[]{:S(2)}, u32[]{:S(2)}) collective-permute-start(f32[2,4,48,128]{3,2,1,0:T(8,128)S(1)} %shard_map.66.refs_0_), channel_id=1, source_target_pairs={{1,2},{2,1},{5,6},{6,5},{9,10},{10,9},{13,14},{14,13},{17,18},{18,... | collective-permute-start | bytes 589832 | tf_op jit(solution)/shard_map/ppermute | solution.py:378
  87.3 12.8 %collective-permute-start.29 = (f32[2,4,48,128]{3,2,1,0:T(8,128)S(1)}, f32[2,4,48,128]{3,2,1,0:T(8,128)S(1)}, u32[]{:S(2)}, u32[]{:S(2)}) collective-permute-start(f32[2,4,48,128]{3,2,1,0:T(8,128)S(1)} %shard_map.68.refs_1_), channel_id=1, source_target_pairs={{0,1},{2,3},{1,0},{3,2},{4,5},{6,7},{5,4},{7,6},{8,9},{10,11},{9,8... | collective-permute-start | bytes 589832 | tf_op jit(solution)/shard_map/ppermute | solution.py:378
  93.0 7.1 %collective-permute-start.30 = (f32[2,4,48,128]{3,2,1,0:T(8,128)S(1)}, f32[2,4,48,128]{3,2,1,0:T(8,128)S(1)}, u32[]{:S(2)}, u32[]{:S(2)}) collective-permute-start(f32[2,4,48,128]{3,2,1,0:T(8,128)S(1)} %shard_map.68.refs_1_), channel_id=1, source_target_pairs={{1,2},{2,1},{5,6},{6,5},{9,10},{10,9},{13,14},{14,13},{17,18},{18,... | collective-permute-start | bytes 589832 | tf_op jit(solution)/shard_map/ppermute | solution.py:378
  93.7 7.0 %collective-permute-start.27 = (f32[2,4,32,128]{3,2,1,0:T(8,128)S(1)}, f32[2,4,32,128]{3,2,1,0:T(8,128)S(1)}, u32[]{:S(2)}, u32[]{:S(2)}) collective-permute-start(f32[2,4,32,128]{3,2,1,0:T(8,128)S(1)} %shard_map.70.refs_2_), channel_id=1, source_target_pairs={{0,1},{2,3},{1,0},{3,2},{4,5},{6,7},{5,4},{7,6},{8,9},{10,11},{9,8... | collective-permute-start | bytes 393224 | tf_op jit(solution)/shard_map/ppermute | solution.py:378
  95.4 5.4 %collective-permute-start.28 = (f32[2,4,32,128]{3,2,1,0:T(8,128)S(1)}, f32[2,4,32,128]{3,2,1,0:T(8,128)S(1)}, u32[]{:S(2)}, u32[]{:S(2)}) collective-permute-start(f32[2,4,32,128]{3,2,1,0:T(8,128)S(1)} %shard_map.70.refs_2_), channel_id=1, source_target_pairs={{1,2},{2,1},{5,6},{6,5},{9,10},{10,9},{13,14},{14,13},{17,18},{18,... | collective-permute-start | bytes 393224 | tf_op jit(solution)/shard_map/ppermute | solution.py:378
  (4 other events, 74.0 us)

commit v4 on v3

--- a/solution.py
+++ b/solution.py
@@ -232,30 +232,35 @@
     return [0, side, -side]
 
 
-def prepare_coulomb(scale, offsets_ref, coulomb_ref, left_high, left_low, right_high, right_low):
+def hits(offsets_ref, row, cells, place):
+    inside = jnp.logical_and(row + place >= 0, row + place < cells)
+    return [jnp.logical_and(inside, offsets_ref[0, j] == place) for j in range(2)]
+
+
+def prepare_coulomb(scale, cells, offsets_ref, coulomb_ref, left_high, left_low, right_high, right_low):
     row = lax.axis_index("cell")
     order = coulomb_ref.shape[-1]
     for slot, place in enumerate(places_of(row)):
-        hit = [offsets_ref[0, j] == place for j in range(2)]
+        hit = hits(offsets_ref, row, cells, place)
         value = chosen(hit, coulomb_ref[0, 0], coulomb_ref[0, 1])
         at = slice(slot * order, (slot + 1) * order)
         left_high[:, at], left_low[:, at] = halves(value)
         right_high[slot], right_low[slot] = halves(value.T * scale)
 
 
-def prepare_green(offsets_ref, green_ref, left_high, left_low, right_high, right_low):
+def prepare_green(cells, offsets_ref, green_ref, left_high, left_low, right_high, right_low):
     row = lax.axis_index("cell")
     local, order = green_ref.shape[1], green_ref.shape[-1]
     low, top = slice(0, order), slice(order, 2 * order)
     for slot, place in enumerate(places_of(row)):
-        hit = [offsets_ref[0, j] == place for j in range(2)]
+        hit = hits(offsets_ref, row, cells, place)
         for e in range(local):
             parts = [chosen(hit, green_ref[i, e, 0, 0], green_ref[i, e, 0, 1]) for i in range(2)]
-            re, im = (halves(p) for p in parts)
+            for i, part in enumerate(parts):
+                at = slice((2 * slot + i) * order, (2 * slot + i + 1) * order)
+                left_high[e, :, at], left_low[e, :, at] = halves(part)
             re_t, im_t = (halves(p.T) for p in parts)
-            for i, (left, right) in enumerate(((left_high, right_high), (left_low, right_low))):
-                left[slot, e, low, low], left[slot, e, top, top] = re[i], re[i]
-                left[slot, e, low, top], left[slot, e, top, low] = -im[i], im[i]
+            for i, right in enumerate((right_high, right_low)):
                 right[slot, e, low, low], right[slot, e, top, top] = re_t[i], re_t[i]
                 right[slot, e, top, low], right[slot, e, low, top] = -im_t[i], im_t[i]
 
@@ -267,20 +272,19 @@
         value = halves(ref[...].reshape(2 * count * rows, order))
         result = halves(product_of(value, (right_high[slot], right_low[slot])))
         at = slice(slot * order + start, slot * order + start + rows)
-        for i, out in enumerate((out_high, out_low)):
-            out[:, :, at] = result[i].reshape(2, count, rows, order)
+        for out, value in zip((out_high, out_low), result):
+            value = value.reshape(2, count, rows, order)
+            for i in range(2):
+                out[:, at, i * order : (i + 1) * order] = value[i]
 
 
 def inverse_kernel(bits, sizes, *refs):
     me = lax.axis_index("wide")
     lesser_refs, refs = refs[: len(sizes)], refs[len(sizes) :]
     left_high, left_low, mid_high, mid_low, keep_ref, send_ref, screened = refs
-    for i in range(2):
-        for f in range(mid_high.shape[1]):
-            screened[i, f] = product_of(
-                (left_high[...], left_low[...]), (mid_high[i, f], mid_low[i, f])
-            )
-    local = keep_ref.shape[1]
+    for f in range(mid_high.shape[0]):
+        screened[f] = product_of((left_high[...], left_low[...]), (mid_high[f], mid_low[f]))
+    local, order = keep_ref.shape[1], keep_ref.shape[-1]
     peers = 1 << bits
     period = 2 * peers * local
     mine = own_bit(me, 0)
@@ -299,7 +303,7 @@
                 for t in range(local):
                     f = top * local + t
                     a = (lesser_ref[0, f, at], lesser_ref[1, f, at])
-                    values.append(times(a, screened[0, f, to], screened[1, f, to]))
+                    values.append(times(a, screened[f, to, :order], screened[f, to, order:]))
                 values = dft(values, 1)
                 tops.append(
                     [v if j == 0 else times(v, *twist[top][j]) for j, v in enumerate(values)]
@@ -322,39 +326,65 @@
 
 def own_dressing_kernel(count, *refs):
     blocks, (left_high, left_low, right_high, right_low, out_ref) = refs[:count], refs[count:]
-    local, order = out_ref.shape[1], out_ref.shape[-1]
+    local, order = out_ref.shape[0], out_ref.shape[1]
     for e in range(local):
         parts = [times_right(b, e, right_high, right_low, 0) for b in blocks]
-        middle = jnp.concatenate(
-            [p[:, :order] for p in parts] + [p[:, order:] for p in parts], axis=0
-        )
-        out = product_of((left_high[0, e], left_low[0, e]), halves(middle))
-        out_ref[0, e], out_ref[1, e] = out[:order], out[order:]
+        value = jnp.concatenate(parts, axis=0)
+        turned = jnp.concatenate([-value[:, order:], value[:, :order]], axis=-1)
+        middle = halves(jnp.concatenate([value, turned], axis=0))
+        out_ref[e] = product_of(
+            (left_high[e, :, : 2 * order], left_low[e, :, : 2 * order]), middle
+        )
 
 
 def dress_kernel(start, *refs):
     blocks, (right_high, right_low), (out_high, out_low) = refs[:2], refs[2:4], refs[-2:]
     local, rows, order = blocks[0].shape[1], blocks[0].shape[2], blocks[0].shape[3]
     for slot, ref in enumerate(blocks):
+        plain = slice(2 * slot * order + start, 2 * slot * order + start + rows)
+        turned = slice((2 * slot + 1) * order + start, (2 * slot + 1) * order + start + rows)
         for e in range(local):
             result = halves(times_right(ref, e, right_high, right_low, slot + 1))
-            for p in range(2):
-                to = slice((2 * slot + p) * order + start, (2 * slot + p) * order + start + rows)
-                at = slice(p * order, (p + 1) * order)
-                out_high[e, to], out_low[e, to] = result[0][:, at], result[1][:, at]
+            for out, value in zip((out_high, out_low), result):
+                out[e, plain] = value
+                out[e, turned, :order], out[e, turned, order:] = -value[:, order:], value[:, :order]
 
 
 def finish_kernel(own_ref, left_high, left_low, mid_high, mid_low, out_ref):
     local, order = out_ref.shape[1], out_ref.shape[-1]
     for e in range(local):
-        total = 0.0
-        for slot in range(2):
-            at = slice(2 * slot * order, 2 * (slot + 1) * order)
-            total = total + product_of(
-                (left_high[slot + 1, e], left_low[slot + 1, e]), (mid_high[e, at], mid_low[e, at])
-            )
-        out_ref[0, e, 0] = own_ref[0, e] + total[:order]
-        out_ref[1, e, 0] = own_ref[1, e] + total[order:]
+        total = own_ref[e] + product_of(
+            (left_high[e, :, 2 * order :], left_low[e, :, 2 * order :]), (mid_high[e], mid_low[e])
+        )
+        out_ref[0, e, 0], out_ref[1, e, 0] = total[:, :order], total[:, order:]
+
+
+def cut_kernel(starts, source_ref, *refs):
+    outs, sems = refs[: len(starts)], refs[len(starts)]
+    copies = [
+        pltpu.make_async_copy(
+            source_ref.at[:, :, :, 0, pl.ds(start, out.shape[3])], out, sems.at[k]
+        )
+        for k, (start, out) in enumerate(zip(starts, outs))
+    ]
+    for copy in copies:
+        copy.start()
+    for copy in copies:
+        copy.wait()
+
+
+def cut(value, starts, sizes):
+    shapes = [full(value.shape[:3] + (size, value.shape[-1])) for size in sizes]
+    return pl.pallas_call(
+        partial(cut_kernel, starts),
+        out_shape=shapes,
+        in_specs=[pl.BlockSpec(memory_space=pl.ANY)],
+        out_specs=[pl.BlockSpec(memory_space=pltpu.VMEM) for _ in shapes],
+        scratch_shapes=[pltpu.SemaphoreType.DMA((len(shapes),))],
+        compiler_params=pltpu.CompilerParams(
+            vmem_limit_bytes=4 * sum(o.size for o in shapes) + (1 << 19)
+        ),
+    )(value)
 
 
 def body(green_pair, coulomb, green_retarded, offsets):
@@ -369,28 +399,34 @@
 
     links = []
     for first in range(2):
-        up = [(i, i + 1) for i in range(first, cells - 1, 2)]
-        links.append(up + [(j, i) for i, j in up])
+        partner = list(range(cells))
+        for i in range(first, cells - 1, 2):
+            partner[i], partner[i + 1] = i + 1, i
+        links.append(
+            [
+                (d * cells + c, (d ^ (c == partner[c])) * cells + partner[c])
+                for d in range(peers) for c in range(cells)
+            ]
+        )
 
     def beside(value):
         blocks = []
         for pairs in links:
-            blocks.append(lax.ppermute(value, "cell", pairs))
+            blocks.append(lax.ppermute(value, ("wide", "cell"), pairs))
         return blocks
 
-    pair = green_pair[:, :, :, 0]
     sizes = heights(order, FORWARD)
-    keep = [
-        lax.slice_in_dim(pair, at, at + size, axis=3) for at, size in zip(starts_of(sizes), sizes)
-    ]
+    starts = starts_of(sizes)
+    keep = [*cut(green_pair, starts[:1], sizes[:1]), *cut(green_pair, starts[1:], sizes[1:])]
     got = [swap(own, bits - 1) for own in keep]
     coulomb_shapes = [(order, 3 * order)] * 2 + [(3, order, order)] * 2
     coulombs = call(
-        partial(prepare_coulomb, scale), [half(c) for c in coulomb_shapes],
+        partial(prepare_coulomb, scale, cells), [half(c) for c in coulomb_shapes],
         offsets, coulomb, smem=(0,),
     )
     greens = call(
-        prepare_green, [half((3, local, 2 * order, 2 * order))] * 4,
+        partial(prepare_green, cells),
+        [half((local, order, 6 * order))] * 2 + [half((3, local, 2 * order, 2 * order))] * 2,
         offsets, green_retarded, smem=(0,),
     )
     lesser, near = [None] * FORWARD, [None] * FORWARD
@@ -411,13 +447,13 @@
     for k, start in enumerate(starts_of(sizes)):
         middle = call(
             partial(screen_kernel, start),
-            [half((2, 2 * local, 3 * order, order))] * 2, *near[k], *coulombs[2:], *middle,
+            [half((2 * local, 3 * order, 2 * order))] * 2, *near[k], *coulombs[2:], *middle,
             alias={5: 0, 6: 1} if k else None,
         )
     keep, send = call(
         partial(inverse_kernel, bits, sizes),
         [(2, local, order, order)] * 2, *lesser, *coulombs[:2], *middle,
-        scratch=[(2, 2 * local, order, order)],
+        scratch=[(2 * local, order, 2 * order)],
     )
     got = swap(send, 0)
     sizes = heights(order, BACKWARD)
@@ -439,13 +475,13 @@
             sigma, = call(add_kernel, [keep[k].shape], keep[k], got[k])
             near[k] = [sigma] + beside(sigma)
     own, = call(
-        partial(own_dressing_kernel, BACKWARD), [(2, local, order, order)],
+        partial(own_dressing_kernel, BACKWARD), [(local, order, 2 * order)],
         *[n[0] for n in near], *greens,
     )
     middle = []
     for k, start in enumerate(starts_of(sizes)):
         middle = call(
-            partial(dress_kernel, start), [half((local, 4 * order, order))] * 2,
+            partial(dress_kernel, start), [half((local, 4 * order, 2 * order))] * 2,
             *near[k][1:], *greens[2:], *middle, alias={4: 0, 5: 1} if k else None,
         )
     result, = call(finish_kernel, [(2, local, 1, order, order)], own, *greens[:2], *middle)

time: 104 us -> 98.6 us (0.948)
  starting transfers between devices: 50.9 us -> 41.9 us
  waiting for transfers between devices: 36.4 us -> 41.5 us
  Pallas kernels: 14.1 us -> 12.8 us
    ppermute x14, starting transfers between devices: 28.6 us -> 19.2 us  [beside(): blocks.append(lax.ppermute(value, ('wide', 'cell'), pairs))]
    ppermute x14, waiting for transfers between devices: 7.95 us -> 13.5 us  [beside(): blocks.append(lax.ppermute(value, ('wide', 'cell'), pairs))]
    pallas_call x31, Pallas kernels: 14.1 us -> 12.7 us  [call(): pl.pallas_call(kernel, out_shape=outs, in_specs=specs, out_specs=[pl.Bloc...]
    slice x1 -> x0, local copies, waits for them, and re-layouts: 1.28 us -> none  [body(): lax.slice_in_dim(pair, at, at + size, axis=3)]
    unnamed x6 -> x10, local copies, waits for them, and re-layouts: 0.01 us -> 1.24 us
  transfers between devices with their start and end apart: 33 -> 33, of which waited for: 10 -> 13; matrix products, arithmetic and copies ran while one was open for 0% -> 0% of each run, Pallas kernels for 9% -> 9%
where the time goes in v4:
time: 98.6 us; the launch traced here: 97.8 us
  starting transfers between devices  41.9 us (42%)
  waiting for transfers between devices  41.5 us (42%)
  Pallas kernels  12.8 us (13%)
  local copies, waits for them, and re-layouts  1.24 us (1%)
    ppermute x19, waiting for transfers between devices, swap(): lax.ppermute(value, 'wide', [(i, i ^ 1 << bit) for i in range(peers)])  27.9 us
    ppermute x19, starting transfers between devices, swap(): lax.ppermute(value, 'wide', [(i, i ^ 1 << bit) for i in range(peers)])  22.8 us
    ppermute x14, starting transfers between devices, beside(): blocks.append(lax.ppermute(value, ('wide', 'cell'), pairs))  19.2 us
    ppermute x14, waiting for transfers between devices, beside(): blocks.append(lax.ppermute(value, ('wide', 'cell'), pairs))  13.5 us
    pallas_call x31, Pallas kernels, call(): pl.pallas_call(kernel, out_shape=outs, in_specs=specs, out_specs=[pl.Bloc...  12.7 us
  transfers between devices with their start and end apart: 33, of which 13 were waited for; matrix products, arithmetic and copies ran while one was open for 0% of the time, Pallas kernels for 9%

profile of v4, /device:TPU:0, one launch (start us, length us, event | category | flops | bytes accessed | tf_op | source)
XLA Modules:
  0.0 97.8 jit_solution(18317950199691296477)
XLA Ops:
  0.0 1.2 %copy-done = f32[2,2,4,1,128,128]{5,4,3,2,1,0:T(8,128)S(1)} copy-done((f32[2,2,4,1,128,128]{5,4,3,2,1,0:T(8,128)S(1)}, f32[2,2,4,1,128,128]{5,4,3,2,1,0:T(8,128)}, u32[]{:S(2)}) %copy-start) | copy-done | bytes 1048600
  1.3 3.1 %collective-permute-start = (f32[2,2,4,32,128]{4,3,2,1,0:T(8,128)S(1)}, f32[2,2,4,32,128]{4,3,2,1,0:T(8,128)S(1)}, u32[]{:S(2)}, u32[]{:S(2)}) collective-permute-start(f32[2,2,4,32,128]{4,3,2,1,0:T(8,128)S(1)} %shard_map.46.own_ref), channel_id=1, source_target_pairs={{0,16},{4,20},{8,24},{12,28},{16,0},{20,4},{24,8},{28,12},{1,17},{... | collective-permute-start | bytes 786440 | tf_op jit(solution)/shard_map/ppermute | solution.py:398
  7.6 3.8 %collective-permute-done.got_ref = f32[2,2,4,32,128]{4,3,2,1,0:T(8,128)S(1)} collective-permute-done((f32[2,2,4,32,128]{4,3,2,1,0:T(8,128)S(1)}, f32[2,2,4,32,128]{4,3,2,1,0:T(8,128)S(1)}, u32[]{:S(2)}, u32[]{:S(2)}) %collective-permute-start) | collective-permute-done | bytes 262176 | tf_op jit(solution)/shard_map/ppermute | solution.py:398
  11.6 2.1 %collective-permute-start.1 = (f32[2,2,4,32,128]{4,3,2,1,0:T(8,128)S(1)}, f32[2,2,4,32,128]{4,3,2,1,0:T(8,128)S(1)}, u32[]{:S(2)}, u32[]{:S(2)}) collective-permute-start(f32[2,2,4,32,128]{4,3,2,1,0:T(8,128)S(1)} %get-tuple-element.69), channel_id=1, source_target_pairs={{0,8},{4,12},{8,0},{12,4},{16,24},{20,28},{24,16},{28,20},{1,9},{5... | collective-permute-start | bytes 786440 | tf_op jit(solution)/shard_map/ppermute | solution.py:398
  13.6 3.5 %collective-permute-done.3.got_ref = f32[2,2,4,32,128]{4,3,2,1,0:T(8,128)S(1)} collective-permute-done((f32[2,2,4,32,128]{4,3,2,1,0:T(8,128)S(1)}, f32[2,2,4,32,128]{4,3,2,1,0:T(8,128)S(1)}, u32[]{:S(2)}, u32[]{:S(2)}) %collective-permute-start.3) | collective-permute-done | bytes 262176 | tf_op jit(solution)/shard_map/ppermute | solution.py:398
  17.2 2.1 %collective-permute-start.4 = (f32[2,2,4,32,128]{4,3,2,1,0:T(8,128)S(1)}, f32[2,2,4,32,128]{4,3,2,1,0:T(8,128)S(1)}, u32[]{:S(2)}, u32[]{:S(2)}) collective-permute-start(f32[2,2,4,32,128]{4,3,2,1,0:T(8,128)S(1)} %get-tuple-element.75), channel_id=1, source_target_pairs={{0,8},{4,12},{8,0},{12,4},{16,24},{20,28},{24,16},{28,20},{1,9},{5... | collective-permute-start | bytes 786440 | tf_op jit(solution)/shard_map/ppermute | solution.py:398
  19.3 3.5 %collective-permute-done.6.got_ref = f32[2,2,4,32,128]{4,3,2,1,0:T(8,128)S(1)} collective-permute-done((f32[2,2,4,32,128]{4,3,2,1,0:T(8,128)S(1)}, f32[2,2,4,32,128]{4,3,2,1,0:T(8,128)S(1)}, u32[]{:S(2)}, u32[]{:S(2)}) %collective-permute-start.6) | collective-permute-done | bytes 262176 | tf_op jit(solution)/shard_map/ppermute | solution.py:398
  22.8 2.1 %collective-permute-start.7 = (f32[2,2,4,32,128]{4,3,2,1,0:T(8,128)S(1)}, f32[2,2,4,32,128]{4,3,2,1,0:T(8,128)S(1)}, u32[]{:S(2)}, u32[]{:S(2)}) collective-permute-start(f32[2,2,4,32,128]{4,3,2,1,0:T(8,128)S(1)} %get-tuple-element.81), channel_id=1, source_target_pairs={{0,8},{4,12},{8,0},{12,4},{16,24},{20,28},{24,16},{28,20},{1,9},{5... | collective-permute-start | bytes 786440 | tf_op jit(solution)/shard_map/ppermute | solution.py:398
  24.9 2.6 %collective-permute-done.9.got_ref = f32[2,2,4,32,128]{4,3,2,1,0:T(8,128)S(1)} collective-permute-done((f32[2,2,4,32,128]{4,3,2,1,0:T(8,128)S(1)}, f32[2,2,4,32,128]{4,3,2,1,0:T(8,128)S(1)}, u32[]{:S(2)}, u32[]{:S(2)}) %collective-permute-start.9) | collective-permute-done | bytes 262176 | tf_op jit(solution)/shard_map/ppermute | solution.py:398
  27.6 1.8 %collective-permute-start.10 = (f32[2,2,4,32,128]{4,3,2,1,0:T(8,128)S(1)}, f32[2,2,4,32,128]{4,3,2,1,0:T(8,128)S(1)}, u32[]{:S(2)}, u32[]{:S(2)}) collective-permute-start(f32[2,2,4,32,128]{4,3,2,1,0:T(8,128)S(1)} %get-tuple-element.87), channel_id=1, source_target_pairs={{0,8},{4,12},{8,0},{12,4},{16,24},{20,28},{24,16},{28,20},{1,9},{5... | collective-permute-start | bytes 786440 | tf_op jit(solution)/shard_map/ppermute | solution.py:398
  30.5 4.7 %collective-permute-done.10.got_ref = f32[2,2,4,32,128]{4,3,2,1,0:T(8,128)S(1)} collective-permute-done((f32[2,2,4,32,128]{4,3,2,1,0:T(8,128)S(1)}, f32[2,2,4,32,128]{4,3,2,1,0:T(8,128)S(1)}, u32[]{:S(2)}, u32[]{:S(2)}) %collective-permute-start.10) | collective-permute-done | bytes 262176 | tf_op jit(solution)/shard_map/ppermute | solution.py:398
  35.6 1.9 %collective-permute-start.18 = (f32[2,8,32,128]{3,2,1,0:T(8,128)S(1)}, f32[2,8,32,128]{3,2,1,0:T(8,128)S(1)}, u32[]{:S(2)}, u32[]{:S(2)}) collective-permute-start(f32[2,8,32,128]{3,2,1,0:T(8,128)S(1)} %get-tuple-element.98.refs_0_), channel_id=1, source_target_pairs={{0,1},{1,0},{2,3},{3,2},{4,5},{5,4},{6,7},{7,6},{8,9},{9,8},{10,11... | collective-permute-start | bytes 786440 | tf_op jit(solution)/shard_map/ppermute | solution.py:415
  37.9 3.1 %collective-permute-start.16 = (f32[2,8,32,128]{3,2,1,0:T(8,128)S(1)}, f32[2,8,32,128]{3,2,1,0:T(8,128)S(1)}, u32[]{:S(2)}, u32[]{:S(2)}) collective-permute-start(f32[2,8,32,128]{3,2,1,0:T(8,128)S(1)} %get-tuple-element.97.refs_0_), channel_id=1, source_target_pairs={{0,1},{1,0},{2,3},{3,2},{4,5},{5,4},{6,7},{7,6},{8,9},{9,8},{10,11... | collective-permute-start | bytes 786440 | tf_op jit(solution)/shard_map/ppermute | solution.py:415
  41.9 3.0 %collective-permute-done.18.refs_1_ = f32[2,8,32,128]{3,2,1,0:T(8,128)S(1)} collective-permute-done((f32[2,8,32,128]{3,2,1,0:T(8,128)S(1)}, f32[2,8,32,128]{3,2,1,0:T(8,128)S(1)}, u32[]{:S(2)}, u32[]{:S(2)}) %collective-permute-start.18) | collective-permute-done | bytes 262176 | tf_op jit(solution)/shard_map/ppermute | solution.py:415
  45.1 3.5 %collective-permute-start.12 = (f32[2,8,32,128]{3,2,1,0:T(8,128)S(1)}, f32[2,8,32,128]{3,2,1,0:T(8,128)S(1)}, u32[]{:S(2)}, u32[]{:S(2)}) collective-permute-start(f32[2,8,32,128]{3,2,1,0:T(8,128)S(1)} %get-tuple-element.93.refs_0_), channel_id=1, source_target_pairs={{0,1},{1,0},{2,3},{3,2},{4,5},{5,4},{6,7},{7,6},{8,9},{9,8},{10,11... | collective-permute-start | bytes 786440 | tf_op jit(solution)/shard_map/ppermute | solution.py:415
  48.6 1.9 %collective-permute-done.16.refs_1_ = f32[2,8,32,128]{3,2,1,0:T(8,128)S(1)} collective-permute-done((f32[2,8,32,128]{3,2,1,0:T(8,128)S(1)}, f32[2,8,32,128]{3,2,1,0:T(8,128)S(1)}, u32[]{:S(2)}, u32[]{:S(2)}) %collective-permute-start.16) | collective-permute-done | bytes 262176 | tf_op jit(solution)/shard_map/ppermute | solution.py:415
  52.2 3.9 %collective-permute-done.14.refs_1_ = f32[2,8,32,128]{3,2,1,0:T(8,128)S(1)} collective-permute-done((f32[2,8,32,128]{3,2,1,0:T(8,128)S(1)}, f32[2,8,32,128]{3,2,1,0:T(8,128)S(1)}, u32[]{:S(2)}, u32[]{:S(2)}) %collective-permute-start.14) | collective-permute-done | bytes 262176 | tf_op jit(solution)/shard_map/ppermute | solution.py:415
  56.6 4.7 %collective-permute-done.12.refs_1_ = f32[2,8,32,128]{3,2,1,0:T(8,128)S(1)} collective-permute-done((f32[2,8,32,128]{3,2,1,0:T(8,128)S(1)}, f32[2,8,32,128]{3,2,1,0:T(8,128)S(1)}, u32[]{:S(2)}, u32[]{:S(2)}) %collective-permute-start.12) | collective-permute-done | bytes 262176 | tf_op jit(solution)/shard_map/ppermute | solution.py:415
  61.7 1.6 %shard_map.65 = (f32[2,4,128,128]{3,2,1,0:T(8,128)S(1)}, f32[2,4,128,128]{3,2,1,0:T(8,128)S(1)}) custom-call(f32[2,8,32,128]{3,2,1,0:T(8,128)S(1)} %get-tuple-element.72.refs_0_, f32[2,8,32,128]{3,2,1,0:T(8,128)S(1)} %get-tuple-element.78.refs_1_, f32[2,8,32,128]{3,2,1,0:T(8,128)S(1)} %get-tuple-element.84.refs_2_, ...), custom_call_target="tpu_custom_call" | custom-call | flops 6488064 | bytes 6488064 | tf_op jit(solution)/shard_map/pallas_call | solution.py:98
  63.4 1.9 %collective-permute-done.20.got_ref = f32[2,4,128,128]{3,2,1,0:T(8,128)S(1)} collective-permute-done((f32[2,4,128,128]{3,2,1,0:T(8,128)S(1)}, f32[2,4,128,128]{3,2,1,0:T(8,128)S(1)}, u32[]{:S(2)}, u32[]{:S(2)}) %collective-permute-start.20) | collective-permute-done | bytes 524320 | tf_op jit(solution)/shard_map/ppermute | solution.py:398
  65.6 1.7 %collective-permute-start.21 = (f32[2,4,48,128]{3,2,1,0:T(8,128)S(1)}, f32[2,4,48,128]{3,2,1,0:T(8,128)S(1)}, u32[]{:S(2)}, u32[]{:S(2)}) collective-permute-start(f32[2,4,48,128]{3,2,1,0:T(8,128)S(1)} %get-tuple-element.110), channel_id=1, source_target_pairs={{0,8},{4,12},{8,0},{12,4},{16,24},{20,28},{24,16},{28,20},{1,9},{5... | collective-permute-start | bytes 589832 | tf_op jit(solution)/shard_map/ppermute | solution.py:398
  67.7 5.7 %collective-permute-done.21.got_ref = f32[2,4,48,128]{3,2,1,0:T(8,128)S(1)} collective-permute-done((f32[2,4,48,128]{3,2,1,0:T(8,128)S(1)}, f32[2,4,48,128]{3,2,1,0:T(8,128)S(1)}, u32[]{:S(2)}, u32[]{:S(2)}) %collective-permute-start.21) | collective-permute-done | bytes 196640 | tf_op jit(solution)/shard_map/ppermute | solution.py:398
  73.5 1.7 %collective-permute-start.22 = (f32[2,4,48,128]{3,2,1,0:T(8,128)S(1)}, f32[2,4,48,128]{3,2,1,0:T(8,128)S(1)}, u32[]{:S(2)}, u32[]{:S(2)}) collective-permute-start(f32[2,4,48,128]{3,2,1,0:T(8,128)S(1)} %get-tuple-element.112), channel_id=1, source_target_pairs={{0,16},{4,20},{8,24},{12,28},{16,0},{20,4},{24,8},{28,12},{1,17},{... | collective-permute-start | bytes 589832 | tf_op jit(solution)/shard_map/ppermute | solution.py:398
  75.2 1.5 %collective-permute-done.23.got_ref = f32[2,4,48,128]{3,2,1,0:T(8,128)S(1)} collective-permute-done((f32[2,4,48,128]{3,2,1,0:T(8,128)S(1)}, f32[2,4,48,128]{3,2,1,0:T(8,128)S(1)}, u32[]{:S(2)}, u32[]{:S(2)}) %collective-permute-start.23) | collective-permute-done | bytes 196640 | tf_op jit(solution)/shard_map/ppermute | solution.py:398
  76.9 1.7 %collective-permute-start.24 = (f32[2,4,48,128]{3,2,1,0:T(8,128)S(1)}, f32[2,4,48,128]{3,2,1,0:T(8,128)S(1)}, u32[]{:S(2)}, u32[]{:S(2)}) collective-permute-start(f32[2,4,48,128]{3,2,1,0:T(8,128)S(1)} %get-tuple-element.116), channel_id=1, source_target_pairs={{0,16},{4,20},{8,24},{12,28},{16,0},{20,4},{24,8},{28,12},{1,17},{... | collective-permute-start | bytes 589832 | tf_op jit(solution)/shard_map/ppermute | solution.py:398
  78.6 1.5 %collective-permute-start.25 = (f32[2,4,32,128]{3,2,1,0:T(8,128)S(1)}, f32[2,4,32,128]{3,2,1,0:T(8,128)S(1)}, u32[]{:S(2)}, u32[]{:S(2)}) collective-permute-start(f32[2,4,32,128]{3,2,1,0:T(8,128)S(1)} %get-tuple-element.118), channel_id=1, source_target_pairs={{0,8},{4,12},{8,0},{12,4},{16,24},{20,28},{24,16},{28,20},{1,9},{5... | collective-permute-start | bytes 393224 | tf_op jit(solution)/shard_map/ppermute | solution.py:398
  80.2 2.8 %collective-permute-start.31 = (f32[2,4,48,128]{3,2,1,0:T(8,128)S(1)}, f32[2,4,48,128]{3,2,1,0:T(8,128)S(1)}, u32[]{:S(2)}, u32[]{:S(2)}) collective-permute-start(f32[2,4,48,128]{3,2,1,0:T(8,128)S(1)} %shard_map.68.refs_0_), channel_id=1, source_target_pairs={{0,1},{1,0},{2,3},{3,2},{4,5},{5,4},{6,7},{7,6},{8,9},{9,8},{10,11... | collective-permute-start | bytes 589832 | tf_op jit(solution)/shard_map/ppermute | solution.py:415
  84.3 4.5 %collective-permute-start.29 = (f32[2,4,48,128]{3,2,1,0:T(8,128)S(1)}, f32[2,4,48,128]{3,2,1,0:T(8,128)S(1)}, u32[]{:S(2)}, u32[]{:S(2)}) collective-permute-start(f32[2,4,48,128]{3,2,1,0:T(8,128)S(1)} %shard_map.70.refs_1_), channel_id=1, source_target_pairs={{0,1},{1,0},{2,3},{3,2},{4,5},{5,4},{6,7},{7,6},{8,9},{9,8},{10,11... | collective-permute-start | bytes 589832 | tf_op jit(solution)/shard_map/ppermute | solution.py:415
  88.8 2.7 %collective-permute-start.27 = (f32[2,4,32,128]{3,2,1,0:T(8,128)S(1)}, f32[2,4,32,128]{3,2,1,0:T(8,128)S(1)}, u32[]{:S(2)}, u32[]{:S(2)}) collective-permute-start(f32[2,4,32,128]{3,2,1,0:T(8,128)S(1)} %shard_map.72.refs_2_), channel_id=1, source_target_pairs={{0,1},{1,0},{2,3},{3,2},{4,5},{5,4},{6,7},{7,6},{8,9},{9,8},{10,11... | collective-permute-start | bytes 393224 | tf_op jit(solution)/shard_map/ppermute | solution.py:415
  91.5 1.3 %shard_map.73 = (bf16[4,128,768]{2,1,0:T(8,128)(2,1)S(1)}, bf16[4,128,768]{2,1,0:T(8,128)(2,1)S(1)}, bf16[3,4,256,256]{3,2,1,0:T(8,128)(2,1)S(1)}, bf16[3,4,256,256]{3,2,1,0:T(8,128)(2,1)S(1)}) custom-call(s32[1,2]{1,0:T(1,128)S(1)} %copy-done.4, f32[2,4,1,2,128,128]{5,4,3,2,1,0:T(8,128)S(1)} %copy-done.2), custom_call_target="tpu_custom_call" | custom-call | flops 5767176 | bytes 5767176 | tf_op jit(solution)/shard_map/pallas_call | solution.py:98
  92.8 1.6 %shard_map.74.own_ref = f32[4,128,256]{2,1,0:T(8,128)S(1)} custom-call(f32[2,4,48,128]{3,2,1,0:T(8,128)S(1)} %shard_map.68.refs_0_, f32[2,4,48,128]{3,2,1,0:T(8,128)S(1)} %shard_map.70.refs_1_, f32[2,4,32,128]{3,2,1,0:T(8,128)S(1)} %shard_map.72.refs_2_, bf16[4,128,768]{2,1,0:T(8,128)(2,1)S(1)} %get-tuple-element.121.refs_3_.left_high, ...), custom_call_target="tpu_custom_call" | custom-call | flops 5767168 | bytes 5767168 | tf_op jit(solution)/shard_map/pallas_call | solution.py:98
  96.4 1.4 %shard_map.78 = f32[2,4,1,128,128]{4,3,2,1,0:T(8,128)} custom-call(f32[4,128,256]{2,1,0:T(8,128)S(1)} %shard_map.74.own_ref, bf16[4,128,768]{2,1,0:T(8,128)(2,1)S(1)} %get-tuple-element.121.refs_3_.left_high, bf16[4,128,768]{2,1,0:T(8,128)(2,1)S(1)} %get-tuple-element.122.refs_4_.left_low, bf16[4,512,256]{2,1,0:T(8,128)(2,1)S(1)} %get-tuple-element.129.mid_high, ...), custom_call_target="tpu_custom_call" | custom-call | flops 4718592 | bytes 4718592 | tf_op jit(solution)/shard_map/pallas_call | solution.py:98
  (77 shorter events, 13.6 us)
Async XLA Ops:
  1.3 10.2 %collective-permute-start = (f32[2,2,4,32,128]{4,3,2,1,0:T(8,128)S(1)}, f32[2,2,4,32,128]{4,3,2,1,0:T(8,128)S(1)}, u32[]{:S(2)}, u32[]{:S(2)}) collective-permute-start(f32[2,2,4,32,128]{4,3,2,1,0:T(8,128)S(1)} %shard_map.46.own_ref), channel_id=1, source_target_pairs={{0,16},{4,20},{8,24},{12,28},{16,0},{20,4},{24,8},{28,12},{1,17},{... | collective-permute-start | bytes 786440 | tf_op jit(solution)/shard_map/ppermute | solution.py:398
  4.4 12.7 %collective-permute-start.3 = (f32[2,2,4,32,128]{4,3,2,1,0:T(8,128)S(1)}, f32[2,2,4,32,128]{4,3,2,1,0:T(8,128)S(1)}, u32[]{:S(2)}, u32[]{:S(2)}) collective-permute-start(f32[2,2,4,32,128]{4,3,2,1,0:T(8,128)S(1)} %get-tuple-element.73.own_ref), channel_id=1, source_target_pairs={{0,16},{4,20},{8,24},{12,28},{16,0},{20,4},{24,8},{28,12},{1,17},{... | collective-permute-start | bytes 786440 | tf_op jit(solution)/shard_map/ppermute | solution.py:398
  5.6 17.1 %collective-permute-start.6 = (f32[2,2,4,32,128]{4,3,2,1,0:T(8,128)S(1)}, f32[2,2,4,32,128]{4,3,2,1,0:T(8,128)S(1)}, u32[]{:S(2)}, u32[]{:S(2)}) collective-permute-start(f32[2,2,4,32,128]{4,3,2,1,0:T(8,128)S(1)} %get-tuple-element.79.own_ref), channel_id=1, source_target_pairs={{0,16},{4,20},{8,24},{12,28},{16,0},{20,4},{24,8},{28,12},{1,17},{... | collective-permute-start | bytes 786440 | tf_op jit(solution)/shard_map/ppermute | solution.py:398
  6.5 21.0 %collective-permute-start.9 = (f32[2,2,4,32,128]{4,3,2,1,0:T(8,128)S(1)}, f32[2,2,4,32,128]{4,3,2,1,0:T(8,128)S(1)}, u32[]{:S(2)}, u32[]{:S(2)}) collective-permute-start(f32[2,2,4,32,128]{4,3,2,1,0:T(8,128)S(1)} %get-tuple-element.85.own_ref), channel_id=1, source_target_pairs={{0,16},{4,20},{8,24},{12,28},{16,0},{20,4},{24,8},{28,12},{1,17},{... | collective-permute-start | bytes 786440 | tf_op jit(solution)/shard_map/ppermute | solution.py:398
  11.6 17.8 %collective-permute-start.1 = (f32[2,2,4,32,128]{4,3,2,1,0:T(8,128)S(1)}, f32[2,2,4,32,128]{4,3,2,1,0:T(8,128)S(1)}, u32[]{:S(2)}, u32[]{:S(2)}) collective-permute-start(f32[2,2,4,32,128]{4,3,2,1,0:T(8,128)S(1)} %get-tuple-element.69), channel_id=1, source_target_pairs={{0,8},{4,12},{8,0},{12,4},{16,24},{20,28},{24,16},{28,20},{1,9},{5... | collective-permute-start | bytes 786440 | tf_op jit(solution)/shard_map/ppermute | solution.py:398
  17.2 12.4 %collective-permute-start.4 = (f32[2,2,4,32,128]{4,3,2,1,0:T(8,128)S(1)}, f32[2,2,4,32,128]{4,3,2,1,0:T(8,128)S(1)}, u32[]{:S(2)}, u32[]{:S(2)}) collective-permute-start(f32[2,2,4,32,128]{4,3,2,1,0:T(8,128)S(1)} %get-tuple-element.75), channel_id=1, source_target_pairs={{0,8},{4,12},{8,0},{12,4},{16,24},{20,28},{24,16},{28,20},{1,9},{5... | collective-permute-start | bytes 786440 | tf_op jit(solution)/shard_map/ppermute | solution.py:398
  22.8 7.4 %collective-permute-start.7 = (f32[2,2,4,32,128]{4,3,2,1,0:T(8,128)S(1)}, f32[2,2,4,32,128]{4,3,2,1,0:T(8,128)S(1)}, u32[]{:S(2)}, u32[]{:S(2)}) collective-permute-start(f32[2,2,4,32,128]{4,3,2,1,0:T(8,128)S(1)} %get-tuple-element.81), channel_id=1, source_target_pairs={{0,8},{4,12},{8,0},{12,4},{16,24},{20,28},{24,16},{28,20},{1,9},{5... | collective-permute-start | bytes 786440 | tf_op jit(solution)/shard_map/ppermute | solution.py:398
  27.6 7.5 %collective-permute-start.10 = (f32[2,2,4,32,128]{4,3,2,1,0:T(8,128)S(1)}, f32[2,2,4,32,128]{4,3,2,1,0:T(8,128)S(1)}, u32[]{:S(2)}, u32[]{:S(2)}) collective-permute-start(f32[2,2,4,32,128]{4,3,2,1,0:T(8,128)S(1)} %get-tuple-element.87), channel_id=1, source_target_pairs={{0,8},{4,12},{8,0},{12,4},{16,24},{20,28},{24,16},{28,20},{1,9},{5... | collective-permute-start | bytes 786440 | tf_op jit(solution)/shard_map/ppermute | solution.py:398
  29.5 5.8 %collective-permute-start.2 = (f32[2,2,4,32,128]{4,3,2,1,0:T(8,128)S(1)}, f32[2,2,4,32,128]{4,3,2,1,0:T(8,128)S(1)}, u32[]{:S(2)}, u32[]{:S(2)}) collective-permute-start(f32[2,2,4,32,128]{4,3,2,1,0:T(8,128)S(1)} %get-tuple-element.71), channel_id=1, source_target_pairs={{0,4},{4,0},{8,12},{12,8},{16,20},{20,16},{24,28},{28,24},{1,5},{5... | collective-permute-start | bytes 786440 | tf_op jit(solution)/shard_map/ppermute | solution.py:398
  29.7 8.0 %collective-permute-start.5 = (f32[2,2,4,32,128]{4,3,2,1,0:T(8,128)S(1)}, f32[2,2,4,32,128]{4,3,2,1,0:T(8,128)S(1)}, u32[]{:S(2)}, u32[]{:S(2)}) collective-permute-start(f32[2,2,4,32,128]{4,3,2,1,0:T(8,128)S(1)} %get-tuple-element.77), channel_id=1, source_target_pairs={{0,4},{4,0},{8,12},{12,8},{16,20},{20,16},{24,28},{28,24},{1,5},{5... | collective-permute-start | bytes 786440 | tf_op jit(solution)/shard_map/ppermute | solution.py:398
  30.3 10.6 %collective-permute-start.8 = (f32[2,2,4,32,128]{4,3,2,1,0:T(8,128)S(1)}, f32[2,2,4,32,128]{4,3,2,1,0:T(8,128)S(1)}, u32[]{:S(2)}, u32[]{:S(2)}) collective-permute-start(f32[2,2,4,32,128]{4,3,2,1,0:T(8,128)S(1)} %get-tuple-element.83), channel_id=1, source_target_pairs={{0,4},{4,0},{8,12},{12,8},{16,20},{20,16},{24,28},{28,24},{1,5},{5... | collective-permute-start | bytes 786440 | tf_op jit(solution)/shard_map/ppermute | solution.py:398
  35.2 6.0 %collective-permute-start.11 = (f32[2,2,4,32,128]{4,3,2,1,0:T(8,128)S(1)}, f32[2,2,4,32,128]{4,3,2,1,0:T(8,128)S(1)}, u32[]{:S(2)}, u32[]{:S(2)}) collective-permute-start(f32[2,2,4,32,128]{4,3,2,1,0:T(8,128)S(1)} %get-tuple-element.89), channel_id=1, source_target_pairs={{0,4},{4,0},{8,12},{12,8},{16,20},{20,16},{24,28},{28,24},{1,5},{5... | collective-permute-start | bytes 786440 | tf_op jit(solution)/shard_map/ppermute | solution.py:398
  35.6 9.2 %collective-permute-start.18 = (f32[2,8,32,128]{3,2,1,0:T(8,128)S(1)}, f32[2,8,32,128]{3,2,1,0:T(8,128)S(1)}, u32[]{:S(2)}, u32[]{:S(2)}) collective-permute-start(f32[2,8,32,128]{3,2,1,0:T(8,128)S(1)} %get-tuple-element.98.refs_0_), channel_id=1, source_target_pairs={{0,1},{1,0},{2,3},{3,2},{4,5},{5,4},{6,7},{7,6},{8,9},{9,8},{10,11... | collective-permute-start | bytes 786440 | tf_op jit(solution)/shard_map/ppermute | solution.py:415
  37.5 7.6 %collective-permute-start.19 = (f32[2,8,32,128]{3,2,1,0:T(8,128)S(1)}, f32[2,8,32,128]{3,2,1,0:T(8,128)S(1)}, u32[]{:S(2)}, u32[]{:S(2)}) collective-permute-start(f32[2,8,32,128]{3,2,1,0:T(8,128)S(1)} %get-tuple-element.98.refs_0_), channel_id=1, source_target_pairs={{0,4},{1,2},{2,1},{3,7},{4,0},{5,6},{6,5},{7,3},{8,12},{9,10},{10,... | collective-permute-start | bytes 786440 | tf_op jit(solution)/shard_map/ppermute | solution.py:415
  37.9 12.6 %collective-permute-start.16 = (f32[2,8,32,128]{3,2,1,0:T(8,128)S(1)}, f32[2,8,32,128]{3,2,1,0:T(8,128)S(1)}, u32[]{:S(2)}, u32[]{:S(2)}) collective-permute-start(f32[2,8,32,128]{3,2,1,0:T(8,128)S(1)} %get-tuple-element.97.refs_0_), channel_id=1, source_target_pairs={{0,1},{1,0},{2,3},{3,2},{4,5},{5,4},{6,7},{7,6},{8,9},{9,8},{10,11... | collective-permute-start | bytes 786440 | tf_op jit(solution)/shard_map/ppermute | solution.py:415
  41.0 10.7 %collective-permute-start.17 = (f32[2,8,32,128]{3,2,1,0:T(8,128)S(1)}, f32[2,8,32,128]{3,2,1,0:T(8,128)S(1)}, u32[]{:S(2)}, u32[]{:S(2)}) collective-permute-start(f32[2,8,32,128]{3,2,1,0:T(8,128)S(1)} %get-tuple-element.97.refs_0_), channel_id=1, source_target_pairs={{0,4},{1,2},{2,1},{3,7},{4,0},{5,6},{6,5},{7,3},{8,12},{9,10},{10,... | collective-permute-start | bytes 786440 | tf_op jit(solution)/shard_map/ppermute | solution.py:415
  41.2 14.9 %collective-permute-start.14 = (f32[2,8,32,128]{3,2,1,0:T(8,128)S(1)}, f32[2,8,32,128]{3,2,1,0:T(8,128)S(1)}, u32[]{:S(2)}, u32[]{:S(2)}) collective-permute-start(f32[2,8,32,128]{3,2,1,0:T(8,128)S(1)} %get-tuple-element.96.refs_0_), channel_id=1, source_target_pairs={{0,1},{1,0},{2,3},{3,2},{4,5},{5,4},{6,7},{7,6},{8,9},{9,8},{10,11... | collective-permute-start | bytes 786440 | tf_op jit(solution)/shard_map/ppermute | solution.py:415
  44.9 11.2 %collective-permute-start.15 = (f32[2,8,32,128]{3,2,1,0:T(8,128)S(1)}, f32[2,8,32,128]{3,2,1,0:T(8,128)S(1)}, u32[]{:S(2)}, u32[]{:S(2)}) collective-permute-start(f32[2,8,32,128]{3,2,1,0:T(8,128)S(1)} %get-tuple-element.96.refs_0_), channel_id=1, source_target_pairs={{0,4},{1,2},{2,1},{3,7},{4,0},{5,6},{6,5},{7,3},{8,12},{9,10},{10,... | collective-permute-start | bytes 786440 | tf_op jit(solution)/shard_map/ppermute | solution.py:415
  45.1 16.2 %collective-permute-start.12 = (f32[2,8,32,128]{3,2,1,0:T(8,128)S(1)}, f32[2,8,32,128]{3,2,1,0:T(8,128)S(1)}, u32[]{:S(2)}, u32[]{:S(2)}) collective-permute-start(f32[2,8,32,128]{3,2,1,0:T(8,128)S(1)} %get-tuple-element.93.refs_0_), channel_id=1, source_target_pairs={{0,1},{1,0},{2,3},{3,2},{4,5},{5,4},{6,7},{7,6},{8,9},{9,8},{10,11... | collective-permute-start | bytes 786440 | tf_op jit(solution)/shard_map/ppermute | solution.py:415
  50.5 10.8 %collective-permute-start.13 = (f32[2,8,32,128]{3,2,1,0:T(8,128)S(1)}, f32[2,8,32,128]{3,2,1,0:T(8,128)S(1)}, u32[]{:S(2)}, u32[]{:S(2)}) collective-permute-start(f32[2,8,32,128]{3,2,1,0:T(8,128)S(1)} %get-tuple-element.93.refs_0_), channel_id=1, source_target_pairs={{0,4},{1,2},{2,1},{3,7},{4,0},{5,6},{6,5},{7,3},{8,12},{9,10},{10,... | collective-permute-start | bytes 786440 | tf_op jit(solution)/shard_map/ppermute | solution.py:415
  65.6 7.8 %collective-permute-start.21 = (f32[2,4,48,128]{3,2,1,0:T(8,128)S(1)}, f32[2,4,48,128]{3,2,1,0:T(8,128)S(1)}, u32[]{:S(2)}, u32[]{:S(2)}) collective-permute-start(f32[2,4,48,128]{3,2,1,0:T(8,128)S(1)} %get-tuple-element.110), channel_id=1, source_target_pairs={{0,8},{4,12},{8,0},{12,4},{16,24},{20,28},{24,16},{28,20},{1,9},{5... | collective-permute-start | bytes 589832 | tf_op jit(solution)/shard_map/ppermute | solution.py:398
  67.3 9.5 %collective-permute-start.23 = (f32[2,4,48,128]{3,2,1,0:T(8,128)S(1)}, f32[2,4,48,128]{3,2,1,0:T(8,128)S(1)}, u32[]{:S(2)}, u32[]{:S(2)}) collective-permute-start(f32[2,4,48,128]{3,2,1,0:T(8,128)S(1)} %get-tuple-element.114), channel_id=1, source_target_pairs={{0,8},{4,12},{8,0},{12,4},{16,24},{20,28},{24,16},{28,20},{1,9},{5... | collective-permute-start | bytes 589832 | tf_op jit(solution)/shard_map/ppermute | solution.py:398
  73.5 6.6 %collective-permute-start.22 = (f32[2,4,48,128]{3,2,1,0:T(8,128)S(1)}, f32[2,4,48,128]{3,2,1,0:T(8,128)S(1)}, u32[]{:S(2)}, u32[]{:S(2)}) collective-permute-start(f32[2,4,48,128]{3,2,1,0:T(8,128)S(1)} %get-tuple-element.112), channel_id=1, source_target_pairs={{0,16},{4,20},{8,24},{12,28},{16,0},{20,4},{24,8},{28,12},{1,17},{... | collective-permute-start | bytes 589832 | tf_op jit(solution)/shard_map/ppermute | solution.py:398
  76.9 7.4 %collective-permute-start.24 = (f32[2,4,48,128]{3,2,1,0:T(8,128)S(1)}, f32[2,4,48,128]{3,2,1,0:T(8,128)S(1)}, u32[]{:S(2)}, u32[]{:S(2)}) collective-permute-start(f32[2,4,48,128]{3,2,1,0:T(8,128)S(1)} %get-tuple-element.116), channel_id=1, source_target_pairs={{0,16},{4,20},{8,24},{12,28},{16,0},{20,4},{24,8},{28,12},{1,17},{... | collective-permute-start | bytes 589832 | tf_op jit(solution)/shard_map/ppermute | solution.py:398
  78.6 5.0 %collective-permute-start.25 = (f32[2,4,32,128]{3,2,1,0:T(8,128)S(1)}, f32[2,4,32,128]{3,2,1,0:T(8,128)S(1)}, u32[]{:S(2)}, u32[]{:S(2)}) collective-permute-start(f32[2,4,32,128]{3,2,1,0:T(8,128)S(1)} %get-tuple-element.118), channel_id=1, source_target_pairs={{0,8},{4,12},{8,0},{12,4},{16,24},{20,28},{24,16},{28,20},{1,9},{5... | collective-permute-start | bytes 393224 | tf_op jit(solution)/shard_map/ppermute | solution.py:398
  80.2 11.3 %collective-permute-start.31 = (f32[2,4,48,128]{3,2,1,0:T(8,128)S(1)}, f32[2,4,48,128]{3,2,1,0:T(8,128)S(1)}, u32[]{:S(2)}, u32[]{:S(2)}) collective-permute-start(f32[2,4,48,128]{3,2,1,0:T(8,128)S(1)} %shard_map.68.refs_0_), channel_id=1, source_target_pairs={{0,1},{1,0},{2,3},{3,2},{4,5},{5,4},{6,7},{7,6},{8,9},{9,8},{10,11... | collective-permute-start | bytes 589832 | tf_op jit(solution)/shard_map/ppermute | solution.py:415
  83.7 5.1 %collective-permute-start.26 = (f32[2,4,32,128]{3,2,1,0:T(8,128)S(1)}, f32[2,4,32,128]{3,2,1,0:T(8,128)S(1)}, u32[]{:S(2)}, u32[]{:S(2)}) collective-permute-start(f32[2,4,32,128]{3,2,1,0:T(8,128)S(1)} %get-tuple-element.120), channel_id=1, source_target_pairs={{0,16},{4,20},{8,24},{12,28},{16,0},{20,4},{24,8},{28,12},{1,17},{... | collective-permute-start | bytes 393224 | tf_op jit(solution)/shard_map/ppermute | solution.py:398
  84.3 10.1 %collective-permute-start.32 = (f32[2,4,48,128]{3,2,1,0:T(8,128)S(1)}, f32[2,4,48,128]{3,2,1,0:T(8,128)S(1)}, u32[]{:S(2)}, u32[]{:S(2)}) collective-permute-start(f32[2,4,48,128]{3,2,1,0:T(8,128)S(1)} %shard_map.68.refs_0_), channel_id=1, source_target_pairs={{0,4},{1,2},{2,1},{3,7},{4,0},{5,6},{6,5},{7,3},{8,12},{9,10},{10,... | collective-permute-start | bytes 589832 | tf_op jit(solution)/shard_map/ppermute | solution.py:415
  84.3 10.8 %collective-permute-start.29 = (f32[2,4,48,128]{3,2,1,0:T(8,128)S(1)}, f32[2,4,48,128]{3,2,1,0:T(8,128)S(1)}, u32[]{:S(2)}, u32[]{:S(2)}) collective-permute-start(f32[2,4,48,128]{3,2,1,0:T(8,128)S(1)} %shard_map.70.refs_1_), channel_id=1, source_target_pairs={{0,1},{1,0},{2,3},{3,2},{4,5},{5,4},{6,7},{7,6},{8,9},{9,8},{10,11... | collective-permute-start | bytes 589832 | tf_op jit(solution)/shard_map/ppermute | solution.py:415
  88.8 6.3 %collective-permute-start.30 = (f32[2,4,48,128]{3,2,1,0:T(8,128)S(1)}, f32[2,4,48,128]{3,2,1,0:T(8,128)S(1)}, u32[]{:S(2)}, u32[]{:S(2)}) collective-permute-start(f32[2,4,48,128]{3,2,1,0:T(8,128)S(1)} %shard_map.70.refs_1_), channel_id=1, source_target_pairs={{0,4},{1,2},{2,1},{3,7},{4,0},{5,6},{6,5},{7,3},{8,12},{9,10},{10,... | collective-permute-start | bytes 589832 | tf_op jit(solution)/shard_map/ppermute | solution.py:415
  88.8 6.9 %collective-permute-start.27 = (f32[2,4,32,128]{3,2,1,0:T(8,128)S(1)}, f32[2,4,32,128]{3,2,1,0:T(8,128)S(1)}, u32[]{:S(2)}, u32[]{:S(2)}) collective-permute-start(f32[2,4,32,128]{3,2,1,0:T(8,128)S(1)} %shard_map.72.refs_2_), channel_id=1, source_target_pairs={{0,1},{1,0},{2,3},{3,2},{4,5},{5,4},{6,7},{7,6},{8,9},{9,8},{10,11... | collective-permute-start | bytes 393224 | tf_op jit(solution)/shard_map/ppermute | solution.py:415
  91.5 4.3 %collective-permute-start.28 = (f32[2,4,32,128]{3,2,1,0:T(8,128)S(1)}, f32[2,4,32,128]{3,2,1,0:T(8,128)S(1)}, u32[]{:S(2)}, u32[]{:S(2)}) collective-permute-start(f32[2,4,32,128]{3,2,1,0:T(8,128)S(1)} %shard_map.72.refs_2_), channel_id=1, source_target_pairs={{0,4},{1,2},{2,1},{3,7},{4,0},{5,6},{6,5},{7,3},{8,12},{9,10},{10,... | collective-permute-start | bytes 393224 | tf_op jit(solution)/shard_map/ppermute | solution.py:415
  (6 other events, 72.8 us)

commit v5 on v4

--- a/solution.py
+++ b/solution.py
@@ -417,7 +417,10 @@
 
     sizes = heights(order, FORWARD)
     starts = starts_of(sizes)
-    keep = [*cut(green_pair, starts[:1], sizes[:1]), *cut(green_pair, starts[1:], sizes[1:])]
+    keep = [
+        lax.slice_in_dim(green_pair[:, :, :, 0], 0, sizes[0], axis=3),
+        *cut(green_pair, starts[1:], sizes[1:]),
+    ]
     got = [swap(own, bits - 1) for own in keep]
     coulomb_shapes = [(order, 3 * order)] * 2 + [(3, order, order)] * 2
     coulombs = call(

time: 98.6 us -> 98.3 us (level)
  starting transfers between devices: 41.9 us -> 40.9 us
    ppermute x19, starting transfers between devices: 22.8 us -> 21.7 us  [swap(): lax.ppermute(value, 'wide', [(i, i ^ 1 << bit) for i in range(peers)])]
where the time goes in v5:
time: 98.3 us; the launch traced here: 97.5 us
  waiting for transfers between devices  41.3 us (42%)
  starting transfers between devices  40.9 us (42%)
  Pallas kernels  12.7 us (13%)
  local copies, waits for them, and re-layouts  2.21 us (2%)
    ppermute x19, waiting for transfers between devices, swap(): lax.ppermute(value, 'wide', [(i, i ^ 1 << bit) for i in range(peers)])  27.8 us
    ppermute x19, starting transfers between devices, swap(): lax.ppermute(value, 'wide', [(i, i ^ 1 << bit) for i in range(peers)])  21.7 us
    ppermute x14, starting transfers between devices, beside(): blocks.append(lax.ppermute(value, ('wide', 'cell'), pairs))  19.2 us
    ppermute x14, waiting for transfers between devices, beside(): blocks.append(lax.ppermute(value, ('wide', 'cell'), pairs))  13.5 us
    pallas_call x31, Pallas kernels, call(): pl.pallas_call(kernel, out_shape=outs, in_specs=specs, out_specs=[pl.Bloc...  12.6 us
  transfers between devices with their start and end apart: 33, of which 13 were waited for; matrix products, arithmetic and copies ran while one was open for 0% of the time, Pallas kernels for 9%

profile of v5, /device:TPU:0, one launch (start us, length us, event | category | flops | bytes accessed | tf_op | source)
XLA Modules:
  0.0 97.5 jit_solution(5728649624981550718)
XLA Ops:
  1.0 3.1 %collective-permute-start = (f32[2,2,4,32,128]{4,3,2,1,0:T(8,128)S(1)}, f32[2,2,4,32,128]{4,3,2,1,0:T(8,128)S(1)}, u32[]{:S(2)}, u32[]{:S(2)}) collective-permute-start(f32[2,2,4,32,128]{4,3,2,1,0:T(8,128)S(1)} %slice.4.own_ref), channel_id=1, source_target_pairs={{0,16},{4,20},{8,24},{12,28},{16,0},{20,4},{24,8},{28,12},{1,17},{... | collective-permute-start | bytes 786440 | tf_op jit(solution)/shard_map/ppermute | solution.py:398
  5.4 2.0 %collective-permute-start.6 = (f32[2,2,4,32,128]{4,3,2,1,0:T(8,128)S(1)}, f32[2,2,4,32,128]{4,3,2,1,0:T(8,128)S(1)}, u32[]{:S(2)}, u32[]{:S(2)}) collective-permute-start(f32[2,2,4,32,128]{4,3,2,1,0:T(8,128)S(1)} %get-tuple-element.79.own_ref), channel_id=1, source_target_pairs={{0,16},{4,20},{8,24},{12,28},{16,0},{20,4},{24,8},{28,12},{1,17},{... | collective-permute-start | bytes 786440 | tf_op jit(solution)/shard_map/ppermute | solution.py:398
  7.5 3.7 %collective-permute-done.got_ref = f32[2,2,4,32,128]{4,3,2,1,0:T(8,128)S(1)} collective-permute-done((f32[2,2,4,32,128]{4,3,2,1,0:T(8,128)S(1)}, f32[2,2,4,32,128]{4,3,2,1,0:T(8,128)S(1)}, u32[]{:S(2)}, u32[]{:S(2)}) %collective-permute-start) | collective-permute-done | bytes 262176 | tf_op jit(solution)/shard_map/ppermute | solution.py:398
  11.3 2.1 %collective-permute-start.1 = (f32[2,2,4,32,128]{4,3,2,1,0:T(8,128)S(1)}, f32[2,2,4,32,128]{4,3,2,1,0:T(8,128)S(1)}, u32[]{:S(2)}, u32[]{:S(2)}) collective-permute-start(f32[2,2,4,32,128]{4,3,2,1,0:T(8,128)S(1)} %get-tuple-element.69), channel_id=1, source_target_pairs={{0,8},{4,12},{8,0},{12,4},{16,24},{20,28},{24,16},{28,20},{1,9},{5... | collective-permute-start | bytes 786440 | tf_op jit(solution)/shard_map/ppermute | solution.py:398
  13.4 3.5 %collective-permute-done.3.got_ref = f32[2,2,4,32,128]{4,3,2,1,0:T(8,128)S(1)} collective-permute-done((f32[2,2,4,32,128]{4,3,2,1,0:T(8,128)S(1)}, f32[2,2,4,32,128]{4,3,2,1,0:T(8,128)S(1)}, u32[]{:S(2)}, u32[]{:S(2)}) %collective-permute-start.3) | collective-permute-done | bytes 262176 | tf_op jit(solution)/shard_map/ppermute | solution.py:398
  16.9 2.1 %collective-permute-start.4 = (f32[2,2,4,32,128]{4,3,2,1,0:T(8,128)S(1)}, f32[2,2,4,32,128]{4,3,2,1,0:T(8,128)S(1)}, u32[]{:S(2)}, u32[]{:S(2)}) collective-permute-start(f32[2,2,4,32,128]{4,3,2,1,0:T(8,128)S(1)} %get-tuple-element.75), channel_id=1, source_target_pairs={{0,8},{4,12},{8,0},{12,4},{16,24},{20,28},{24,16},{28,20},{1,9},{5... | collective-permute-start | bytes 786440 | tf_op jit(solution)/shard_map/ppermute | solution.py:398
  19.0 3.5 %collective-permute-done.6.got_ref = f32[2,2,4,32,128]{4,3,2,1,0:T(8,128)S(1)} collective-permute-done((f32[2,2,4,32,128]{4,3,2,1,0:T(8,128)S(1)}, f32[2,2,4,32,128]{4,3,2,1,0:T(8,128)S(1)}, u32[]{:S(2)}, u32[]{:S(2)}) %collective-permute-start.6) | collective-permute-done | bytes 262176 | tf_op jit(solution)/shard_map/ppermute | solution.py:398
  22.5 2.1 %collective-permute-start.7 = (f32[2,2,4,32,128]{4,3,2,1,0:T(8,128)S(1)}, f32[2,2,4,32,128]{4,3,2,1,0:T(8,128)S(1)}, u32[]{:S(2)}, u32[]{:S(2)}) collective-permute-start(f32[2,2,4,32,128]{4,3,2,1,0:T(8,128)S(1)} %get-tuple-element.81), channel_id=1, source_target_pairs={{0,8},{4,12},{8,0},{12,4},{16,24},{20,28},{24,16},{28,20},{1,9},{5... | collective-permute-start | bytes 786440 | tf_op jit(solution)/shard_map/ppermute | solution.py:398
  24.6 2.6 %collective-permute-done.9.got_ref = f32[2,2,4,32,128]{4,3,2,1,0:T(8,128)S(1)} collective-permute-done((f32[2,2,4,32,128]{4,3,2,1,0:T(8,128)S(1)}, f32[2,2,4,32,128]{4,3,2,1,0:T(8,128)S(1)}, u32[]{:S(2)}, u32[]{:S(2)}) %collective-permute-start.9) | collective-permute-done | bytes 262176 | tf_op jit(solution)/shard_map/ppermute | solution.py:398
  27.3 1.8 %collective-permute-start.10 = (f32[2,2,4,32,128]{4,3,2,1,0:T(8,128)S(1)}, f32[2,2,4,32,128]{4,3,2,1,0:T(8,128)S(1)}, u32[]{:S(2)}, u32[]{:S(2)}) collective-permute-start(f32[2,2,4,32,128]{4,3,2,1,0:T(8,128)S(1)} %get-tuple-element.87), channel_id=1, source_target_pairs={{0,8},{4,12},{8,0},{12,4},{16,24},{20,28},{24,16},{28,20},{1,9},{5... | collective-permute-start | bytes 786440 | tf_op jit(solution)/shard_map/ppermute | solution.py:398
  30.1 4.7 %collective-permute-done.10.got_ref = f32[2,2,4,32,128]{4,3,2,1,0:T(8,128)S(1)} collective-permute-done((f32[2,2,4,32,128]{4,3,2,1,0:T(8,128)S(1)}, f32[2,2,4,32,128]{4,3,2,1,0:T(8,128)S(1)}, u32[]{:S(2)}, u32[]{:S(2)}) %collective-permute-start.10) | collective-permute-done | bytes 262176 | tf_op jit(solution)/shard_map/ppermute | solution.py:398
  35.3 1.9 %collective-permute-start.18 = (f32[2,8,32,128]{3,2,1,0:T(8,128)S(1)}, f32[2,8,32,128]{3,2,1,0:T(8,128)S(1)}, u32[]{:S(2)}, u32[]{:S(2)}) collective-permute-start(f32[2,8,32,128]{3,2,1,0:T(8,128)S(1)} %get-tuple-element.98.refs_0_), channel_id=1, source_target_pairs={{0,1},{1,0},{2,3},{3,2},{4,5},{5,4},{6,7},{7,6},{8,9},{9,8},{10,11... | collective-permute-start | bytes 786440 | tf_op jit(solution)/shard_map/ppermute | solution.py:415
  37.6 3.1 %collective-permute-start.16 = (f32[2,8,32,128]{3,2,1,0:T(8,128)S(1)}, f32[2,8,32,128]{3,2,1,0:T(8,128)S(1)}, u32[]{:S(2)}, u32[]{:S(2)}) collective-permute-start(f32[2,8,32,128]{3,2,1,0:T(8,128)S(1)} %get-tuple-element.97.refs_0_), channel_id=1, source_target_pairs={{0,1},{1,0},{2,3},{3,2},{4,5},{5,4},{6,7},{7,6},{8,9},{9,8},{10,11... | collective-permute-start | bytes 786440 | tf_op jit(solution)/shard_map/ppermute | solution.py:415
  41.6 3.0 %collective-permute-done.18.refs_1_ = f32[2,8,32,128]{3,2,1,0:T(8,128)S(1)} collective-permute-done((f32[2,8,32,128]{3,2,1,0:T(8,128)S(1)}, f32[2,8,32,128]{3,2,1,0:T(8,128)S(1)}, u32[]{:S(2)}, u32[]{:S(2)}) %collective-permute-start.18) | collective-permute-done | bytes 262176 | tf_op jit(solution)/shard_map/ppermute | solution.py:415
  44.8 3.5 %collective-permute-start.12 = (f32[2,8,32,128]{3,2,1,0:T(8,128)S(1)}, f32[2,8,32,128]{3,2,1,0:T(8,128)S(1)}, u32[]{:S(2)}, u32[]{:S(2)}) collective-permute-start(f32[2,8,32,128]{3,2,1,0:T(8,128)S(1)} %get-tuple-element.93.refs_0_), channel_id=1, source_target_pairs={{0,1},{1,0},{2,3},{3,2},{4,5},{5,4},{6,7},{7,6},{8,9},{9,8},{10,11... | collective-permute-start | bytes 786440 | tf_op jit(solution)/shard_map/ppermute | solution.py:415
  48.3 1.9 %collective-permute-done.16.refs_1_ = f32[2,8,32,128]{3,2,1,0:T(8,128)S(1)} collective-permute-done((f32[2,8,32,128]{3,2,1,0:T(8,128)S(1)}, f32[2,8,32,128]{3,2,1,0:T(8,128)S(1)}, u32[]{:S(2)}, u32[]{:S(2)}) %collective-permute-start.16) | collective-permute-done | bytes 262176 | tf_op jit(solution)/shard_map/ppermute | solution.py:415
  51.9 3.9 %collective-permute-done.14.refs_1_ = f32[2,8,32,128]{3,2,1,0:T(8,128)S(1)} collective-permute-done((f32[2,8,32,128]{3,2,1,0:T(8,128)S(1)}, f32[2,8,32,128]{3,2,1,0:T(8,128)S(1)}, u32[]{:S(2)}, u32[]{:S(2)}) %collective-permute-start.14) | collective-permute-done | bytes 262176 | tf_op jit(solution)/shard_map/ppermute | solution.py:415
  56.3 4.7 %collective-permute-done.12.refs_1_ = f32[2,8,32,128]{3,2,1,0:T(8,128)S(1)} collective-permute-done((f32[2,8,32,128]{3,2,1,0:T(8,128)S(1)}, f32[2,8,32,128]{3,2,1,0:T(8,128)S(1)}, u32[]{:S(2)}, u32[]{:S(2)}) %collective-permute-start.12) | collective-permute-done | bytes 262176 | tf_op jit(solution)/shard_map/ppermute | solution.py:415
  61.4 1.6 %shard_map.64 = (f32[2,4,128,128]{3,2,1,0:T(8,128)S(1)}, f32[2,4,128,128]{3,2,1,0:T(8,128)S(1)}) custom-call(f32[2,8,32,128]{3,2,1,0:T(8,128)S(1)} %get-tuple-element.72.refs_0_, f32[2,8,32,128]{3,2,1,0:T(8,128)S(1)} %get-tuple-element.78.refs_1_, f32[2,8,32,128]{3,2,1,0:T(8,128)S(1)} %get-tuple-element.84.refs_2_, ...), custom_call_target="tpu_custom_call" | custom-call | flops 6488064 | bytes 6488064 | tf_op jit(solution)/shard_map/pallas_call | solution.py:98
  63.1 1.9 %collective-permute-done.20.got_ref = f32[2,4,128,128]{3,2,1,0:T(8,128)S(1)} collective-permute-done((f32[2,4,128,128]{3,2,1,0:T(8,128)S(1)}, f32[2,4,128,128]{3,2,1,0:T(8,128)S(1)}, u32[]{:S(2)}, u32[]{:S(2)}) %collective-permute-start.20) | collective-permute-done | bytes 524320 | tf_op jit(solution)/shard_map/ppermute | solution.py:398
  65.3 1.7 %collective-permute-start.21 = (f32[2,4,48,128]{3,2,1,0:T(8,128)S(1)}, f32[2,4,48,128]{3,2,1,0:T(8,128)S(1)}, u32[]{:S(2)}, u32[]{:S(2)}) collective-permute-start(f32[2,4,48,128]{3,2,1,0:T(8,128)S(1)} %get-tuple-element.110), channel_id=1, source_target_pairs={{0,8},{4,12},{8,0},{12,4},{16,24},{20,28},{24,16},{28,20},{1,9},{5... | collective-permute-start | bytes 589832 | tf_op jit(solution)/shard_map/ppermute | solution.py:398
  67.4 5.7 %collective-permute-done.21.got_ref = f32[2,4,48,128]{3,2,1,0:T(8,128)S(1)} collective-permute-done((f32[2,4,48,128]{3,2,1,0:T(8,128)S(1)}, f32[2,4,48,128]{3,2,1,0:T(8,128)S(1)}, u32[]{:S(2)}, u32[]{:S(2)}) %collective-permute-start.21) | collective-permute-done | bytes 196640 | tf_op jit(solution)/shard_map/ppermute | solution.py:398
  73.2 1.7 %collective-permute-start.22 = (f32[2,4,48,128]{3,2,1,0:T(8,128)S(1)}, f32[2,4,48,128]{3,2,1,0:T(8,128)S(1)}, u32[]{:S(2)}, u32[]{:S(2)}) collective-permute-start(f32[2,4,48,128]{3,2,1,0:T(8,128)S(1)} %get-tuple-element.112), channel_id=1, source_target_pairs={{0,16},{4,20},{8,24},{12,28},{16,0},{20,4},{24,8},{28,12},{1,17},{... | collective-permute-start | bytes 589832 | tf_op jit(solution)/shard_map/ppermute | solution.py:398
  74.9 1.5 %collective-permute-done.23.got_ref = f32[2,4,48,128]{3,2,1,0:T(8,128)S(1)} collective-permute-done((f32[2,4,48,128]{3,2,1,0:T(8,128)S(1)}, f32[2,4,48,128]{3,2,1,0:T(8,128)S(1)}, u32[]{:S(2)}, u32[]{:S(2)}) %collective-permute-start.23) | collective-permute-done | bytes 196640 | tf_op jit(solution)/shard_map/ppermute | solution.py:398
  76.6 1.7 %collective-permute-start.24 = (f32[2,4,48,128]{3,2,1,0:T(8,128)S(1)}, f32[2,4,48,128]{3,2,1,0:T(8,128)S(1)}, u32[]{:S(2)}, u32[]{:S(2)}) collective-permute-start(f32[2,4,48,128]{3,2,1,0:T(8,128)S(1)} %get-tuple-element.116), channel_id=1, source_target_pairs={{0,16},{4,20},{8,24},{12,28},{16,0},{20,4},{24,8},{28,12},{1,17},{... | collective-permute-start | bytes 589832 | tf_op jit(solution)/shard_map/ppermute | solution.py:398
  78.3 1.5 %collective-permute-start.25 = (f32[2,4,32,128]{3,2,1,0:T(8,128)S(1)}, f32[2,4,32,128]{3,2,1,0:T(8,128)S(1)}, u32[]{:S(2)}, u32[]{:S(2)}) collective-permute-start(f32[2,4,32,128]{3,2,1,0:T(8,128)S(1)} %get-tuple-element.118), channel_id=1, source_target_pairs={{0,8},{4,12},{8,0},{12,4},{16,24},{20,28},{24,16},{28,20},{1,9},{5... | collective-permute-start | bytes 393224 | tf_op jit(solution)/shard_map/ppermute | solution.py:398
  79.8 2.8 %collective-permute-start.31 = (f32[2,4,48,128]{3,2,1,0:T(8,128)S(1)}, f32[2,4,48,128]{3,2,1,0:T(8,128)S(1)}, u32[]{:S(2)}, u32[]{:S(2)}) collective-permute-start(f32[2,4,48,128]{3,2,1,0:T(8,128)S(1)} %shard_map.67.refs_0_), channel_id=1, source_target_pairs={{0,1},{1,0},{2,3},{3,2},{4,5},{5,4},{6,7},{7,6},{8,9},{9,8},{10,11... | collective-permute-start | bytes 589832 | tf_op jit(solution)/shard_map/ppermute | solution.py:415
  84.0 4.5 %collective-permute-start.29 = (f32[2,4,48,128]{3,2,1,0:T(8,128)S(1)}, f32[2,4,48,128]{3,2,1,0:T(8,128)S(1)}, u32[]{:S(2)}, u32[]{:S(2)}) collective-permute-start(f32[2,4,48,128]{3,2,1,0:T(8,128)S(1)} %shard_map.69.refs_1_), channel_id=1, source_target_pairs={{0,1},{1,0},{2,3},{3,2},{4,5},{5,4},{6,7},{7,6},{8,9},{9,8},{10,11... | collective-permute-start | bytes 589832 | tf_op jit(solution)/shard_map/ppermute | solution.py:415
  88.5 2.7 %collective-permute-start.27 = (f32[2,4,32,128]{3,2,1,0:T(8,128)S(1)}, f32[2,4,32,128]{3,2,1,0:T(8,128)S(1)}, u32[]{:S(2)}, u32[]{:S(2)}) collective-permute-start(f32[2,4,32,128]{3,2,1,0:T(8,128)S(1)} %shard_map.71.refs_2_), channel_id=1, source_target_pairs={{0,1},{1,0},{2,3},{3,2},{4,5},{5,4},{6,7},{7,6},{8,9},{9,8},{10,11... | collective-permute-start | bytes 393224 | tf_op jit(solution)/shard_map/ppermute | solution.py:415
  91.2 1.3 %shard_map.72 = (bf16[4,128,768]{2,1,0:T(8,128)(2,1)S(1)}, bf16[4,128,768]{2,1,0:T(8,128)(2,1)S(1)}, bf16[3,4,256,256]{3,2,1,0:T(8,128)(2,1)S(1)}, bf16[3,4,256,256]{3,2,1,0:T(8,128)(2,1)S(1)}) custom-call(s32[1,2]{1,0:T(1,128)S(1)} %copy-done.3, f32[2,4,1,2,128,128]{5,4,3,2,1,0:T(8,128)S(1)} %copy-done.1), custom_call_target="tpu_custom_call" | custom-call | flops 5767176 | bytes 5767176 | tf_op jit(solution)/shard_map/pallas_call | solution.py:98
  92.5 1.6 %shard_map.73.own_ref = f32[4,128,256]{2,1,0:T(8,128)S(1)} custom-call(f32[2,4,48,128]{3,2,1,0:T(8,128)S(1)} %shard_map.67.refs_0_, f32[2,4,48,128]{3,2,1,0:T(8,128)S(1)} %shard_map.69.refs_1_, f32[2,4,32,128]{3,2,1,0:T(8,128)S(1)} %shard_map.71.refs_2_, bf16[4,128,768]{2,1,0:T(8,128)(2,1)S(1)} %get-tuple-element.121.refs_3_.left_high, ...), custom_call_target="tpu_custom_call" | custom-call | flops 5767168 | bytes 5767168 | tf_op jit(solution)/shard_map/pallas_call | solution.py:98
  96.1 1.4 %shard_map.77 = f32[2,4,1,128,128]{4,3,2,1,0:T(8,128)} custom-call(f32[4,128,256]{2,1,0:T(8,128)S(1)} %shard_map.73.own_ref, bf16[4,128,768]{2,1,0:T(8,128)(2,1)S(1)} %get-tuple-element.121.refs_3_.left_high, bf16[4,128,768]{2,1,0:T(8,128)(2,1)S(1)} %get-tuple-element.122.refs_4_.left_low, bf16[4,512,256]{2,1,0:T(8,128)(2,1)S(1)} %get-tuple-element.129.mid_high, ...), custom_call_target="tpu_custom_call" | custom-call | flops 4718592 | bytes 4718592 | tf_op jit(solution)/shard_map/pallas_call | solution.py:98
  (75 shorter events, 12.7 us)
Async XLA Ops:
  1.0 10.2 %collective-permute-start = (f32[2,2,4,32,128]{4,3,2,1,0:T(8,128)S(1)}, f32[2,2,4,32,128]{4,3,2,1,0:T(8,128)S(1)}, u32[]{:S(2)}, u32[]{:S(2)}) collective-permute-start(f32[2,2,4,32,128]{4,3,2,1,0:T(8,128)S(1)} %slice.4.own_ref), channel_id=1, source_target_pairs={{0,16},{4,20},{8,24},{12,28},{16,0},{20,4},{24,8},{28,12},{1,17},{... | collective-permute-start | bytes 786440 | tf_op jit(solution)/shard_map/ppermute | solution.py:398
  5.4 11.5 %collective-permute-start.3 = (f32[2,2,4,32,128]{4,3,2,1,0:T(8,128)S(1)}, f32[2,2,4,32,128]{4,3,2,1,0:T(8,128)S(1)}, u32[]{:S(2)}, u32[]{:S(2)}) collective-permute-start(f32[2,2,4,32,128]{4,3,2,1,0:T(8,128)S(1)} %get-tuple-element.73.own_ref), channel_id=1, source_target_pairs={{0,16},{4,20},{8,24},{12,28},{16,0},{20,4},{24,8},{28,12},{1,17},{... | collective-permute-start | bytes 786440 | tf_op jit(solution)/shard_map/ppermute | solution.py:398
  5.4 17.0 %collective-permute-start.6 = (f32[2,2,4,32,128]{4,3,2,1,0:T(8,128)S(1)}, f32[2,2,4,32,128]{4,3,2,1,0:T(8,128)S(1)}, u32[]{:S(2)}, u32[]{:S(2)}) collective-permute-start(f32[2,2,4,32,128]{4,3,2,1,0:T(8,128)S(1)} %get-tuple-element.79.own_ref), channel_id=1, source_target_pairs={{0,16},{4,20},{8,24},{12,28},{16,0},{20,4},{24,8},{28,12},{1,17},{... | collective-permute-start | bytes 786440 | tf_op jit(solution)/shard_map/ppermute | solution.py:398
  7.4 19.7 %collective-permute-start.9 = (f32[2,2,4,32,128]{4,3,2,1,0:T(8,128)S(1)}, f32[2,2,4,32,128]{4,3,2,1,0:T(8,128)S(1)}, u32[]{:S(2)}, u32[]{:S(2)}) collective-permute-start(f32[2,2,4,32,128]{4,3,2,1,0:T(8,128)S(1)} %get-tuple-element.85.own_ref), channel_id=1, source_target_pairs={{0,16},{4,20},{8,24},{12,28},{16,0},{20,4},{24,8},{28,12},{1,17},{... | collective-permute-start | bytes 786440 | tf_op jit(solution)/shard_map/ppermute | solution.py:398
  11.3 17.8 %collective-permute-start.1 = (f32[2,2,4,32,128]{4,3,2,1,0:T(8,128)S(1)}, f32[2,2,4,32,128]{4,3,2,1,0:T(8,128)S(1)}, u32[]{:S(2)}, u32[]{:S(2)}) collective-permute-start(f32[2,2,4,32,128]{4,3,2,1,0:T(8,128)S(1)} %get-tuple-element.69), channel_id=1, source_target_pairs={{0,8},{4,12},{8,0},{12,4},{16,24},{20,28},{24,16},{28,20},{1,9},{5... | collective-permute-start | bytes 786440 | tf_op jit(solution)/shard_map/ppermute | solution.py:398
  16.9 12.3 %collective-permute-start.4 = (f32[2,2,4,32,128]{4,3,2,1,0:T(8,128)S(1)}, f32[2,2,4,32,128]{4,3,2,1,0:T(8,128)S(1)}, u32[]{:S(2)}, u32[]{:S(2)}) collective-permute-start(f32[2,2,4,32,128]{4,3,2,1,0:T(8,128)S(1)} %get-tuple-element.75), channel_id=1, source_target_pairs={{0,8},{4,12},{8,0},{12,4},{16,24},{20,28},{24,16},{28,20},{1,9},{5... | collective-permute-start | bytes 786440 | tf_op jit(solution)/shard_map/ppermute | solution.py:398
  22.5 7.4 %collective-permute-start.7 = (f32[2,2,4,32,128]{4,3,2,1,0:T(8,128)S(1)}, f32[2,2,4,32,128]{4,3,2,1,0:T(8,128)S(1)}, u32[]{:S(2)}, u32[]{:S(2)}) collective-permute-start(f32[2,2,4,32,128]{4,3,2,1,0:T(8,128)S(1)} %get-tuple-element.81), channel_id=1, source_target_pairs={{0,8},{4,12},{8,0},{12,4},{16,24},{20,28},{24,16},{28,20},{1,9},{5... | collective-permute-start | bytes 786440 | tf_op jit(solution)/shard_map/ppermute | solution.py:398
  27.3 7.5 %collective-permute-start.10 = (f32[2,2,4,32,128]{4,3,2,1,0:T(8,128)S(1)}, f32[2,2,4,32,128]{4,3,2,1,0:T(8,128)S(1)}, u32[]{:S(2)}, u32[]{:S(2)}) collective-permute-start(f32[2,2,4,32,128]{4,3,2,1,0:T(8,128)S(1)} %get-tuple-element.87), channel_id=1, source_target_pairs={{0,8},{4,12},{8,0},{12,4},{16,24},{20,28},{24,16},{28,20},{1,9},{5... | collective-permute-start | bytes 786440 | tf_op jit(solution)/shard_map/ppermute | solution.py:398
  29.2 5.8 %collective-permute-start.2 = (f32[2,2,4,32,128]{4,3,2,1,0:T(8,128)S(1)}, f32[2,2,4,32,128]{4,3,2,1,0:T(8,128)S(1)}, u32[]{:S(2)}, u32[]{:S(2)}) collective-permute-start(f32[2,2,4,32,128]{4,3,2,1,0:T(8,128)S(1)} %get-tuple-element.71), channel_id=1, source_target_pairs={{0,4},{4,0},{8,12},{12,8},{16,20},{20,16},{24,28},{28,24},{1,5},{5... | collective-permute-start | bytes 786440 | tf_op jit(solution)/shard_map/ppermute | solution.py:398
  29.4 8.0 %collective-permute-start.5 = (f32[2,2,4,32,128]{4,3,2,1,0:T(8,128)S(1)}, f32[2,2,4,32,128]{4,3,2,1,0:T(8,128)S(1)}, u32[]{:S(2)}, u32[]{:S(2)}) collective-permute-start(f32[2,2,4,32,128]{4,3,2,1,0:T(8,128)S(1)} %get-tuple-element.77), channel_id=1, source_target_pairs={{0,4},{4,0},{8,12},{12,8},{16,20},{20,16},{24,28},{28,24},{1,5},{5... | collective-permute-start | bytes 786440 | tf_op jit(solution)/shard_map/ppermute | solution.py:398
  30.0 10.7 %collective-permute-start.8 = (f32[2,2,4,32,128]{4,3,2,1,0:T(8,128)S(1)}, f32[2,2,4,32,128]{4,3,2,1,0:T(8,128)S(1)}, u32[]{:S(2)}, u32[]{:S(2)}) collective-permute-start(f32[2,2,4,32,128]{4,3,2,1,0:T(8,128)S(1)} %get-tuple-element.83), channel_id=1, source_target_pairs={{0,4},{4,0},{8,12},{12,8},{16,20},{20,16},{24,28},{28,24},{1,5},{5... | collective-permute-start | bytes 786440 | tf_op jit(solution)/shard_map/ppermute | solution.py:398
  34.9 6.0 %collective-permute-start.11 = (f32[2,2,4,32,128]{4,3,2,1,0:T(8,128)S(1)}, f32[2,2,4,32,128]{4,3,2,1,0:T(8,128)S(1)}, u32[]{:S(2)}, u32[]{:S(2)}) collective-permute-start(f32[2,2,4,32,128]{4,3,2,1,0:T(8,128)S(1)} %get-tuple-element.89), channel_id=1, source_target_pairs={{0,4},{4,0},{8,12},{12,8},{16,20},{20,16},{24,28},{28,24},{1,5},{5... | collective-permute-start | bytes 786440 | tf_op jit(solution)/shard_map/ppermute | solution.py:398
  35.3 9.2 %collective-permute-start.18 = (f32[2,8,32,128]{3,2,1,0:T(8,128)S(1)}, f32[2,8,32,128]{3,2,1,0:T(8,128)S(1)}, u32[]{:S(2)}, u32[]{:S(2)}) collective-permute-start(f32[2,8,32,128]{3,2,1,0:T(8,128)S(1)} %get-tuple-element.98.refs_0_), channel_id=1, source_target_pairs={{0,1},{1,0},{2,3},{3,2},{4,5},{5,4},{6,7},{7,6},{8,9},{9,8},{10,11... | collective-permute-start | bytes 786440 | tf_op jit(solution)/shard_map/ppermute | solution.py:415
  37.2 7.6 %collective-permute-start.19 = (f32[2,8,32,128]{3,2,1,0:T(8,128)S(1)}, f32[2,8,32,128]{3,2,1,0:T(8,128)S(1)}, u32[]{:S(2)}, u32[]{:S(2)}) collective-permute-start(f32[2,8,32,128]{3,2,1,0:T(8,128)S(1)} %get-tuple-element.98.refs_0_), channel_id=1, source_target_pairs={{0,4},{1,2},{2,1},{3,7},{4,0},{5,6},{6,5},{7,3},{8,12},{9,10},{10,... | collective-permute-start | bytes 786440 | tf_op jit(solution)/shard_map/ppermute | solution.py:415
  37.6 12.6 %collective-permute-start.16 = (f32[2,8,32,128]{3,2,1,0:T(8,128)S(1)}, f32[2,8,32,128]{3,2,1,0:T(8,128)S(1)}, u32[]{:S(2)}, u32[]{:S(2)}) collective-permute-start(f32[2,8,32,128]{3,2,1,0:T(8,128)S(1)} %get-tuple-element.97.refs_0_), channel_id=1, source_target_pairs={{0,1},{1,0},{2,3},{3,2},{4,5},{5,4},{6,7},{7,6},{8,9},{9,8},{10,11... | collective-permute-start | bytes 786440 | tf_op jit(solution)/shard_map/ppermute | solution.py:415
  40.7 10.7 %collective-permute-start.17 = (f32[2,8,32,128]{3,2,1,0:T(8,128)S(1)}, f32[2,8,32,128]{3,2,1,0:T(8,128)S(1)}, u32[]{:S(2)}, u32[]{:S(2)}) collective-permute-start(f32[2,8,32,128]{3,2,1,0:T(8,128)S(1)} %get-tuple-element.97.refs_0_), channel_id=1, source_target_pairs={{0,4},{1,2},{2,1},{3,7},{4,0},{5,6},{6,5},{7,3},{8,12},{9,10},{10,... | collective-permute-start | bytes 786440 | tf_op jit(solution)/shard_map/ppermute | solution.py:415
  40.9 14.9 %collective-permute-start.14 = (f32[2,8,32,128]{3,2,1,0:T(8,128)S(1)}, f32[2,8,32,128]{3,2,1,0:T(8,128)S(1)}, u32[]{:S(2)}, u32[]{:S(2)}) collective-permute-start(f32[2,8,32,128]{3,2,1,0:T(8,128)S(1)} %get-tuple-element.96.refs_0_), channel_id=1, source_target_pairs={{0,1},{1,0},{2,3},{3,2},{4,5},{5,4},{6,7},{7,6},{8,9},{9,8},{10,11... | collective-permute-start | bytes 786440 | tf_op jit(solution)/shard_map/ppermute | solution.py:415
  44.6 11.2 %collective-permute-start.15 = (f32[2,8,32,128]{3,2,1,0:T(8,128)S(1)}, f32[2,8,32,128]{3,2,1,0:T(8,128)S(1)}, u32[]{:S(2)}, u32[]{:S(2)}) collective-permute-start(f32[2,8,32,128]{3,2,1,0:T(8,128)S(1)} %get-tuple-element.96.refs_0_), channel_id=1, source_target_pairs={{0,4},{1,2},{2,1},{3,7},{4,0},{5,6},{6,5},{7,3},{8,12},{9,10},{10,... | collective-permute-start | bytes 786440 | tf_op jit(solution)/shard_map/ppermute | solution.py:415
  44.8 16.2 %collective-permute-start.12 = (f32[2,8,32,128]{3,2,1,0:T(8,128)S(1)}, f32[2,8,32,128]{3,2,1,0:T(8,128)S(1)}, u32[]{:S(2)}, u32[]{:S(2)}) collective-permute-start(f32[2,8,32,128]{3,2,1,0:T(8,128)S(1)} %get-tuple-element.93.refs_0_), channel_id=1, source_target_pairs={{0,1},{1,0},{2,3},{3,2},{4,5},{5,4},{6,7},{7,6},{8,9},{9,8},{10,11... | collective-permute-start | bytes 786440 | tf_op jit(solution)/shard_map/ppermute | solution.py:415
  50.2 10.8 %collective-permute-start.13 = (f32[2,8,32,128]{3,2,1,0:T(8,128)S(1)}, f32[2,8,32,128]{3,2,1,0:T(8,128)S(1)}, u32[]{:S(2)}, u32[]{:S(2)}) collective-permute-start(f32[2,8,32,128]{3,2,1,0:T(8,128)S(1)} %get-tuple-element.93.refs_0_), channel_id=1, source_target_pairs={{0,4},{1,2},{2,1},{3,7},{4,0},{5,6},{6,5},{7,3},{8,12},{9,10},{10,... | collective-permute-start | bytes 786440 | tf_op jit(solution)/shard_map/ppermute | solution.py:415
  65.3 7.8 %collective-permute-start.21 = (f32[2,4,48,128]{3,2,1,0:T(8,128)S(1)}, f32[2,4,48,128]{3,2,1,0:T(8,128)S(1)}, u32[]{:S(2)}, u32[]{:S(2)}) collective-permute-start(f32[2,4,48,128]{3,2,1,0:T(8,128)S(1)} %get-tuple-element.110), channel_id=1, source_target_pairs={{0,8},{4,12},{8,0},{12,4},{16,24},{20,28},{24,16},{28,20},{1,9},{5... | collective-permute-start | bytes 589832 | tf_op jit(solution)/shard_map/ppermute | solution.py:398
  67.0 9.5 %collective-permute-start.23 = (f32[2,4,48,128]{3,2,1,0:T(8,128)S(1)}, f32[2,4,48,128]{3,2,1,0:T(8,128)S(1)}, u32[]{:S(2)}, u32[]{:S(2)}) collective-permute-start(f32[2,4,48,128]{3,2,1,0:T(8,128)S(1)} %get-tuple-element.114), channel_id=1, source_target_pairs={{0,8},{4,12},{8,0},{12,4},{16,24},{20,28},{24,16},{28,20},{1,9},{5... | collective-permute-start | bytes 589832 | tf_op jit(solution)/shard_map/ppermute | solution.py:398
  73.2 6.6 %collective-permute-start.22 = (f32[2,4,48,128]{3,2,1,0:T(8,128)S(1)}, f32[2,4,48,128]{3,2,1,0:T(8,128)S(1)}, u32[]{:S(2)}, u32[]{:S(2)}) collective-permute-start(f32[2,4,48,128]{3,2,1,0:T(8,128)S(1)} %get-tuple-element.112), channel_id=1, source_target_pairs={{0,16},{4,20},{8,24},{12,28},{16,0},{20,4},{24,8},{28,12},{1,17},{... | collective-permute-start | bytes 589832 | tf_op jit(solution)/shard_map/ppermute | solution.py:398
  76.6 7.4 %collective-permute-start.24 = (f32[2,4,48,128]{3,2,1,0:T(8,128)S(1)}, f32[2,4,48,128]{3,2,1,0:T(8,128)S(1)}, u32[]{:S(2)}, u32[]{:S(2)}) collective-permute-start(f32[2,4,48,128]{3,2,1,0:T(8,128)S(1)} %get-tuple-element.116), channel_id=1, source_target_pairs={{0,16},{4,20},{8,24},{12,28},{16,0},{20,4},{24,8},{28,12},{1,17},{... | collective-permute-start | bytes 589832 | tf_op jit(solution)/shard_map/ppermute | solution.py:398
  78.3 5.0 %collective-permute-start.25 = (f32[2,4,32,128]{3,2,1,0:T(8,128)S(1)}, f32[2,4,32,128]{3,2,1,0:T(8,128)S(1)}, u32[]{:S(2)}, u32[]{:S(2)}) collective-permute-start(f32[2,4,32,128]{3,2,1,0:T(8,128)S(1)} %get-tuple-element.118), channel_id=1, source_target_pairs={{0,8},{4,12},{8,0},{12,4},{16,24},{20,28},{24,16},{28,20},{1,9},{5... | collective-permute-start | bytes 393224 | tf_op jit(solution)/shard_map/ppermute | solution.py:398
  79.8 11.3 %collective-permute-start.31 = (f32[2,4,48,128]{3,2,1,0:T(8,128)S(1)}, f32[2,4,48,128]{3,2,1,0:T(8,128)S(1)}, u32[]{:S(2)}, u32[]{:S(2)}) collective-permute-start(f32[2,4,48,128]{3,2,1,0:T(8,128)S(1)} %shard_map.67.refs_0_), channel_id=1, source_target_pairs={{0,1},{1,0},{2,3},{3,2},{4,5},{5,4},{6,7},{7,6},{8,9},{9,8},{10,11... | collective-permute-start | bytes 589832 | tf_op jit(solution)/shard_map/ppermute | solution.py:415
  83.4 5.1 %collective-permute-start.26 = (f32[2,4,32,128]{3,2,1,0:T(8,128)S(1)}, f32[2,4,32,128]{3,2,1,0:T(8,128)S(1)}, u32[]{:S(2)}, u32[]{:S(2)}) collective-permute-start(f32[2,4,32,128]{3,2,1,0:T(8,128)S(1)} %get-tuple-element.120), channel_id=1, source_target_pairs={{0,16},{4,20},{8,24},{12,28},{16,0},{20,4},{24,8},{28,12},{1,17},{... | collective-permute-start | bytes 393224 | tf_op jit(solution)/shard_map/ppermute | solution.py:398
  83.9 10.1 %collective-permute-start.32 = (f32[2,4,48,128]{3,2,1,0:T(8,128)S(1)}, f32[2,4,48,128]{3,2,1,0:T(8,128)S(1)}, u32[]{:S(2)}, u32[]{:S(2)}) collective-permute-start(f32[2,4,48,128]{3,2,1,0:T(8,128)S(1)} %shard_map.67.refs_0_), channel_id=1, source_target_pairs={{0,4},{1,2},{2,1},{3,7},{4,0},{5,6},{6,5},{7,3},{8,12},{9,10},{10,... | collective-permute-start | bytes 589832 | tf_op jit(solution)/shard_map/ppermute | solution.py:415
  84.0 10.8 %collective-permute-start.29 = (f32[2,4,48,128]{3,2,1,0:T(8,128)S(1)}, f32[2,4,48,128]{3,2,1,0:T(8,128)S(1)}, u32[]{:S(2)}, u32[]{:S(2)}) collective-permute-start(f32[2,4,48,128]{3,2,1,0:T(8,128)S(1)} %shard_map.69.refs_1_), channel_id=1, source_target_pairs={{0,1},{1,0},{2,3},{3,2},{4,5},{5,4},{6,7},{7,6},{8,9},{9,8},{10,11... | collective-permute-start | bytes 589832 | tf_op jit(solution)/shard_map/ppermute | solution.py:415
  88.5 6.3 %collective-permute-start.30 = (f32[2,4,48,128]{3,2,1,0:T(8,128)S(1)}, f32[2,4,48,128]{3,2,1,0:T(8,128)S(1)}, u32[]{:S(2)}, u32[]{:S(2)}) collective-permute-start(f32[2,4,48,128]{3,2,1,0:T(8,128)S(1)} %shard_map.69.refs_1_), channel_id=1, source_target_pairs={{0,4},{1,2},{2,1},{3,7},{4,0},{5,6},{6,5},{7,3},{8,12},{9,10},{10,... | collective-permute-start | bytes 589832 | tf_op jit(solution)/shard_map/ppermute | solution.py:415
  88.5 6.9 %collective-permute-start.27 = (f32[2,4,32,128]{3,2,1,0:T(8,128)S(1)}, f32[2,4,32,128]{3,2,1,0:T(8,128)S(1)}, u32[]{:S(2)}, u32[]{:S(2)}) collective-permute-start(f32[2,4,32,128]{3,2,1,0:T(8,128)S(1)} %shard_map.71.refs_2_), channel_id=1, source_target_pairs={{0,1},{1,0},{2,3},{3,2},{4,5},{5,4},{6,7},{7,6},{8,9},{9,8},{10,11... | collective-permute-start | bytes 393224 | tf_op jit(solution)/shard_map/ppermute | solution.py:415
  91.2 4.3 %collective-permute-start.28 = (f32[2,4,32,128]{3,2,1,0:T(8,128)S(1)}, f32[2,4,32,128]{3,2,1,0:T(8,128)S(1)}, u32[]{:S(2)}, u32[]{:S(2)}) collective-permute-start(f32[2,4,32,128]{3,2,1,0:T(8,128)S(1)} %shard_map.71.refs_2_), channel_id=1, source_target_pairs={{0,4},{1,2},{2,1},{3,7},{4,0},{5,6},{6,5},{7,3},{8,12},{9,10},{10,... | collective-permute-start | bytes 393224 | tf_op jit(solution)/shard_map/ppermute | solution.py:415
  (5 other events, 69.7 us)
